TPU v7x, 128 devices: a whole 4x4x4 slice. The times are simulated.
128 devices in a mesh: lat: 8 (over x, y_lo), lon: 16 (over y_hi, z, core).
Axes of the slice: x: 4, y: 4 (y_hi: 2, y_lo: 2; y = y_hi * 2 + y_lo), z: 4, core: 2. Of those that a mesh axis runs over, the one named last changes fastest.
Arguments:
- innovations: float32 [25, 65536], P(None, ('lat', 'lon')), may hold values from -6 to 6
- owners: int32 [65536, 1], P(('lat', 'lon')), may hold values from 0 to 127, as said below
- prof_row: int32 [65536], P(('lat', 'lon')), may hold values from 0 to 254
- prof_col: int32 [65536], P(('lat', 'lon')), may hold values from 0 to 126
- interp_weights: float32 [4, 65536], P(None, ('lat', 'lon')), may hold values from 0.1 to 1
- model_tiles: float32 [25, 4096, 8, 128], P(None, ('lat', 'lon')), may hold values from -6 to 6
- model_ids: int32 [1, 4096], P(None, ('lat', 'lon')), may hold values from 0 to 31, as said below
- face_x: float32 [2048, 2048], P('lat', 'lon'), may hold values from 0.02 to 0.12
- face_y: float32 [2048, 2048], P('lat', 'lon'), may hold values from 0.02 to 0.12
- cross_term: float32 [2048, 2048], P('lat', 'lon'), may hold values from -0.08 to 0.08
- wet_mask: int32 [2048, 2048], P('lat', 'lon'), may hold values 0 or 1
- norm_factor: float32 [25, 2048, 2048], P(None, 'lat', 'lon'), may hold values from 0.4 to 2.5
Outputs:
- smoothed: float32 [25, 2048, 2048], P(None, 'lat', 'lon')
- profile_values: float32 [25, 65536], P(None, ('lat', 'lon'))
Inputs may be any that keep to these rules, and one draw needn't show every extreme that they name: `owners`: among the 512 profiles of one device no owner appears more than 8 times; in every draw one owner appears exactly 8 times among every device's profiles. Owners count analysis blocks in lat-major order. `model_ids`: the 32 slots of the model device at lat index i and lon index g form as many equal groups as the lon axis has devices; group j holds tiles of the analysis block at lat index i and lon index j, and every analysis block's 32 tiles appear exactly once over its lat row.
All inputs are finite; a program needn't handle non-finite values. No bound on the sum of `wet_mask` on one device may be relied on, other than what follows from the above.
Results may differ from a plain program's by a relative error of at most 0.00002.
Values sent between devices are 32-bit elements; how exact they have to be, the bound alone decides.
A program may use at most 128 MiB of HBM per device.

v0:
```python
import jax
import jax.numpy as jnp
from jax import lax
from jax.sharding import PartitionSpec as P

STEPS = 10


def with_halo(cells, sides, width, closed):
    for axis, dim in sides:
        count = lax.axis_size(axis)
        ends = count if closed else count - 1
        head = lax.slice_in_dim(cells, 0, width, axis=dim)
        tail = lax.slice_in_dim(cells, cells.shape[dim] - width, cells.shape[dim], axis=dim)
        cells = jnp.concatenate(
            [
                lax.ppermute(tail, axis, [(i, (i + 1) % count) for i in range(ends)]),
                cells,
                lax.ppermute(head, axis, [((i + 1) % count, i) for i in range(ends)]),
            ],
            axis=dim,
        )
    return cells


def rims(values, width):
    widened = with_halo(values, (("lon", 2),), width, True)
    return with_halo(widened, (("lat", 1),), width, False)


def face_weights(stack):
    face_east = stack[0]
    face_north = stack[1]
    twist_field = stack[2]
    wet_cells = stack[3]
    east_face = face_east[1:-1, 1:-1] * wet_cells[1:-1, 1:-1] * wet_cells[1:-1, 2:]
    west_face = face_east[1:-1, :-2] * wet_cells[1:-1, :-2] * wet_cells[1:-1, 1:-1]
    north_face = face_north[1:-1, 1:-1] * wet_cells[1:-1, 1:-1] * wet_cells[2:, 1:-1]
    south_face = face_north[:-2, 1:-1] * wet_cells[:-2, 1:-1] * wet_cells[1:-1, 1:-1]
    twist_face = twist_field[1:-1, 1:-1] * wet_cells[1:-1, 1:-1]
    return (east_face, west_face, north_face, south_face, twist_face)


def trimmed(weights, offset):
    height = weights[0].shape[0]
    across = weights[0].shape[1]
    return tuple(
        (weight[offset : height - offset, offset : across - offset][None] for weight in weights)
    )


def advance(padded, sectioned):
    east_face, west_face, north_face, south_face, twist_face = sectioned
    centre = padded[:, 1:-1, 1:-1]
    return (
        centre
        + east_face * (padded[:, 1:-1, 2:] - centre)
        + west_face * (padded[:, 1:-1, :-2] - centre)
        + north_face * (padded[:, 2:, 1:-1] - centre)
        + south_face * (padded[:, :-2, 1:-1] - centre)
        + 0.25
        * twist_face
        * (padded[:, 2:, 2:] - padded[:, 2:, :-2] - padded[:, :-2, 2:] + padded[:, :-2, :-2])
    )


def on_device(
    innovations,
    owners,
    prof_row,
    prof_col,
    interp_weights,
    model_tiles,
    model_ids,
    face_x,
    face_y,
    cross_term,
    wet_mask,
    norm_factor,
):
    levels = norm_factor.shape[0]
    lat_cells = norm_factor.shape[1]
    lon_cells = norm_factor.shape[2]
    moved_tiles, moved_ids = (
        lax.all_to_all(model_tiles, "lon", split_axis=1, concat_axis=1, tiled=True),
        lax.all_to_all(model_ids, "lon", split_axis=1, concat_axis=1, tiled=True),
    )
    increment = jnp.zeros_like(moved_tiles).at[:, moved_ids[0]].set(moved_tiles)
    increment = increment.reshape(levels, lat_cells, lon_cells)
    devices = lax.axis_size(("lat", "lon"))
    local_count = innovations.shape[1]
    capacity = 2 * local_count // devices
    owner_list = owners[:, 0]
    one_hot = (owner_list[:, None] == jnp.arange(devices, dtype=jnp.int32)[None, :]).astype(
        jnp.int32
    )
    running = jnp.cumsum(one_hot, axis=0)
    rank_in = jnp.sum(running * one_hot, axis=1) - 1
    slot_of = owner_list * capacity + rank_in
    payload = jnp.concatenate([innovations, interp_weights], axis=0)
    send_float = (
        jnp.zeros((levels + 4, devices * capacity), jnp.float32).at[:, slot_of].set(payload)
    )
    location = prof_row * lon_cells + prof_col
    send_index = jnp.zeros((1, devices * capacity), jnp.int32).at[0, slot_of].set(location)
    recv_float, recv_index = (
        lax.all_to_all(send_float, ("lat", "lon"), split_axis=1, concat_axis=1, tiled=True),
        lax.all_to_all(send_index, ("lat", "lon"), split_axis=1, concat_axis=1, tiled=True),
    )
    base_cell = recv_index[0]
    recv_values = recv_float[:levels]
    recv_weights = recv_float[levels:]
    corner_cells = jnp.concatenate(
        [base_cell, base_cell + 1, base_cell + lon_cells, base_cell + lon_cells + 1]
    )
    spread = jnp.concatenate(
        [recv_values * recv_weights[corner][None, :] for corner in range(4)], axis=1
    )
    observed = (
        jnp.zeros((levels, lat_cells * lon_cells), jnp.float32).at[:, corner_cells].add(spread)
    )
    observed = observed.reshape(levels, lat_cells, lon_cells)
    field = norm_factor * (observed + increment)
    depth = 1
    stacked = jnp.stack([face_x, face_y, cross_term, wet_mask.astype(jnp.float32)])
    weights = face_weights(rims(stacked, depth + 1))
    sectioned_list = [trimmed(weights, 1)]

    def sweep(number, values):
        padded = rims(values, depth)
        padded = advance(padded, sectioned_list[0])
        return padded

    field = lax.fori_loop(0, STEPS // depth, sweep, field)
    smoothed = norm_factor * field
    flat_field = smoothed.reshape(levels, -1)
    sampled = (
        recv_weights[0][None, :] * flat_field[:, base_cell]
        + recv_weights[1][None, :] * flat_field[:, base_cell + 1]
        + recv_weights[2][None, :] * flat_field[:, base_cell + lon_cells]
        + recv_weights[3][None, :] * flat_field[:, base_cell + lon_cells + 1]
    )
    returned = lax.all_to_all(sampled, ("lat", "lon"), split_axis=1, concat_axis=1, tiled=True)
    profile_values = returned[:, slot_of]
    return (smoothed, profile_values)


def solution(mesh):
    in_specs = (
        P(None, ("lat", "lon")),
        P(("lat", "lon"), None),
        P(("lat", "lon")),
        P(("lat", "lon")),
        P(None, ("lat", "lon")),
        P(None, ("lat", "lon"), None, None),
        P(None, ("lat", "lon")),
        P("lat", "lon"),
        P("lat", "lon"),
        P("lat", "lon"),
        P("lat", "lon"),
        P(None, "lat", "lon"),
    )
    out_specs = (P(None, "lat", "lon"), P(None, ("lat", "lon")))
    return jax.shard_map(
        on_device, mesh=mesh, in_specs=in_specs, out_specs=out_specs, check_vma=False
    )
```

profile of v0, /device:TPU:1, one launch (start us, length us, event | category | flops | bytes accessed | tf_op | source)
XLA Modules:
  0.0 929.4 jit_solution(13546743064360122939)
XLA Ops:
  3.3 9.5 %all-to-all-start.2 = ((s32[1,16,2]{2,0,1:T(1,128)}), s32[1,16,2]{2,0,1:T(1,128)}, u32[]{:S(2)}, u32[]{:S(2)}) async-start(s32[1,16,2]{2,0,1:T(1,128)} %bitcast.19), calls=%async_computation.2 | async-start | bytes 16384 | tf_op jit(solution)/shard_map/all_to_all | solution.py:86
  34.0 10.6 %all-to-all-start = ((s32[1,128,8]{2,0,1:T(1,128)}), s32[1,128,8]{2,0,1:T(1,128)S(1)}, u32[]{:S(2)}, u32[]{:S(2)}) async-start(s32[1,128,8]{2,0,1:T(1,128)} %bitcast.170), calls=%async_computation | async-start | bytes 131072 | tf_op jit(solution)/shard_map/all_to_all | solution.py:108
  46.6 7.7 all-to-all-done
  60.5 8.2 all-to-all-done.1
  79.1 44.3 %collective-permute-done.6 = f32[4,2,132]{1,2,0:T(8,128)S(1)} collective-permute-done((f32[4,2,132]{1,2,0:T(8,128)S(1)}, f32[4,2,132]{1,2,0:T(8,128)S(1)}, u32[]{:S(2)}, u32[]{:S(2)}) %collective-permute-start.6) | collective-permute-done | bytes 4256 | tf_op jit(solution)/shard_map/ppermute | solution.py:17
  137.0 29.1 %scatter_custom_fusion.2 = f32[25,32768]{0,1:T(8,128)} fusion(s32[4096]{0:T(1024)S(1)} %bitcast.174, f32[4096,25]{1,0:T(8,128)S(1)} %copy.121, f32[]{:T(128)} %constant.8.clone.1), kind=kCustom, calls=%fused_computation.34 | custom fusion | flops 102400 | bytes 3276804 | tf_op jit(solution)/shard_map/scatter-add | solution.py:120
  166.1 13.8 %copy.124 = f32[25,256,128]{1,2,0:T(8,128)} copy(f32[25,256,128]{0,2,1:T(8,128)} %bitcast.142) | data formatting | bytes 6553600 | tf_op jit(solution)/shard_map/reshape | solution.py:122
  180.5 5.0 scatter_fusion
  193.2 662.8 %while.10 = (s32[]{:T(128)}, f32[25,256,128]{1,2,0:T(8,128)S(1)}, f32[1,256,128]{1,2,0:T(8,128)}, f32[1,256,128]{1,2,0:T(8,128)S(1)}, f32[1,256,128]{1,2,0:T(8,1...) while((s32[]{:T(128)}, f32[25,256,128]{1,2,0:T(8,128)S(1)}, ...), condition=%wide.region_8.9_spmd, body=%wide.region_7.8_spmd.sunk | while | flops 20622068 | bytes 71233680 | solution.py:134
  194.3 6.1 collective-permute-start.1
  213.2 5.3 collective-permute-start.3
  225.3 14.4 %pad_maximum_fusion.15 = (f32[25,257,130]{2,1,0:T(8,128)}, f32[25,257,130]{2,1,0:T(8,128)}) fusion(f32[25,1,130]{2,1,0:T(1,128)} %collective-permute-done.2, f32[25,256,1]{2,1,0:T(8,128)} %copy.159, f32[25,256,128]{2,1,0:T(8,128)S(1)} %copy.160, f32[25,256,1]{2,1,0:T(8,128)} %copy.161, f32[25,1,130]{2,1,0:T(1,128)} %collective-permute-done.3), kind=kLoop, calls=%fused_computation.9.clone.1 | loop fusion | flops 5011500 | bytes 10036000 | tf_op jit(solution)/shard_map/while/body/eval_jaxpr/concatenate | solution.py:15
  239.7 17.5 %fusion.46 = f32[25,256,128]{2,1,0:T(8,128)} fusion(f32[25,257,130]{2,1,0:T(8,128)} %get-tuple-element.182, f32[25,257,130]{2,1,0:T(8,128)} %get-tuple-element.183, f32[25,256,128]{2,1,0:T(8,128)S(1)} %copy.160, f32[25,256,1]{2,1,0:T(8,128)} %copy.161, f32[25,256,1]{2,1,0:T(8,128)} %copy.159, f32[256,128]{1,0:T(8,128)} %copy.162, ...), kind=kLoop, calls=%fused_computation.13.clone.1 | loop fusion | flops 15564800 | bytes 26920960 | tf_op jit(solution)/shard_map/while/body/eval_jaxpr/add | solution.py:56
  276.4 5.2 collective-permute-start.3
  288.3 14.4 %pad_maximum_fusion.15 = (f32[25,257,130]{2,1,0:T(8,128)}, f32[25,257,130]{2,1,0:T(8,128)}) fusion(f32[25,1,130]{2,1,0:T(1,128)} %collective-permute-done.2, f32[25,256,1]{2,1,0:T(8,128)} %copy.159, f32[25,256,128]{2,1,0:T(8,128)S(1)} %copy.160, f32[25,256,1]{2,1,0:T(8,128)} %copy.161, f32[25,1,130]{2,1,0:T(1,128)} %collective-permute-done.3), kind=kLoop, calls=%fused_computation.9.clone.1 | loop fusion | flops 5011500 | bytes 10036000 | tf_op jit(solution)/shard_map/while/body/eval_jaxpr/concatenate | solution.py:15
  302.7 17.5 %fusion.46 = f32[25,256,128]{2,1,0:T(8,128)} fusion(f32[25,257,130]{2,1,0:T(8,128)} %get-tuple-element.182, f32[25,257,130]{2,1,0:T(8,128)} %get-tuple-element.183, f32[25,256,128]{2,1,0:T(8,128)S(1)} %copy.160, f32[25,256,1]{2,1,0:T(8,128)} %copy.161, f32[25,256,1]{2,1,0:T(8,128)} %copy.159, f32[256,128]{1,0:T(8,128)} %copy.162, ...), kind=kLoop, calls=%fused_computation.13.clone.1 | loop fusion | flops 15564800 | bytes 26920960 | tf_op jit(solution)/shard_map/while/body/eval_jaxpr/add | solution.py:56
  342.2 5.2 collective-permute-start.3
  354.1 14.4 %pad_maximum_fusion.15 = (f32[25,257,130]{2,1,0:T(8,128)}, f32[25,257,130]{2,1,0:T(8,128)}) fusion(f32[25,1,130]{2,1,0:T(1,128)} %collective-permute-done.2, f32[25,256,1]{2,1,0:T(8,128)} %copy.159, f32[25,256,128]{2,1,0:T(8,128)S(1)} %copy.160, f32[25,256,1]{2,1,0:T(8,128)} %copy.161, f32[25,1,130]{2,1,0:T(1,128)} %collective-permute-done.3), kind=kLoop, calls=%fused_computation.9.clone.1 | loop fusion | flops 5011500 | bytes 10036000 | tf_op jit(solution)/shard_map/while/body/eval_jaxpr/concatenate | solution.py:15
  368.5 17.5 %fusion.46 = f32[25,256,128]{2,1,0:T(8,128)} fusion(f32[25,257,130]{2,1,0:T(8,128)} %get-tuple-element.182, f32[25,257,130]{2,1,0:T(8,128)} %get-tuple-element.183, f32[25,256,128]{2,1,0:T(8,128)S(1)} %copy.160, f32[25,256,1]{2,1,0:T(8,128)} %copy.161, f32[25,256,1]{2,1,0:T(8,128)} %copy.159, f32[256,128]{1,0:T(8,128)} %copy.162, ...), kind=kLoop, calls=%fused_computation.13.clone.1 | loop fusion | flops 15564800 | bytes 26920960 | tf_op jit(solution)/shard_map/while/body/eval_jaxpr/add | solution.py:56
  391.3 4.7 collective-permute-start
  408.8 5.2 collective-permute-start.3
  420.7 14.4 %pad_maximum_fusion.15 = (f32[25,257,130]{2,1,0:T(8,128)}, f32[25,257,130]{2,1,0:T(8,128)}) fusion(f32[25,1,130]{2,1,0:T(1,128)} %collective-permute-done.2, f32[25,256,1]{2,1,0:T(8,128)} %copy.159, f32[25,256,128]{2,1,0:T(8,128)S(1)} %copy.160, f32[25,256,1]{2,1,0:T(8,128)} %copy.161, f32[25,1,130]{2,1,0:T(1,128)} %collective-permute-done.3), kind=kLoop, calls=%fused_computation.9.clone.1 | loop fusion | flops 5011500 | bytes 10036000 | tf_op jit(solution)/shard_map/while/body/eval_jaxpr/concatenate | solution.py:15
  435.1 17.5 %fusion.46 = f32[25,256,128]{2,1,0:T(8,128)} fusion(f32[25,257,130]{2,1,0:T(8,128)} %get-tuple-element.182, f32[25,257,130]{2,1,0:T(8,128)} %get-tuple-element.183, f32[25,256,128]{2,1,0:T(8,128)S(1)} %copy.160, f32[25,256,1]{2,1,0:T(8,128)} %copy.161, f32[25,256,1]{2,1,0:T(8,128)} %copy.159, f32[256,128]{1,0:T(8,128)} %copy.162, ...), kind=kLoop, calls=%fused_computation.13.clone.1 | loop fusion | flops 15564800 | bytes 26920960 | tf_op jit(solution)/shard_map/while/body/eval_jaxpr/add | solution.py:56
  475.5 5.2 collective-permute-start.3
  487.4 14.4 %pad_maximum_fusion.15 = (f32[25,257,130]{2,1,0:T(8,128)}, f32[25,257,130]{2,1,0:T(8,128)}) fusion(f32[25,1,130]{2,1,0:T(1,128)} %collective-permute-done.2, f32[25,256,1]{2,1,0:T(8,128)} %copy.159, f32[25,256,128]{2,1,0:T(8,128)S(1)} %copy.160, f32[25,256,1]{2,1,0:T(8,128)} %copy.161, f32[25,1,130]{2,1,0:T(1,128)} %collective-permute-done.3), kind=kLoop, calls=%fused_computation.9.clone.1 | loop fusion | flops 5011500 | bytes 10036000 | tf_op jit(solution)/shard_map/while/body/eval_jaxpr/concatenate | solution.py:15
  501.8 17.5 %fusion.46 = f32[25,256,128]{2,1,0:T(8,128)} fusion(f32[25,257,130]{2,1,0:T(8,128)} %get-tuple-element.182, f32[25,257,130]{2,1,0:T(8,128)} %get-tuple-element.183, f32[25,256,128]{2,1,0:T(8,128)S(1)} %copy.160, f32[25,256,1]{2,1,0:T(8,128)} %copy.161, f32[25,256,1]{2,1,0:T(8,128)} %copy.159, f32[256,128]{1,0:T(8,128)} %copy.162, ...), kind=kLoop, calls=%fused_computation.13.clone.1 | loop fusion | flops 15564800 | bytes 26920960 | tf_op jit(solution)/shard_map/while/body/eval_jaxpr/add | solution.py:56
  542.1 5.2 collective-permute-start.3
  554.0 14.4 %pad_maximum_fusion.15 = (f32[25,257,130]{2,1,0:T(8,128)}, f32[25,257,130]{2,1,0:T(8,128)}) fusion(f32[25,1,130]{2,1,0:T(1,128)} %collective-permute-done.2, f32[25,256,1]{2,1,0:T(8,128)} %copy.159, f32[25,256,128]{2,1,0:T(8,128)S(1)} %copy.160, f32[25,256,1]{2,1,0:T(8,128)} %copy.161, f32[25,1,130]{2,1,0:T(1,128)} %collective-permute-done.3), kind=kLoop, calls=%fused_computation.9.clone.1 | loop fusion | flops 5011500 | bytes 10036000 | tf_op jit(solution)/shard_map/while/body/eval_jaxpr/concatenate | solution.py:15
  568.4 17.5 %fusion.46 = f32[25,256,128]{2,1,0:T(8,128)} fusion(f32[25,257,130]{2,1,0:T(8,128)} %get-tuple-element.182, f32[25,257,130]{2,1,0:T(8,128)} %get-tuple-element.183, f32[25,256,128]{2,1,0:T(8,128)S(1)} %copy.160, f32[25,256,1]{2,1,0:T(8,128)} %copy.161, f32[25,256,1]{2,1,0:T(8,128)} %copy.159, f32[256,128]{1,0:T(8,128)} %copy.162, ...), kind=kLoop, calls=%fused_computation.13.clone.1 | loop fusion | flops 15564800 | bytes 26920960 | tf_op jit(solution)/shard_map/while/body/eval_jaxpr/add | solution.py:56
  608.8 5.2 collective-permute-start.3
  620.7 14.4 %pad_maximum_fusion.15 = (f32[25,257,130]{2,1,0:T(8,128)}, f32[25,257,130]{2,1,0:T(8,128)}) fusion(f32[25,1,130]{2,1,0:T(1,128)} %collective-permute-done.2, f32[25,256,1]{2,1,0:T(8,128)} %copy.159, f32[25,256,128]{2,1,0:T(8,128)S(1)} %copy.160, f32[25,256,1]{2,1,0:T(8,128)} %copy.161, f32[25,1,130]{2,1,0:T(1,128)} %collective-permute-done.3), kind=kLoop, calls=%fused_computation.9.clone.1 | loop fusion | flops 5011500 | bytes 10036000 | tf_op jit(solution)/shard_map/while/body/eval_jaxpr/concatenate | solution.py:15
  635.1 17.5 %fusion.46 = f32[25,256,128]{2,1,0:T(8,128)} fusion(f32[25,257,130]{2,1,0:T(8,128)} %get-tuple-element.182, f32[25,257,130]{2,1,0:T(8,128)} %get-tuple-element.183, f32[25,256,128]{2,1,0:T(8,128)S(1)} %copy.160, f32[25,256,1]{2,1,0:T(8,128)} %copy.161, f32[25,256,1]{2,1,0:T(8,128)} %copy.159, f32[256,128]{1,0:T(8,128)} %copy.162, ...), kind=kLoop, calls=%fused_computation.13.clone.1 | loop fusion | flops 15564800 | bytes 26920960 | tf_op jit(solution)/shard_map/while/body/eval_jaxpr/add | solution.py:56
  675.4 5.2 collective-permute-start.3
  687.3 14.4 %pad_maximum_fusion.15 = (f32[25,257,130]{2,1,0:T(8,128)}, f32[25,257,130]{2,1,0:T(8,128)}) fusion(f32[25,1,130]{2,1,0:T(1,128)} %collective-permute-done.2, f32[25,256,1]{2,1,0:T(8,128)} %copy.159, f32[25,256,128]{2,1,0:T(8,128)S(1)} %copy.160, f32[25,256,1]{2,1,0:T(8,128)} %copy.161, f32[25,1,130]{2,1,0:T(1,128)} %collective-permute-done.3), kind=kLoop, calls=%fused_computation.9.clone.1 | loop fusion | flops 5011500 | bytes 10036000 | tf_op jit(solution)/shard_map/while/body/eval_jaxpr/concatenate | solution.py:15
  701.7 17.5 %fusion.46 = f32[25,256,128]{2,1,0:T(8,128)} fusion(f32[25,257,130]{2,1,0:T(8,128)} %get-tuple-element.182, f32[25,257,130]{2,1,0:T(8,128)} %get-tuple-element.183, f32[25,256,128]{2,1,0:T(8,128)S(1)} %copy.160, f32[25,256,1]{2,1,0:T(8,128)} %copy.161, f32[25,256,1]{2,1,0:T(8,128)} %copy.159, f32[256,128]{1,0:T(8,128)} %copy.162, ...), kind=kLoop, calls=%fused_computation.13.clone.1 | loop fusion | flops 15564800 | bytes 26920960 | tf_op jit(solution)/shard_map/while/body/eval_jaxpr/add | solution.py:56
  742.0 5.2 collective-permute-start.3
  753.9 14.4 %pad_maximum_fusion.15 = (f32[25,257,130]{2,1,0:T(8,128)}, f32[25,257,130]{2,1,0:T(8,128)}) fusion(f32[25,1,130]{2,1,0:T(1,128)} %collective-permute-done.2, f32[25,256,1]{2,1,0:T(8,128)} %copy.159, f32[25,256,128]{2,1,0:T(8,128)S(1)} %copy.160, f32[25,256,1]{2,1,0:T(8,128)} %copy.161, f32[25,1,130]{2,1,0:T(1,128)} %collective-permute-done.3), kind=kLoop, calls=%fused_computation.9.clone.1 | loop fusion | flops 5011500 | bytes 10036000 | tf_op jit(solution)/shard_map/while/body/eval_jaxpr/concatenate | solution.py:15
  768.3 17.5 %fusion.46 = f32[25,256,128]{2,1,0:T(8,128)} fusion(f32[25,257,130]{2,1,0:T(8,128)} %get-tuple-element.182, f32[25,257,130]{2,1,0:T(8,128)} %get-tuple-element.183, f32[25,256,128]{2,1,0:T(8,128)S(1)} %copy.160, f32[25,256,1]{2,1,0:T(8,128)} %copy.161, f32[25,256,1]{2,1,0:T(8,128)} %copy.159, f32[256,128]{1,0:T(8,128)} %copy.162, ...), kind=kLoop, calls=%fused_computation.13.clone.1 | loop fusion | flops 15564800 | bytes 26920960 | tf_op jit(solution)/shard_map/while/body/eval_jaxpr/add | solution.py:56
  791.1 4.7 collective-permute-start
  808.7 5.2 collective-permute-start.3
  820.6 14.4 %pad_maximum_fusion.15 = (f32[25,257,130]{2,1,0:T(8,128)}, f32[25,257,130]{2,1,0:T(8,128)}) fusion(f32[25,1,130]{2,1,0:T(1,128)} %collective-permute-done.2, f32[25,256,1]{2,1,0:T(8,128)} %copy.159, f32[25,256,128]{2,1,0:T(8,128)S(1)} %copy.160, f32[25,256,1]{2,1,0:T(8,128)} %copy.161, f32[25,1,130]{2,1,0:T(1,128)} %collective-permute-done.3), kind=kLoop, calls=%fused_computation.9.clone.1 | loop fusion | flops 5011500 | bytes 10036000 | tf_op jit(solution)/shard_map/while/body/eval_jaxpr/concatenate | solution.py:15
  835.0 17.5 %fusion.46 = f32[25,256,128]{2,1,0:T(8,128)} fusion(f32[25,257,130]{2,1,0:T(8,128)} %get-tuple-element.182, f32[25,257,130]{2,1,0:T(8,128)} %get-tuple-element.183, f32[25,256,128]{2,1,0:T(8,128)S(1)} %copy.160, f32[25,256,1]{2,1,0:T(8,128)} %copy.161, f32[25,256,1]{2,1,0:T(8,128)} %copy.159, f32[256,128]{1,0:T(8,128)} %copy.162, ...), kind=kLoop, calls=%fused_computation.13.clone.1 | loop fusion | flops 15564800 | bytes 26920960 | tf_op jit(solution)/shard_map/while/body/eval_jaxpr/add | solution.py:56
  862.4 9.0 copy.133
  871.5 8.6 gather_fusion.3
  880.1 8.6 gather_fusion.2
  888.7 8.6 gather_fusion.1
  897.3 8.6 gather_fusion
  906.9 19.4 %all_to_all.41 = f32[128,1,200]{2,1,0:T(1,128)S(1)} all-to-all(f32[128,1,200]{2,1,0:T(1,128)S(1)} %reshape.502), channel_id=1, replica_groups=mesh['lat'=8,'lon'=16] {'lat','lon'}, dimensions={0} | all-to-all | bytes 204800 | tf_op jit(solution)/shard_map/all_to_all | solution.py:143
  (449 shorter events, 349.4 us)
Async XLA Ops:
  3.3 30.7 %all-to-all-start.2 = ((s32[1,16,2]{2,0,1:T(1,128)}), s32[1,16,2]{2,0,1:T(1,128)}, u32[]{:S(2)}, u32[]{:S(2)}) async-start(s32[1,16,2]{2,0,1:T(1,128)} %bitcast.19), calls=%async_computation.2 | async-start | bytes 16384 | tf_op jit(solution)/shard_map/all_to_all | solution.py:86
  17.5 57.0 %collective-permute-start.4 = (f32[4,256,2]{1,2,0:T(2,128)}, f32[4,256,2]{1,2,0:T(2,128)S(1)}, u32[]{:S(2)}, u32[]{:S(2)}) collective-permute-start(f32[4,256,2]{1,2,0:T(2,128)} %get-tuple-element.95), channel_id=1, source_target_pairs={{0,1},{1,2},{2,3},{3,4},{4,5},{5,6},{6,7},{7,8},{8,9},{9,10},{10,1... | collective-permute-start | bytes 24584 | tf_op jit(solution)/shard_map/ppermute | solution.py:17
  19.2 55.4 %collective-permute-start.5 = (f32[4,256,2]{1,2,0:T(2,128)}, f32[4,256,2]{1,2,0:T(2,128)S(1)}, u32[]{:S(2)}, u32[]{:S(2)}) collective-permute-start(f32[4,256,2]{1,2,0:T(2,128)} %get-tuple-element.96), channel_id=1, source_target_pairs={{1,0},{2,1},{3,2},{4,3},{5,4},{6,5},{7,6},{8,7},{9,8},{10,9},{11,1... | collective-permute-start | bytes 24584 | tf_op jit(solution)/shard_map/ppermute | solution.py:19
  34.0 20.3 %all-to-all-start = ((s32[1,128,8]{2,0,1:T(1,128)}), s32[1,128,8]{2,0,1:T(1,128)S(1)}, u32[]{:S(2)}, u32[]{:S(2)}) async-start(s32[1,128,8]{2,0,1:T(1,128)} %bitcast.170), calls=%async_computation | async-start | bytes 131072 | tf_op jit(solution)/shard_map/all_to_all | solution.py:108
  54.3 14.4 %all-to-all-start.1 = ((f32[128,1,232]{2,1,0:T(1,128)}), f32[128,1,232]{2,1,0:T(1,128)S(1)}, u32[]{:S(2)}, u32[]{:S(2)}) async-start(f32[128,1,232]{2,1,0:T(1,128)} %reshape.500), calls=%async_computation.1 | async-start | bytes 262144 | tf_op jit(solution)/shard_map/all_to_all | solution.py:107
  68.7 111.1 %all-to-all-start.3 = ((f32[25,32,8,128]{3,2,0,1:T(8,128)}), f32[25,32,8,128]{3,2,0,1:T(8,128)}, u32[]{:S(2)}, u32[]{:S(2)}) async-start(f32[25,32,8,128]{3,2,0,1:T(8,128)} %copy.123), calls=%async_computation.3 | async-start | bytes 6553600 | tf_op jit(solution)/shard_map/all_to_all | solution.py:85
  74.8 48.7 %collective-permute-start.6 = (f32[4,2,132]{1,2,0:T(8,128)S(1)}, f32[4,2,132]{1,2,0:T(8,128)S(1)}, u32[]{:S(2)}, u32[]{:S(2)}) collective-permute-start(f32[4,2,132]{1,2,0:T(8,128)S(1)} %get-tuple-element.89), channel_id=1, source_target_pairs={{0,16},{16,32},{32,48},{48,64},{64,80},{80,96},{96,112},{1,17},{17... | collective-permute-start | bytes 12680 | tf_op jit(solution)/shard_map/ppermute | solution.py:17
  77.1 46.4 %collective-permute-start.7 = (f32[4,2,132]{1,2,0:T(8,128)S(1)}, f32[4,2,132]{1,2,0:T(8,128)S(1)}, u32[]{:S(2)}, u32[]{:S(2)}) collective-permute-start(f32[4,2,132]{1,2,0:T(8,128)S(1)} %get-tuple-element.90), channel_id=1, source_target_pairs={{16,0},{32,16},{48,32},{64,48},{80,64},{96,80},{112,96},{17,1},{33... | collective-permute-start | bytes 12680 | tf_op jit(solution)/shard_map/ppermute | solution.py:19
  194.3 9.8 %collective-permute-start.1 = (f32[25,256,1]{1,2,0:T(1,128)}, f32[25,256,1]{1,2,0:T(1,128)}, u32[]{:S(2)}, u32[]{:S(2)}) collective-permute-start(f32[25,256,1]{1,2,0:T(1,128)} %get-tuple-element.179), channel_id=1, source_target_pairs={{0,1},{1,2},{2,3},{3,4},{4,5},{5,6},{6,7},{7,8},{8,9},{9,10},{10,1... | collective-permute-start | bytes 76808 | tf_op jit(solution)/shard_map/while/body/eval_jaxpr/ppermute | solution.py:17
  200.4 6.7 collective-permute-start
  211.9 13.3 %collective-permute-start.2 = (f32[25,1,130]{2,1,0:T(1,128)}, f32[25,1,130]{2,1,0:T(1,128)}, u32[]{:S(2)}, u32[]{:S(2)}) collective-permute-start(f32[25,1,130]{2,1,0:T(1,128)} %get-tuple-element.180), channel_id=1, source_target_pairs={{16,0},{32,16},{48,32},{64,48},{80,64},{96,80},{112,96},{17,1},{33... | collective-permute-start | bytes 39008 | tf_op jit(solution)/shard_map/while/body/eval_jaxpr/ppermute | solution.py:19
  213.2 12.0 %collective-permute-start.3 = (f32[25,1,130]{2,1,0:T(1,128)}, f32[25,1,130]{2,1,0:T(1,128)}, u32[]{:S(2)}, u32[]{:S(2)}) collective-permute-start(f32[25,1,130]{2,1,0:T(1,128)} %get-tuple-element.181), channel_id=1, source_target_pairs={{0,16},{16,32},{32,48},{48,64},{64,80},{80,96},{96,112},{1,17},{17... | collective-permute-start | bytes 39008 | tf_op jit(solution)/shard_map/while/body/eval_jaxpr/ppermute | solution.py:17
  261.6 5.7 collective-permute-start.1
  263.6 6.7 collective-permute-start
  275.1 13.2 %collective-permute-start.2 = (f32[25,1,130]{2,1,0:T(1,128)}, f32[25,1,130]{2,1,0:T(1,128)}, u32[]{:S(2)}, u32[]{:S(2)}) collective-permute-start(f32[25,1,130]{2,1,0:T(1,128)} %get-tuple-element.180), channel_id=1, source_target_pairs={{16,0},{32,16},{48,32},{64,48},{80,64},{96,80},{112,96},{17,1},{33... | collective-permute-start | bytes 39008 | tf_op jit(solution)/shard_map/while/body/eval_jaxpr/ppermute | solution.py:19
  276.4 11.9 %collective-permute-start.3 = (f32[25,1,130]{2,1,0:T(1,128)}, f32[25,1,130]{2,1,0:T(1,128)}, u32[]{:S(2)}, u32[]{:S(2)}) collective-permute-start(f32[25,1,130]{2,1,0:T(1,128)} %get-tuple-element.181), channel_id=1, source_target_pairs={{0,16},{16,32},{32,48},{48,64},{64,80},{80,96},{96,112},{1,17},{17... | collective-permute-start | bytes 39008 | tf_op jit(solution)/shard_map/while/body/eval_jaxpr/ppermute | solution.py:17
  324.6 8.5 collective-permute-start.1
  326.6 9.4 %collective-permute-start = (f32[25,256,1]{1,2,0:T(1,128)}, f32[25,256,1]{1,2,0:T(1,128)}, u32[]{:S(2)}, u32[]{:S(2)}) collective-permute-start(f32[25,256,1]{1,2,0:T(1,128)} %get-tuple-element.178), channel_id=1, source_target_pairs={{1,0},{2,1},{3,2},{4,3},{5,4},{6,5},{7,6},{8,7},{9,8},{10,9},{11,1... | collective-permute-start | bytes 76808 | tf_op jit(solution)/shard_map/while/body/eval_jaxpr/ppermute | solution.py:19
  340.9 13.2 %collective-permute-start.2 = (f32[25,1,130]{2,1,0:T(1,128)}, f32[25,1,130]{2,1,0:T(1,128)}, u32[]{:S(2)}, u32[]{:S(2)}) collective-permute-start(f32[25,1,130]{2,1,0:T(1,128)} %get-tuple-element.180), channel_id=1, source_target_pairs={{16,0},{32,16},{48,32},{64,48},{80,64},{96,80},{112,96},{17,1},{33... | collective-permute-start | bytes 39008 | tf_op jit(solution)/shard_map/while/body/eval_jaxpr/ppermute | solution.py:19
  342.2 11.9 %collective-permute-start.3 = (f32[25,1,130]{2,1,0:T(1,128)}, f32[25,1,130]{2,1,0:T(1,128)}, u32[]{:S(2)}, u32[]{:S(2)}) collective-permute-start(f32[25,1,130]{2,1,0:T(1,128)} %get-tuple-element.181), channel_id=1, source_target_pairs={{0,16},{16,32},{32,48},{48,64},{64,80},{80,96},{96,112},{1,17},{17... | collective-permute-start | bytes 39008 | tf_op jit(solution)/shard_map/while/body/eval_jaxpr/ppermute | solution.py:17
  390.4 9.3 %collective-permute-start.1 = (f32[25,256,1]{1,2,0:T(1,128)}, f32[25,256,1]{1,2,0:T(1,128)}, u32[]{:S(2)}, u32[]{:S(2)}) collective-permute-start(f32[25,256,1]{1,2,0:T(1,128)} %get-tuple-element.179), channel_id=1, source_target_pairs={{0,1},{1,2},{2,3},{3,4},{4,5},{5,6},{6,7},{7,8},{8,9},{9,10},{10,1... | collective-permute-start | bytes 76808 | tf_op jit(solution)/shard_map/while/body/eval_jaxpr/ppermute | solution.py:17
  391.3 11.4 %collective-permute-start = (f32[25,256,1]{1,2,0:T(1,128)}, f32[25,256,1]{1,2,0:T(1,128)}, u32[]{:S(2)}, u32[]{:S(2)}) collective-permute-start(f32[25,256,1]{1,2,0:T(1,128)} %get-tuple-element.178), channel_id=1, source_target_pairs={{1,0},{2,1},{3,2},{4,3},{5,4},{6,5},{7,6},{8,7},{9,8},{10,9},{11,1... | collective-permute-start | bytes 76808 | tf_op jit(solution)/shard_map/while/body/eval_jaxpr/ppermute | solution.py:19
  407.5 13.2 %collective-permute-start.2 = (f32[25,1,130]{2,1,0:T(1,128)}, f32[25,1,130]{2,1,0:T(1,128)}, u32[]{:S(2)}, u32[]{:S(2)}) collective-permute-start(f32[25,1,130]{2,1,0:T(1,128)} %get-tuple-element.180), channel_id=1, source_target_pairs={{16,0},{32,16},{48,32},{64,48},{80,64},{96,80},{112,96},{17,1},{33... | collective-permute-start | bytes 39008 | tf_op jit(solution)/shard_map/while/body/eval_jaxpr/ppermute | solution.py:19
  408.8 11.9 %collective-permute-start.3 = (f32[25,1,130]{2,1,0:T(1,128)}, f32[25,1,130]{2,1,0:T(1,128)}, u32[]{:S(2)}, u32[]{:S(2)}) collective-permute-start(f32[25,1,130]{2,1,0:T(1,128)} %get-tuple-element.181), channel_id=1, source_target_pairs={{0,16},{16,32},{32,48},{48,64},{64,80},{80,96},{96,112},{1,17},{17... | collective-permute-start | bytes 39008 | tf_op jit(solution)/shard_map/while/body/eval_jaxpr/ppermute | solution.py:17
  457.0 9.3 %collective-permute-start.1 = (f32[25,256,1]{1,2,0:T(1,128)}, f32[25,256,1]{1,2,0:T(1,128)}, u32[]{:S(2)}, u32[]{:S(2)}) collective-permute-start(f32[25,256,1]{1,2,0:T(1,128)} %get-tuple-element.179), channel_id=1, source_target_pairs={{0,1},{1,2},{2,3},{3,4},{4,5},{5,6},{6,7},{7,8},{8,9},{9,10},{10,1... | collective-permute-start | bytes 76808 | tf_op jit(solution)/shard_map/while/body/eval_jaxpr/ppermute | solution.py:17
  457.9 11.4 %collective-permute-start = (f32[25,256,1]{1,2,0:T(1,128)}, f32[25,256,1]{1,2,0:T(1,128)}, u32[]{:S(2)}, u32[]{:S(2)}) collective-permute-start(f32[25,256,1]{1,2,0:T(1,128)} %get-tuple-element.178), channel_id=1, source_target_pairs={{1,0},{2,1},{3,2},{4,3},{5,4},{6,5},{7,6},{8,7},{9,8},{10,9},{11,1... | collective-permute-start | bytes 76808 | tf_op jit(solution)/shard_map/while/body/eval_jaxpr/ppermute | solution.py:19
  474.2 13.2 %collective-permute-start.2 = (f32[25,1,130]{2,1,0:T(1,128)}, f32[25,1,130]{2,1,0:T(1,128)}, u32[]{:S(2)}, u32[]{:S(2)}) collective-permute-start(f32[25,1,130]{2,1,0:T(1,128)} %get-tuple-element.180), channel_id=1, source_target_pairs={{16,0},{32,16},{48,32},{64,48},{80,64},{96,80},{112,96},{17,1},{33... | collective-permute-start | bytes 39008 | tf_op jit(solution)/shard_map/while/body/eval_jaxpr/ppermute | solution.py:19
  475.5 11.9 %collective-permute-start.3 = (f32[25,1,130]{2,1,0:T(1,128)}, f32[25,1,130]{2,1,0:T(1,128)}, u32[]{:S(2)}, u32[]{:S(2)}) collective-permute-start(f32[25,1,130]{2,1,0:T(1,128)} %get-tuple-element.181), channel_id=1, source_target_pairs={{0,16},{16,32},{32,48},{48,64},{64,80},{80,96},{96,112},{1,17},{17... | collective-permute-start | bytes 39008 | tf_op jit(solution)/shard_map/while/body/eval_jaxpr/ppermute | solution.py:17
  523.6 9.3 %collective-permute-start.1 = (f32[25,256,1]{1,2,0:T(1,128)}, f32[25,256,1]{1,2,0:T(1,128)}, u32[]{:S(2)}, u32[]{:S(2)}) collective-permute-start(f32[25,256,1]{1,2,0:T(1,128)} %get-tuple-element.179), channel_id=1, source_target_pairs={{0,1},{1,2},{2,3},{3,4},{4,5},{5,6},{6,7},{7,8},{8,9},{9,10},{10,1... | collective-permute-start | bytes 76808 | tf_op jit(solution)/shard_map/while/body/eval_jaxpr/ppermute | solution.py:17
  524.6 11.4 %collective-permute-start = (f32[25,256,1]{1,2,0:T(1,128)}, f32[25,256,1]{1,2,0:T(1,128)}, u32[]{:S(2)}, u32[]{:S(2)}) collective-permute-start(f32[25,256,1]{1,2,0:T(1,128)} %get-tuple-element.178), channel_id=1, source_target_pairs={{1,0},{2,1},{3,2},{4,3},{5,4},{6,5},{7,6},{8,7},{9,8},{10,9},{11,1... | collective-permute-start | bytes 76808 | tf_op jit(solution)/shard_map/while/body/eval_jaxpr/ppermute | solution.py:19
  540.8 13.2 %collective-permute-start.2 = (f32[25,1,130]{2,1,0:T(1,128)}, f32[25,1,130]{2,1,0:T(1,128)}, u32[]{:S(2)}, u32[]{:S(2)}) collective-permute-start(f32[25,1,130]{2,1,0:T(1,128)} %get-tuple-element.180), channel_id=1, source_target_pairs={{16,0},{32,16},{48,32},{64,48},{80,64},{96,80},{112,96},{17,1},{33... | collective-permute-start | bytes 39008 | tf_op jit(solution)/shard_map/while/body/eval_jaxpr/ppermute | solution.py:19
  542.1 11.9 %collective-permute-start.3 = (f32[25,1,130]{2,1,0:T(1,128)}, f32[25,1,130]{2,1,0:T(1,128)}, u32[]{:S(2)}, u32[]{:S(2)}) collective-permute-start(f32[25,1,130]{2,1,0:T(1,128)} %get-tuple-element.181), channel_id=1, source_target_pairs={{0,16},{16,32},{32,48},{48,64},{64,80},{80,96},{96,112},{1,17},{17... | collective-permute-start | bytes 39008 | tf_op jit(solution)/shard_map/while/body/eval_jaxpr/ppermute | solution.py:17
  590.3 9.3 %collective-permute-start.1 = (f32[25,256,1]{1,2,0:T(1,128)}, f32[25,256,1]{1,2,0:T(1,128)}, u32[]{:S(2)}, u32[]{:S(2)}) collective-permute-start(f32[25,256,1]{1,2,0:T(1,128)} %get-tuple-element.179), channel_id=1, source_target_pairs={{0,1},{1,2},{2,3},{3,4},{4,5},{5,6},{6,7},{7,8},{8,9},{9,10},{10,1... | collective-permute-start | bytes 76808 | tf_op jit(solution)/shard_map/while/body/eval_jaxpr/ppermute | solution.py:17
  591.2 11.4 %collective-permute-start = (f32[25,256,1]{1,2,0:T(1,128)}, f32[25,256,1]{1,2,0:T(1,128)}, u32[]{:S(2)}, u32[]{:S(2)}) collective-permute-start(f32[25,256,1]{1,2,0:T(1,128)} %get-tuple-element.178), channel_id=1, source_target_pairs={{1,0},{2,1},{3,2},{4,3},{5,4},{6,5},{7,6},{8,7},{9,8},{10,9},{11,1... | collective-permute-start | bytes 76808 | tf_op jit(solution)/shard_map/while/body/eval_jaxpr/ppermute | solution.py:19
  607.5 13.2 %collective-permute-start.2 = (f32[25,1,130]{2,1,0:T(1,128)}, f32[25,1,130]{2,1,0:T(1,128)}, u32[]{:S(2)}, u32[]{:S(2)}) collective-permute-start(f32[25,1,130]{2,1,0:T(1,128)} %get-tuple-element.180), channel_id=1, source_target_pairs={{16,0},{32,16},{48,32},{64,48},{80,64},{96,80},{112,96},{17,1},{33... | collective-permute-start | bytes 39008 | tf_op jit(solution)/shard_map/while/body/eval_jaxpr/ppermute | solution.py:19
  608.8 11.9 %collective-permute-start.3 = (f32[25,1,130]{2,1,0:T(1,128)}, f32[25,1,130]{2,1,0:T(1,128)}, u32[]{:S(2)}, u32[]{:S(2)}) collective-permute-start(f32[25,1,130]{2,1,0:T(1,128)} %get-tuple-element.181), channel_id=1, source_target_pairs={{0,16},{16,32},{32,48},{48,64},{64,80},{80,96},{96,112},{1,17},{17... | collective-permute-start | bytes 39008 | tf_op jit(solution)/shard_map/while/body/eval_jaxpr/ppermute | solution.py:17
  656.9 9.3 %collective-permute-start.1 = (f32[25,256,1]{1,2,0:T(1,128)}, f32[25,256,1]{1,2,0:T(1,128)}, u32[]{:S(2)}, u32[]{:S(2)}) collective-permute-start(f32[25,256,1]{1,2,0:T(1,128)} %get-tuple-element.179), channel_id=1, source_target_pairs={{0,1},{1,2},{2,3},{3,4},{4,5},{5,6},{6,7},{7,8},{8,9},{9,10},{10,1... | collective-permute-start | bytes 76808 | tf_op jit(solution)/shard_map/while/body/eval_jaxpr/ppermute | solution.py:17
  657.9 11.4 %collective-permute-start = (f32[25,256,1]{1,2,0:T(1,128)}, f32[25,256,1]{1,2,0:T(1,128)}, u32[]{:S(2)}, u32[]{:S(2)}) collective-permute-start(f32[25,256,1]{1,2,0:T(1,128)} %get-tuple-element.178), channel_id=1, source_target_pairs={{1,0},{2,1},{3,2},{4,3},{5,4},{6,5},{7,6},{8,7},{9,8},{10,9},{11,1... | collective-permute-start | bytes 76808 | tf_op jit(solution)/shard_map/while/body/eval_jaxpr/ppermute | solution.py:19
  674.1 13.2 %collective-permute-start.2 = (f32[25,1,130]{2,1,0:T(1,128)}, f32[25,1,130]{2,1,0:T(1,128)}, u32[]{:S(2)}, u32[]{:S(2)}) collective-permute-start(f32[25,1,130]{2,1,0:T(1,128)} %get-tuple-element.180), channel_id=1, source_target_pairs={{16,0},{32,16},{48,32},{64,48},{80,64},{96,80},{112,96},{17,1},{33... | collective-permute-start | bytes 39008 | tf_op jit(solution)/shard_map/while/body/eval_jaxpr/ppermute | solution.py:19
  675.4 11.9 %collective-permute-start.3 = (f32[25,1,130]{2,1,0:T(1,128)}, f32[25,1,130]{2,1,0:T(1,128)}, u32[]{:S(2)}, u32[]{:S(2)}) collective-permute-start(f32[25,1,130]{2,1,0:T(1,128)} %get-tuple-element.181), channel_id=1, source_target_pairs={{0,16},{16,32},{32,48},{48,64},{64,80},{80,96},{96,112},{1,17},{17... | collective-permute-start | bytes 39008 | tf_op jit(solution)/shard_map/while/body/eval_jaxpr/ppermute | solution.py:17
  723.6 9.3 %collective-permute-start.1 = (f32[25,256,1]{1,2,0:T(1,128)}, f32[25,256,1]{1,2,0:T(1,128)}, u32[]{:S(2)}, u32[]{:S(2)}) collective-permute-start(f32[25,256,1]{1,2,0:T(1,128)} %get-tuple-element.179), channel_id=1, source_target_pairs={{0,1},{1,2},{2,3},{3,4},{4,5},{5,6},{6,7},{7,8},{8,9},{9,10},{10,1... | collective-permute-start | bytes 76808 | tf_op jit(solution)/shard_map/while/body/eval_jaxpr/ppermute | solution.py:17
  724.5 11.4 %collective-permute-start = (f32[25,256,1]{1,2,0:T(1,128)}, f32[25,256,1]{1,2,0:T(1,128)}, u32[]{:S(2)}, u32[]{:S(2)}) collective-permute-start(f32[25,256,1]{1,2,0:T(1,128)} %get-tuple-element.178), channel_id=1, source_target_pairs={{1,0},{2,1},{3,2},{4,3},{5,4},{6,5},{7,6},{8,7},{9,8},{10,9},{11,1... | collective-permute-start | bytes 76808 | tf_op jit(solution)/shard_map/while/body/eval_jaxpr/ppermute | solution.py:19
  740.7 13.2 %collective-permute-start.2 = (f32[25,1,130]{2,1,0:T(1,128)}, f32[25,1,130]{2,1,0:T(1,128)}, u32[]{:S(2)}, u32[]{:S(2)}) collective-permute-start(f32[25,1,130]{2,1,0:T(1,128)} %get-tuple-element.180), channel_id=1, source_target_pairs={{16,0},{32,16},{48,32},{64,48},{80,64},{96,80},{112,96},{17,1},{33... | collective-permute-start | bytes 39008 | tf_op jit(solution)/shard_map/while/body/eval_jaxpr/ppermute | solution.py:19
  742.0 11.9 %collective-permute-start.3 = (f32[25,1,130]{2,1,0:T(1,128)}, f32[25,1,130]{2,1,0:T(1,128)}, u32[]{:S(2)}, u32[]{:S(2)}) collective-permute-start(f32[25,1,130]{2,1,0:T(1,128)} %get-tuple-element.181), channel_id=1, source_target_pairs={{0,16},{16,32},{32,48},{48,64},{64,80},{80,96},{96,112},{1,17},{17... | collective-permute-start | bytes 39008 | tf_op jit(solution)/shard_map/while/body/eval_jaxpr/ppermute | solution.py:17
  790.2 9.3 %collective-permute-start.1 = (f32[25,256,1]{1,2,0:T(1,128)}, f32[25,256,1]{1,2,0:T(1,128)}, u32[]{:S(2)}, u32[]{:S(2)}) collective-permute-start(f32[25,256,1]{1,2,0:T(1,128)} %get-tuple-element.179), channel_id=1, source_target_pairs={{0,1},{1,2},{2,3},{3,4},{4,5},{5,6},{6,7},{7,8},{8,9},{9,10},{10,1... | collective-permute-start | bytes 76808 | tf_op jit(solution)/shard_map/while/body/eval_jaxpr/ppermute | solution.py:17
  791.1 11.4 %collective-permute-start = (f32[25,256,1]{1,2,0:T(1,128)}, f32[25,256,1]{1,2,0:T(1,128)}, u32[]{:S(2)}, u32[]{:S(2)}) collective-permute-start(f32[25,256,1]{1,2,0:T(1,128)} %get-tuple-element.178), channel_id=1, source_target_pairs={{1,0},{2,1},{3,2},{4,3},{5,4},{6,5},{7,6},{8,7},{9,8},{10,9},{11,1... | collective-permute-start | bytes 76808 | tf_op jit(solution)/shard_map/while/body/eval_jaxpr/ppermute | solution.py:19
  807.4 13.2 %collective-permute-start.2 = (f32[25,1,130]{2,1,0:T(1,128)}, f32[25,1,130]{2,1,0:T(1,128)}, u32[]{:S(2)}, u32[]{:S(2)}) collective-permute-start(f32[25,1,130]{2,1,0:T(1,128)} %get-tuple-element.180), channel_id=1, source_target_pairs={{16,0},{32,16},{48,32},{64,48},{80,64},{96,80},{112,96},{17,1},{33... | collective-permute-start | bytes 39008 | tf_op jit(solution)/shard_map/while/body/eval_jaxpr/ppermute | solution.py:19
  808.7 11.9 %collective-permute-start.3 = (f32[25,1,130]{2,1,0:T(1,128)}, f32[25,1,130]{2,1,0:T(1,128)}, u32[]{:S(2)}, u32[]{:S(2)}) collective-permute-start(f32[25,1,130]{2,1,0:T(1,128)} %get-tuple-element.181), channel_id=1, source_target_pairs={{0,16},{16,32},{32,48},{48,64},{64,80},{80,96},{96,112},{1,17},{17... | collective-permute-start | bytes 39008 | tf_op jit(solution)/shard_map/while/body/eval_jaxpr/ppermute | solution.py:17
  (83 other events, 953.2 us)
where the time goes:
time: 934 us; the launch traced here: 929 us
  other arithmetic  394 us (42%)
  local copies, waits for them, and re-layouts  308 us (33%)
  starting transfers between devices  145 us (16%)
  waiting for transfers between devices  60.4 us (6%)
  blocking collectives  19.4 us (2%)
    add x10, other arithmetic, advance(): centre + east_face * (padded[:, 1:-1, 2:] - centre)  175 us
    concatenate x12, other arithmetic, with_halo(): jnp.concatenate([lax.ppermute(tail, axis, [(i, (i + 1) % count) for i in...  144 us
    another operation x23, local copies, waits for them, and re-layouts  72.4 us
    ppermute x22, starting transfers between devices, with_halo(): lax.ppermute(tail, axis, [(i, (i + 1) % count) for i in range(ends)])  66.1 us
    ppermute x22, starting transfers between devices, with_halo(): lax.ppermute(head, axis, [((i + 1) % count, i) for i in range(ends)])  50 us
    ppermute x22, waiting for transfers between devices, with_halo(): lax.ppermute(tail, axis, [(i, (i + 1) % count) for i in range(ends)])  44.4 us
    ppermute x10, local copies, waits for them, and re-layouts, with_halo(): lax.ppermute(tail, axis, [(i, (i + 1) % count) for i in range(ends)])  29.6 us
    ppermute x10, local copies, waits for them, and re-layouts, with_halo(): lax.ppermute(head, axis, [((i + 1) % count, i) for i in range(ends)])  29.4 us
  transfers between devices with their start and end apart: 48, of which 3 were waited for; matrix products, arithmetic and copies ran while one was open for 23% of the time, Pallas kernels for 0%

commit v1 on v0

--- a/solution.py
+++ b/solution.py
@@ -1,67 +1,289 @@
+import functools
+
 import jax
 import jax.numpy as jnp
 from jax import lax
+from jax.experimental import pallas as pl
+from jax.experimental.pallas import tpu as pltpu
 from jax.sharding import PartitionSpec as P
 
 STEPS = 10
-
-
-def with_halo(cells, sides, width, closed):
-    for axis, dim in sides:
-        count = lax.axis_size(axis)
-        ends = count if closed else count - 1
-        head = lax.slice_in_dim(cells, 0, width, axis=dim)
-        tail = lax.slice_in_dim(cells, cells.shape[dim] - width, cells.shape[dim], axis=dim)
-        cells = jnp.concatenate(
-            [
-                lax.ppermute(tail, axis, [(i, (i + 1) % count) for i in range(ends)]),
-                cells,
-                lax.ppermute(head, axis, [((i + 1) % count, i) for i in range(ends)]),
-            ],
-            axis=dim,
+HALO = 16
+LANES = 128
+SLOTS = LANES // HALO
+CHUNK = 8
+EDGE = 4
+MESH = pl.DeviceIdType.MESH
+
+
+def lane_ids(shape):
+    return lax.broadcasted_iota(jnp.int32, shape, len(shape) - 1)
+
+
+def exchange_kernel(
+    n_lat,
+    n_lon,
+    field,
+    coef,
+    west_cols,
+    east_cols,
+    south_field,
+    north_field,
+    south_coef,
+    north_coef,
+    pack_first,
+    pack_last,
+    send_sem,
+    recv_sem,
+):
+    lat = lax.axis_index("lat")
+    lon = lax.axis_index("lon")
+    up = lax.rem(lat + 1, n_lat)
+    down = lax.rem(lat + n_lat - 1, n_lat)
+    right = lax.rem(lon + 1, n_lon)
+    left = lax.rem(lon + n_lon - 1, n_lon)
+    rows = field.shape[1]
+
+    barrier = pltpu.get_barrier_semaphore()
+    for there in (
+        (lat, right),
+        (lat, left),
+        (up, lon),
+        (down, lon),
+        (up, right),
+        (up, left),
+        (down, right),
+        (down, left),
+    ):
+        pl.semaphore_signal(barrier, inc=1, device_id=there, device_id_type=MESH)
+    pl.semaphore_wait(barrier, 8)
+
+    copies = []
+
+    def send(source, target, there):
+        number = len(copies)
+        copy = pltpu.make_async_remote_copy(
+            src_ref=source,
+            dst_ref=target,
+            send_sem=send_sem.at[number],
+            recv_sem=recv_sem.at[number],
+            device_id=there,
+            device_id_type=MESH,
         )
-    return cells
-
-
-def rims(values, width):
-    widened = with_halo(values, (("lon", 2),), width, True)
-    return with_halo(widened, (("lat", 1),), width, False)
-
-
-def face_weights(stack):
-    face_east = stack[0]
-    face_north = stack[1]
-    twist_field = stack[2]
-    wet_cells = stack[3]
-    east_face = face_east[1:-1, 1:-1] * wet_cells[1:-1, 1:-1] * wet_cells[1:-1, 2:]
-    west_face = face_east[1:-1, :-2] * wet_cells[1:-1, :-2] * wet_cells[1:-1, 1:-1]
-    north_face = face_north[1:-1, 1:-1] * wet_cells[1:-1, 1:-1] * wet_cells[2:, 1:-1]
-    south_face = face_north[:-2, 1:-1] * wet_cells[:-2, 1:-1] * wet_cells[1:-1, 1:-1]
-    twist_face = twist_field[1:-1, 1:-1] * wet_cells[1:-1, 1:-1]
-    return (east_face, west_face, north_face, south_face, twist_face)
-
-
-def trimmed(weights, offset):
-    height = weights[0].shape[0]
-    across = weights[0].shape[1]
-    return tuple(
-        (weight[offset : height - offset, offset : across - offset][None] for weight in weights)
-    )
-
-
-def advance(padded, sectioned):
-    east_face, west_face, north_face, south_face, twist_face = sectioned
-    centre = padded[:, 1:-1, 1:-1]
-    return (
-        centre
-        + east_face * (padded[:, 1:-1, 2:] - centre)
-        + west_face * (padded[:, 1:-1, :-2] - centre)
-        + north_face * (padded[:, 2:, 1:-1] - centre)
-        + south_face * (padded[:, :-2, 1:-1] - centre)
-        + 0.25
-        * twist_face
-        * (padded[:, 2:, 2:] - padded[:, 2:, :-2] - padded[:, :-2, 2:] + padded[:, :-2, :-2])
-    )
+        copy.start()
+        copies.append(copy)
+
+    first = pl.ds(0, HALO)
+    last = pl.ds(rows - HALO, HALO)
+    send(field.at[:, last, :], south_field, (up, lon))
+    send(field.at[:, first, :], north_field, (down, lon))
+    send(coef.at[:, last, :], south_coef, (up, lon))
+    send(coef.at[:, first, :], north_coef, (down, lon))
+
+    levels = field.shape[0]
+    planes = levels + coef.shape[0]
+    slot = lane_ids((rows, LANES)) // HALO
+    for tile in range(pack_first.shape[0]):
+        low = jnp.zeros((rows, LANES), jnp.float32)
+        high = jnp.zeros((rows, LANES), jnp.float32)
+        for k in range(SLOTS):
+            plane = tile * SLOTS + k
+            if plane >= planes:
+                continue
+            values = field[plane] if plane < levels else coef[plane - levels]
+            if k:
+                values = pltpu.roll(values, HALO * k, 1)
+            low = jnp.where(slot == k, values, low)
+            high = jnp.where(slot == (k + SLOTS - 1) % SLOTS, values, high)
+        pack_first[tile] = low
+        pack_last[tile] = high
+
+    own = pl.ds(HALO, rows)
+    above = pl.ds(HALO + rows, HALO)
+    send(pack_last, west_cols.at[:, own, :], (lat, right))
+    send(pack_first, east_cols.at[:, own, :], (lat, left))
+    send(pack_last.at[:, last, :], west_cols.at[:, first, :], (up, right))
+    send(pack_first.at[:, last, :], east_cols.at[:, first, :], (up, left))
+    send(pack_last.at[:, first, :], west_cols.at[:, above, :], (down, right))
+    send(pack_first.at[:, first, :], east_cols.at[:, above, :], (down, left))
+    for copy in copies:
+        copy.wait()
+
+
+def exchange(field, coef, n_lat, n_lon):
+    levels, rows, lanes = field.shape
+    planes = levels + coef.shape[0]
+    tiles = -(-planes // SLOTS)
+    whole = pl.BlockSpec(memory_space=pltpu.VMEM)
+    packed = jax.ShapeDtypeStruct((tiles, rows + 2 * HALO, lanes), jnp.float32)
+    edge_field = jax.ShapeDtypeStruct((levels, HALO, lanes), jnp.float32)
+    edge_coef = jax.ShapeDtypeStruct((coef.shape[0], HALO, lanes), jnp.float32)
+    return pl.pallas_call(
+        functools.partial(exchange_kernel, n_lat, n_lon),
+        out_shape=(packed, packed, edge_field, edge_field, edge_coef, edge_coef),
+        in_specs=[whole] * 2,
+        out_specs=[whole] * 6,
+        scratch_shapes=[
+            pltpu.VMEM((tiles, rows, lanes), jnp.float32),
+            pltpu.VMEM((tiles, rows, lanes), jnp.float32),
+            pltpu.SemaphoreType.DMA((10,)),
+            pltpu.SemaphoreType.DMA((10,)),
+        ],
+        compiler_params=pltpu.CompilerParams(
+            collective_id=0, has_side_effects=True, vmem_limit_bytes=40 << 20
+        ),
+    )(field, coef)
+
+
+def rolled(main, side, shift):
+    lanes = lane_ids(main.shape)
+    seam = lanes == (0 if shift == 1 else LANES - 1)
+    main = pltpu.roll(main, shift % LANES, 1)
+    side = pltpu.roll(side, shift % LANES, 1)
+    return jnp.where(seam, side, main), jnp.where(seam, main, side)
+
+
+def diffuse_kernel(
+    n_lat,
+    field,
+    coef,
+    norm,
+    west_cols,
+    east_cols,
+    south_field,
+    north_field,
+    south_coef,
+    north_coef,
+    out,
+    main,
+    side,
+    raw,
+    weights,
+):
+    lat = lax.axis_index("lat")
+    levels, rows, lanes = field.shape
+    tall = rows + 2 * HALO
+    has_south = lat > 0
+    has_north = lat < n_lat - 1
+
+    lane = lane_ids((tall, lanes))
+    row = lax.broadcasted_iota(jnp.int32, (tall, lanes), 0)
+    inside = jnp.logical_and(
+        jnp.logical_or(row >= HALO, has_south), jnp.logical_or(row < HALO + rows, has_north)
+    )
+    from_east = jnp.logical_and(lane < HALO, inside)
+    from_west = jnp.logical_and(lane >= lanes - HALO, inside)
+
+    def side_plane(plane):
+        tile, k = divmod(plane, SLOTS)
+        east = east_cols[tile]
+        west = west_cols[tile]
+        if k:
+            east = pltpu.roll(east, lanes - HALO * k, 1)
+            west = pltpu.roll(west, lanes - HALO * k, 1)
+        return jnp.where(from_east, east, jnp.where(from_west, west, 0.0))
+
+    for level in range(levels):
+        main[0, level, pl.ds(0, HALO), :] = jnp.where(has_south, south_field[level], 0.0)
+        main[0, level, pl.ds(HALO, rows), :] = field[level]
+        main[0, level, pl.ds(HALO + rows, HALO), :] = jnp.where(has_north, north_field[level], 0.0)
+        side[0, level] = side_plane(level)
+    for number in range(coef.shape[0]):
+        raw[number, 0, pl.ds(0, HALO), :] = jnp.where(has_south, south_coef[number], 0.0)
+        raw[number, 0, pl.ds(HALO, rows), :] = coef[number]
+        raw[number, 0, pl.ds(HALO + rows, HALO), :] = jnp.where(
+            has_north, north_coef[number], 0.0
+        )
+        raw[number, 1] = side_plane(levels + number)
+
+    count = (tall - 2 * EDGE) // CHUNK
+
+    def make_weights(step, carry):
+        start = EDGE + step * CHUNK
+        here = pl.ds(start, CHUNK)
+        below = pl.ds(start - 1, CHUNK)
+        above = pl.ds(start + 1, CHUNK)
+        face_x = (raw[0, 0, here, :], raw[0, 1, here, :])
+        cross = (raw[2, 0, here, :], raw[2, 1, here, :])
+        wet = (raw[3, 0, here, :], raw[3, 1, here, :])
+        wet_right = rolled(*wet, -1)
+        east = tuple(face_x[t] * wet[t] * wet_right[t] for t in range(2))
+        west = rolled(*east, 1)
+        twist = tuple(0.25 * cross[t] * wet[t] for t in range(2))
+        twist_right = rolled(*twist, 1)
+        twist_left = rolled(*twist, -1)
+        for t in range(2):
+            north = raw[1, t, here, :] * wet[t] * raw[3, t, above, :]
+            south = raw[1, t, below, :] * raw[3, t, below, :] * wet[t]
+            keep = 1.0 - (east[t] + west[t] + north + south)
+            for number, value in enumerate(
+                (keep, north, south, west[t], twist_right[t], east[t], -twist_left[t])
+            ):
+                weights[number, t, pl.ds(step * CHUNK, CHUNK), :] = value
+        return carry
+
+    lax.fori_loop(0, count, make_weights, 0)
+
+    seam_right = lane_ids((CHUNK, lanes)) == lanes - 1
+    seam_left = lane_ids((CHUNK, lanes)) == 0
+
+    def sweep(source, target):
+        def one_chunk(step, carry):
+            start = EDGE + step * CHUNK
+            here = pl.ds(start, CHUNK)
+            below = pl.ds(start - 1, CHUNK)
+            above = pl.ds(start + 1, CHUNK)
+            own = pl.ds(step * CHUNK, CHUNK)
+            table = [[weights[number, t, own, :] for number in range(7)] for t in range(2)]
+
+            for level in range(levels):
+                partial, going_left, going_right = [], [], []
+                for t, buffer in enumerate((main, side)):
+                    keep, north, south, to_left, twist_left, to_right, twist_right = table[t]
+                    centre = buffer[source, level, here, :]
+                    upper = buffer[source, level, above, :]
+                    lower = buffer[source, level, below, :]
+                    tilt = upper - lower
+                    partial.append(keep * centre + (north * upper + south * lower))
+                    going_left.append(pltpu.roll(to_left * centre + twist_left * tilt, lanes - 1, 1))
+                    going_right.append(pltpu.roll(to_right * centre + twist_right * tilt, 1, 1))
+                for t, buffer in enumerate((main, side)):
+                    buffer[target, level, here, :] = (
+                        partial[t]
+                        + jnp.where(seam_right, going_left[1 - t], going_left[t])
+                        + jnp.where(seam_left, going_right[1 - t], going_right[t])
+                    )
+            return carry
+
+        lax.fori_loop(0, count, one_chunk, 0)
+
+    def two_steps(number, carry):
+        sweep(0, 1)
+        sweep(1, 0)
+        return carry
+
+    lax.fori_loop(0, STEPS // 2, two_steps, 0)
+    for level in range(levels):
+        out[level] = norm[level] * main[0, level, pl.ds(HALO, rows), :]
+
+
+def diffuse(field, coef, norm, halos, n_lat):
+    levels, rows, lanes = field.shape
+    tall = rows + 2 * HALO
+    whole = pl.BlockSpec(memory_space=pltpu.VMEM)
+    return pl.pallas_call(
+        functools.partial(diffuse_kernel, n_lat),
+        out_shape=jax.ShapeDtypeStruct(field.shape, jnp.float32),
+        in_specs=[whole] * (3 + len(halos)),
+        out_specs=whole,
+        scratch_shapes=[
+            pltpu.VMEM((2, levels, tall, lanes), jnp.float32),
+            pltpu.VMEM((2, levels, tall, lanes), jnp.float32),
+            pltpu.VMEM((coef.shape[0], 2, tall, lanes), jnp.float32),
+            pltpu.VMEM((7, 2, tall - 2 * EDGE, lanes), jnp.float32),
+        ],
+        compiler_params=pltpu.CompilerParams(vmem_limit_bytes=56 << 20),
+    )(field, coef, norm, *halos)
 
 
 def on_device(
@@ -121,18 +343,10 @@
     )
     observed = observed.reshape(levels, lat_cells, lon_cells)
     field = norm_factor * (observed + increment)
-    depth = 1
-    stacked = jnp.stack([face_x, face_y, cross_term, wet_mask.astype(jnp.float32)])
-    weights = face_weights(rims(stacked, depth + 1))
-    sectioned_list = [trimmed(weights, 1)]
-
-    def sweep(number, values):
-        padded = rims(values, depth)
-        padded = advance(padded, sectioned_list[0])
-        return padded
-
-    field = lax.fori_loop(0, STEPS // depth, sweep, field)
-    smoothed = norm_factor * field
+    coef = jnp.stack([face_x, face_y, cross_term, wet_mask.astype(jnp.float32)])
+    n_lat = lax.axis_size("lat")
+    halos = exchange(field, coef, n_lat, lax.axis_size("lon"))
+    smoothed = diffuse(field, coef, norm_factor, halos, n_lat)
     flat_field = smoothed.reshape(levels, -1)
     sampled = (
         recv_weights[0][None, :] * flat_field[:, base_cell]

time: 934 us -> 299 us (0.32)
  other arithmetic: 394 us -> 43.5 us
  local copies, waits for them, and re-layouts: 308 us -> 92.7 us
  starting transfers between devices: 145 us -> 27.6 us
  Pallas kernels: 0 us -> 98.9 us
  waiting for transfers between devices: 60.4 us -> 17.5 us
    add x10 -> x0, other arithmetic: 175 us -> none  [advance(): centre + east_face * (padded[:, 1:-1, 2:] - centre)]
    concatenate x12 -> x0, other arithmetic: 144 us -> none  [with_halo(): jnp.concatenate([lax.ppermute(tail, axis, [(i, (i + 1) % count) for i in...]
    ppermute x44 -> x0, starting transfers between devices: 116 us -> none  [the longest x22 66.1 us: with_halo(): lax.ppermute(tail, axis, [(i, (i + 1) % count) for i in range(ends)])]
    pallas_call x0 -> x2, Pallas kernels: none -> 98.9 us  [the longest x1 76.7 us: diffuse(): pl.pallas_call(functools.partial(diffuse_kernel, n_lat), out_shape=jax.Sh...]
    another operation x23 -> x3, local copies, waits for them, and re-layouts: 72.4 us -> 0.03 us
    mul x51 -> x0, local copies, waits for them, and re-layouts: 69.3 us -> none  [the longest x10 16.5 us: advance(): north_face * (padded[:, 2:, 1:-1] - centre)]
    ppermute x20 -> x0, local copies, waits for them, and re-layouts: 59.1 us -> none  [the longest x10 29.6 us: with_halo(): lax.ppermute(tail, axis, [(i, (i + 1) % count) for i in range(ends)])]
    ppermute x44 -> x0, waiting for transfers between devices: 44.4 us -> none  [the longest x22 44.4 us: with_halo(): lax.ppermute(tail, axis, [(i, (i + 1) % count) for i in range(ends)])]
  transfers between devices with their start and end apart: 48 -> 4, of which waited for: 3 -> 2; matrix products, arithmetic and copies ran while one was open for 23% -> 22% of each run, Pallas kernels for 0% -> 0%
where the time goes in v1:
time: 299 us; the launch traced here: 298 us
  Pallas kernels  98.9 us (33%)
  local copies, waits for them, and re-layouts  92.7 us (31%)
  other arithmetic  43.5 us (15%)
  starting transfers between devices  27.6 us (9%)
  waiting for transfers between devices  17.5 us (6%)
  blocking collectives  17.3 us (6%)
    pallas_call x1, Pallas kernels, diffuse(): pl.pallas_call(functools.partial(diffuse_kernel, n_lat), out_shape=jax.Sh...  76.7 us
    scatter-add x1, other arithmetic, on_device(): jnp.zeros((levels, lat_cells * lon_cells), jnp.float32).at[:, corner_cells]  29.1 us
    pallas_call x1, Pallas kernels, exchange(): pl.pallas_call(functools.partial(exchange_kernel, n_lat, n_lon), out_shap...  22.2 us
    all_to_all x1, blocking collectives, on_device(): lax.all_to_all(sampled, ('lat', 'lon'), split_axis=1, concat_axis=1, tile...  17.3 us
    reshape x1, local copies, waits for them, and re-layouts, on_device(): observed = observed.reshape(levels, lat_cells, lon_cells)  11.3 us
    unnamed x42, local copies, waits for them, and re-layouts  11 us
    reshape x1, local copies, waits for them, and re-layouts, on_device(): flat_field = smoothed.reshape(levels, -1)  10.1 us
    all_to_all x1, starting transfers between devices, on_device(): lax.all_to_all(model_ids, 'lon', split_axis=1, concat_axis=1, tiled=True)  9.46 us
  transfers between devices with their start and end apart: 4, of which 2 were waited for; matrix products, arithmetic and copies ran while one was open for 22% of the time, Pallas kernels for 0%

profile of v1, /device:TPU:1, one launch (start us, length us, event | category | flops | bytes accessed | tf_op | source)
XLA Modules:
  0.0 298.5 jit_solution(7373156215561432327)
XLA Ops:
  1.2 1.2 reduce.30
  2.4 0.7 all_to_all.31
  3.1 9.5 %all-to-all-start.2 = ((s32[1,16,2]{2,0,1:T(1,128)}), s32[1,16,2]{2,0,1:T(1,128)S(1)}, u32[]{:S(2)}, u32[]{:S(2)}) async-start(s32[1,16,2]{2,0,1:T(1,128)} %bitcast.14), calls=%async_computation.2 | async-start | bytes 16384 | tf_op jit(solution)/shard_map/all_to_all | solution.py:308
  12.6 0.8 copy.92
  13.7 0.9 fusion.10
  14.6 0.7 compare_select_fusion.5
  15.3 0.7 multiply_add_fusion
  16.0 2.4 scatter_custom_fusion
  18.4 0.7 all_to_all.27
  19.1 0.9 maximum_bitcast_fusion.1
  20.2 1.8 scatter_custom_fusion.1
  22.0 1.0 reshape.493
  23.2 4.1 %copy.111 = f32[25,32,8,128]{3,2,0,1:T(8,128)} copy(f32[25,32,8,128]{3,2,1,0:T(8,128)} %param.17) | data formatting | bytes 6553600 | tf_op args[5]
  27.3 9.3 %all-to-all-start = ((s32[1,128,8]{2,0,1:T(1,128)}), s32[1,128,8]{2,0,1:T(1,128)S(1)}, u32[]{:S(2)}, u32[]{:S(2)}) async-start(s32[1,128,8]{2,0,1:T(1,128)} %bitcast.7), calls=%async_computation | async-start | bytes 131072 | tf_op jit(solution)/shard_map/all_to_all | solution.py:330
  37.2 9.0 %all-to-all-done = s32[1,128,8]{2,0,1:T(1,128)S(1)} async-done(((s32[1,128,8]{2,0,1:T(1,128)}), s32[1,128,8]{2,0,1:T(1,128)S(1)}, u32[]{:S(2)}, u32[]{:S(2)}) %all-to-all-start) | async-done | bytes 4128 | tf_op jit(solution)/shard_map/all_to_all | solution.py:330
  46.2 4.3 %all-to-all-start.1 = ((f32[128,1,232]{2,1,0:T(1,128)}), f32[128,1,232]{2,1,0:T(1,128)S(1)}, u32[]{:S(2)}, u32[]{:S(2)}) async-start(f32[128,1,232]{2,1,0:T(1,128)} %reshape.493), calls=%async_computation.1 | async-start | bytes 262144 | tf_op jit(solution)/shard_map/all_to_all | solution.py:329
  50.5 1.3 add_reduce_fusion
  52.2 8.5 %all-to-all-done.1 = f32[128,1,232]{2,1,0:T(1,128)S(1)} async-done(((f32[128,1,232]{2,1,0:T(1,128)}), f32[128,1,232]{2,1,0:T(1,128)S(1)}, u32[]{:S(2)}, u32[]{:S(2)}) %all-to-all-start.1) | async-done | bytes 118816 | tf_op jit(solution)/shard_map/all_to_all | solution.py:329
  60.6 4.6 %all-to-all-start.3 = ((f32[25,32,8,128]{3,2,0,1:T(8,128)}), f32[25,32,8,128]{3,2,0,1:T(8,128)}, u32[]{:S(2)}, u32[]{:S(2)}) async-start(f32[25,32,8,128]{3,2,0,1:T(8,128)} %copy.111), calls=%async_computation.3 | async-start | bytes 6553600 | tf_op jit(solution)/shard_map/all_to_all | solution.py:307
  65.9 0.9 reduce.33
  67.1 2.0 slice_reduce_fusion.3
  70.9 0.6 copy.108
  71.6 29.1 %scatter_custom_fusion.2 = f32[25,32768]{0,1:T(8,128)} fusion(s32[4096]{0:T(1024)S(1)} %bitcast.128, f32[4096,25]{1,0:T(8,128)S(1)} %copy.108, f32[]{:T(128)} %constant.13.clone.1), kind=kCustom, calls=%fused_computation.9 | custom fusion | flops 102400 | bytes 3276804 | tf_op jit(solution)/shard_map/scatter-add | solution.py:342
  100.7 11.3 %copy.121 = f32[25,256,128]{2,1,0:T(8,128)} copy(f32[25,256,128]{0,2,1:T(8,128)} %bitcast.108) | data formatting | bytes 6553600 | tf_op jit(solution)/shard_map/reshape | solution.py:344
  112.0 0.8 copy.134
  112.8 0.8 copy.133
  113.6 0.8 copy.132
  114.4 0.8 copy.131
  115.3 2.1 broadcast_in_dim.11
  117.3 7.6 %scatter_fusion = f32[25,32,8,128]{3,2,1,0:T(8,128)} fusion(f32[25,32,8,128]{3,2,1,0:T(8,128)} %broadcast_in_dim.11, s32[32]{0:T(128)S(1)} %fusion.18, f32[32,25,8,128]{3,2,1,0:T(8,128)} %bitcast.16), kind=kCustom, calls=%fused_computation.8 | custom fusion | bytes 9830528 | tf_op jit(solution)/shard_map/scatter | solution.py:310
  125.0 4.7 %fusion.2.field = f32[25,256,128]{2,1,0:T(8,128)S(1)} fusion(f32[25,256,128]{2,1,0:T(8,128)} %norm.1, f32[25,256,128]{2,1,0:T(8,128)} %copy.121, f32[25,32,8,128]{3,2,1,0:T(8,128)} %scatter_fusion), kind=kLoop, calls=%fused_computation.12 | loop fusion | flops 1638400 | bytes 13107200 | tf_op jit(solution)/shard_map/mul | solution.py:345
  129.7 22.2 %shard_map.131 = (f32[4,288,128]{2,1,0:T(8,128)S(1)}, f32[4,288,128]{2,1,0:T(8,128)S(1)}, f32[25,16,128]{2,1,0:T(8,128)S(1)}, f32[25,16,128]{2,1,0:T(8,128)S(1)}...) custom-call(f32[25,256,128]{2,1,0:T(8,128)S(1)} %fusion.2.field, f32[4,256,128]{2,1,0:T(8,128)S(1)} %pad_maximum_fusion.coef), custom_call_target="tpu_custom_call" | custom-call | tf_op jit(solution)/shard_map/pallas_call | solution.py:121
  151.9 0.8 copy-done.2
  152.8 0.8 copy-done.3
  153.6 0.7 copy-done.4
  154.2 0.7 copy-done.5
  155.0 0.6 copy-done.6
  156.2 76.7 %shard_map.132 = f32[25,256,128]{2,1,0:T(8,128)} custom-call(f32[25,256,128]{2,1,0:T(8,128)} %copy-done, f32[4,256,128]{2,1,0:T(8,128)} %copy-done.1, f32[25,256,128]{2,1,0:T(8,128)} %norm.1, f32[4,288,128]{2,1,0:T(8,128)} %copy-done.2, f32[4,288,128]{2,1,0:T(8,128)} %copy-done.3, f32[25,16,128]{2,1,0:T(8,128)} %copy-done.4, f32[25,16,128]{2,1,0:T(8,128)} %copy-done.5, ...), custom_call_target="tpu_custom_call" | custom-call | tf_op jit(solution)/shard_map/pallas_call | solution.py:274
  232.8 10.1 %copy.122 = f32[25,256,128]{0,2,1:T(8,128)} copy(f32[25,256,128]{2,1,0:T(8,128)} %shard_map.132) | data formatting | bytes 6553600 | tf_op jit(solution)/shard_map/reshape | solution.py:350
  242.9 8.6 %gather_fusion.3 = f32[1024,25]{1,0:T(8,128)S(1)} fusion(f32[25,32768]{0,1:T(8,128)} %bitcast.109, s32[1024]{0:T(1024)S(1)} %get-tuple-element.46), kind=kCustom, calls=%fused_computation.3 | custom fusion | bytes 208896 | tf_op jit(solution)/shard_map/gather | solution.py:355
  251.5 8.6 %gather_fusion.2 = f32[1024,25]{1,0:T(8,128)S(1)} fusion(f32[25,32768]{0,1:T(8,128)} %bitcast.110, s32[1024]{0:T(1024)S(1)} %get-tuple-element.47), kind=kCustom, calls=%fused_computation.2 | custom fusion | bytes 208896 | tf_op jit(solution)/shard_map/gather | solution.py:354
  260.1 8.6 %gather_fusion.1 = f32[1024,25]{1,0:T(8,128)S(1)} fusion(f32[25,32768]{0,1:T(8,128)} %bitcast.111, s32[1024]{0:T(1024)S(1)} %get-tuple-element.48), kind=kCustom, calls=%fused_computation.1 | custom fusion | bytes 208896 | tf_op jit(solution)/shard_map/gather | solution.py:353
  268.6 8.6 %gather_fusion = f32[1024,25]{1,0:T(8,128)S(1)} fusion(f32[25,32768]{0,1:T(8,128)} %bitcast.112, s32[1024]{0:T(1024)S(1)} %broadcast_clamp_fusion.3), kind=kCustom, calls=%fused_computation | custom fusion | bytes 208896 | tf_op jit(solution)/shard_map/gather | solution.py:352
  277.2 0.6 fusion.19
  278.2 17.3 %all_to_all.41 = f32[128,1,200]{2,1,0:T(1,128)S(1)} all-to-all(f32[128,1,200]{2,1,0:T(1,128)S(1)} %reshape.495), channel_id=1, replica_groups=mesh['lat'=8,'lon'=16] {'lat','lon'}, dimensions={0} | all-to-all | bytes 204800 | tf_op jit(solution)/shard_map/all_to_all | solution.py:357
  295.5 0.9 reduce.34
  296.7 1.0 gather_fusion.4
  297.7 0.8 copy.120
  (72 shorter events, 6.0 us)
Async XLA Ops:
  0.6 22.5 %copy-start.12 = (s32[256,128]{1,0:T(8,128)S(1)}, s32[256,128]{1,0:T(8,128)}, u32[]{:S(2)}) copy-start(s32[256,128]{1,0:T(8,128)} %param.22) | copy-start | bytes 393220
  0.6 22.5 %copy-start.13 = (f32[256,128]{1,0:T(8,128)S(1)}, f32[256,128]{1,0:T(8,128)}, u32[]{:S(2)}) copy-start(f32[256,128]{1,0:T(8,128)} %param.21) | copy-start | bytes 393220
  0.7 22.5 %copy-start.14 = (f32[256,128]{1,0:T(8,128)S(1)}, f32[256,128]{1,0:T(8,128)}, u32[]{:S(2)}) copy-start(f32[256,128]{1,0:T(8,128)} %param.20) | copy-start | bytes 393220
  0.7 22.5 %copy-start.15 = (f32[256,128]{1,0:T(8,128)S(1)}, f32[256,128]{1,0:T(8,128)}, u32[]{:S(2)}) copy-start(f32[256,128]{1,0:T(8,128)} %param.19) | copy-start | bytes 393220
  3.1 24.2 %all-to-all-start.2 = ((s32[1,16,2]{2,0,1:T(1,128)}), s32[1,16,2]{2,0,1:T(1,128)S(1)}, u32[]{:S(2)}, u32[]{:S(2)}) async-start(s32[1,16,2]{2,0,1:T(1,128)} %bitcast.14), calls=%async_computation.2 | async-start | bytes 16384 | tf_op jit(solution)/shard_map/all_to_all | solution.py:308
  23.2 106.5 %copy-start.1 = (f32[4,256,128]{2,1,0:T(8,128)}, f32[4,256,128]{2,1,0:T(8,128)S(1)}, u32[]{:S(2)}) copy-start(f32[4,256,128]{2,1,0:T(8,128)S(1)} %pad_maximum_fusion.coef) | copy-start | bytes 1572868
  27.3 19.0 %all-to-all-start = ((s32[1,128,8]{2,0,1:T(1,128)}), s32[1,128,8]{2,0,1:T(1,128)S(1)}, u32[]{:S(2)}, u32[]{:S(2)}) async-start(s32[1,128,8]{2,0,1:T(1,128)} %bitcast.7), calls=%async_computation | async-start | bytes 131072 | tf_op jit(solution)/shard_map/all_to_all | solution.py:330
  46.2 14.4 %all-to-all-start.1 = ((f32[128,1,232]{2,1,0:T(1,128)}), f32[128,1,232]{2,1,0:T(1,128)S(1)}, u32[]{:S(2)}, u32[]{:S(2)}) async-start(f32[128,1,232]{2,1,0:T(1,128)} %reshape.493), calls=%async_computation.1 | async-start | bytes 262144 | tf_op jit(solution)/shard_map/all_to_all | solution.py:329
  60.6 54.6 %all-to-all-start.3 = ((f32[25,32,8,128]{3,2,0,1:T(8,128)}), f32[25,32,8,128]{3,2,0,1:T(8,128)}, u32[]{:S(2)}, u32[]{:S(2)}) async-start(f32[25,32,8,128]{3,2,0,1:T(8,128)} %copy.111), calls=%async_computation.3 | async-start | bytes 6553600 | tf_op jit(solution)/shard_map/all_to_all | solution.py:307
  100.7 11.3 %copy-start.11 = (f32[1,128,8]{0,2,1:T(8,128)S(1)}, f32[1,128,8]{0,2,1:T(8,128)}, u32[]{:S(2)}) copy-start(f32[1,128,8]{0,2,1:T(8,128)} %get-tuple-element.35) | copy-start | bytes 12292
  100.7 12.1 %copy-start.10 = (f32[1,128,8]{0,2,1:T(8,128)S(1)}, f32[1,128,8]{0,2,1:T(8,128)}, u32[]{:S(2)}) copy-start(f32[1,128,8]{0,2,1:T(8,128)} %get-tuple-element.34) | copy-start | bytes 12292
  100.7 12.9 %copy-start.9 = (f32[1,128,8]{0,2,1:T(8,128)S(1)}, f32[1,128,8]{0,2,1:T(8,128)}, u32[]{:S(2)}) copy-start(f32[1,128,8]{0,2,1:T(8,128)} %get-tuple-element.33) | copy-start | bytes 12292
  100.7 13.8 %copy-start.8 = (f32[1,128,8]{0,2,1:T(8,128)S(1)}, f32[1,128,8]{0,2,1:T(8,128)}, u32[]{:S(2)}) copy-start(f32[1,128,8]{0,2,1:T(8,128)} %get-tuple-element.32) | copy-start | bytes 12292
  129.7 26.5 %copy-start = (f32[25,256,128]{2,1,0:T(8,128)}, f32[25,256,128]{2,1,0:T(8,128)S(1)}, u32[]{:S(2)}) copy-start(f32[25,256,128]{2,1,0:T(8,128)S(1)} %fusion.2.field) | copy-start | bytes 9830404
  151.9 0.8 copy-start.2
  152.8 0.8 copy-start.3
  153.6 0.7 copy-start.4
  154.2 0.7 copy-start.5
  155.0 0.6 copy-start.6
  155.6 0.6 copy-start.7

commit v2 on v1

v2 whole, which is shorter than its diff:
```python
import functools

import jax
import jax.numpy as jnp
from jax import lax
from jax.experimental import pallas as pl
from jax.experimental.pallas import tpu as pltpu
from jax.sharding import PartitionSpec as P

STEPS = 10
CAPACITY = 8
PAD = 32
HALO = 16
LANES = 128
COLS = 12
PAIRS = 5
CHUNK = 40
EDGE = 4
MESH = pl.DeviceIdType.MESH


def lane_ids(shape):
    return lax.broadcasted_iota(jnp.int32, shape, len(shape) - 1)


def exchange_kernel(
    n_lat,
    n_lon,
    field,
    coef,
    west_cols,
    east_cols,
    south_field,
    north_field,
    south_coef,
    north_coef,
    pack_first,
    pack_last,
    send_sem,
    recv_sem,
):
    lat = lax.axis_index("lat")
    lon = lax.axis_index("lon")
    up = lax.rem(lat + 1, n_lat)
    down = lax.rem(lat + n_lat - 1, n_lat)
    right = lax.rem(lon + 1, n_lon)
    left = lax.rem(lon + n_lon - 1, n_lon)
    rows = field.shape[1]

    barrier = pltpu.get_barrier_semaphore()
    for there in (
        (lat, right),
        (lat, left),
        (up, lon),
        (down, lon),
        (up, right),
        (up, left),
        (down, right),
        (down, left),
    ):
        pl.semaphore_signal(barrier, inc=1, device_id=there, device_id_type=MESH)
    pl.semaphore_wait(barrier, 8)

    copies = []

    def send(source, target, there):
        number = len(copies)
        copy = pltpu.make_async_remote_copy(
            src_ref=source,
            dst_ref=target,
            send_sem=send_sem.at[number],
            recv_sem=recv_sem.at[number],
            device_id=there,
            device_id_type=MESH,
        )
        copy.start()
        copies.append(copy)

    first = pl.ds(0, HALO)
    last = pl.ds(rows - HALO, HALO)
    send(field.at[:, last, :], south_field, (up, lon))
    send(field.at[:, first, :], north_field, (down, lon))
    send(coef.at[:, last, :], south_coef, (up, lon))
    send(coef.at[:, first, :], north_coef, (down, lon))

    levels = field.shape[0]
    planes = levels + (levels % 2) + coef.shape[0]
    lane = lane_ids((rows, LANES))

    def within(start):
        start = start % LANES
        return jnp.logical_and(lane >= start, lane < start + COLS)

    for tile in range(pack_first.shape[0]):
        low = jnp.zeros((rows, LANES), jnp.float32)
        high = jnp.zeros((rows, LANES), jnp.float32)
        for k in range(PAIRS):
            for half in range(2):
                plane = 2 * (tile * PAIRS + k) + half
                if plane >= planes or levels <= plane < levels + (levels % 2):
                    continue
                values = field[plane] if plane < levels else coef[plane - planes + coef.shape[0]]
                shift = COLS * k + (LANES // 2) * half
                if shift:
                    values = pltpu.roll(values, shift, 1)
                low = jnp.where(within(shift), values, low)
                high = jnp.where(within(LANES - COLS + shift), values, high)
        pack_first[tile] = low
        pack_last[tile] = high

    own = pl.ds(HALO, rows)
    above = pl.ds(HALO + rows, HALO)
    send(pack_last, west_cols.at[:, own, :], (lat, right))
    send(pack_first, east_cols.at[:, own, :], (lat, left))
    send(pack_last.at[:, last, :], west_cols.at[:, first, :], (up, right))
    send(pack_first.at[:, last, :], east_cols.at[:, first, :], (up, left))
    send(pack_last.at[:, first, :], west_cols.at[:, above, :], (down, right))
    send(pack_first.at[:, first, :], east_cols.at[:, above, :], (down, left))
    for copy in copies:
        copy.wait()


def exchange(field, coef, n_lat, n_lon):
    levels, rows, lanes = field.shape
    pairs = (levels + 1) // 2 + coef.shape[0] // 2
    tiles = -(-pairs // PAIRS)
    whole = pl.BlockSpec(memory_space=pltpu.VMEM)
    packed = jax.ShapeDtypeStruct((tiles, rows + 2 * HALO, lanes), jnp.float32)
    edge_field = jax.ShapeDtypeStruct((levels, HALO, lanes), jnp.float32)
    edge_coef = jax.ShapeDtypeStruct((coef.shape[0], HALO, lanes), jnp.float32)
    return pl.pallas_call(
        functools.partial(exchange_kernel, n_lat, n_lon),
        out_shape=(packed, packed, edge_field, edge_field, edge_coef, edge_coef),
        in_specs=[whole] * 2,
        out_specs=[whole] * 6,
        scratch_shapes=[
            pltpu.VMEM((tiles, rows, lanes), jnp.float32),
            pltpu.VMEM((tiles, rows, lanes), jnp.float32),
            pltpu.SemaphoreType.DMA((10,)),
            pltpu.SemaphoreType.DMA((10,)),
        ],
        compiler_params=pltpu.CompilerParams(
            collective_id=0, has_side_effects=True, vmem_limit_bytes=40 << 20
        ),
    )(field, coef)


def diffuse_kernel(
    n_lat,
    field,
    coef,
    norm,
    west_cols,
    east_cols,
    south_field,
    north_field,
    south_coef,
    north_coef,
    corner_weights,
    corner_cells,
    out,
    sampled,
    grid,
    other,
    raw,
    weights,
    turned,
):
    lat = lax.axis_index("lat")
    levels, rows, lanes = field.shape
    tall = rows + 2 * HALO
    half = lanes // 2
    strips = (levels + 1) // 2
    has_south = lat > 0
    has_north = lat < n_lat - 1

    lane = lane_ids((tall, lanes)) % half
    upper_half = lane_ids((tall, lanes)) >= half
    row = lax.broadcasted_iota(jnp.int32, (tall, lanes), 0)
    inside = jnp.logical_and(
        jnp.logical_or(row >= HALO, has_south), jnp.logical_or(row < HALO + rows, has_north)
    )
    west_side = lane < half // 2
    from_west = lane < COLS
    from_east = lane >= half - COLS

    def turn(values, shift):
        shift = shift % lanes
        return pltpu.roll(values, shift, 1) if shift else values

    def strip(pair, first, second):
        tile, k = divmod(pair, PAIRS)
        low = jnp.where(west_side, turn(first, COLS), turn(first, half - COLS))
        high = jnp.where(west_side, turn(second, COLS + half), turn(second, -COLS))
        own = jnp.where(upper_half, high, low)
        east = turn(east_cols[tile], half - COLS - COLS * k)
        west = turn(west_cols[tile], COLS - COLS * k)
        halo = jnp.where(inside, jnp.where(from_east, east, west), 0.0)
        return jnp.where(jnp.logical_or(from_east, from_west), halo, own)

    for level in range(levels):
        grid[level, pl.ds(0, HALO), :] = jnp.where(has_south, south_field[level], 0.0)
        grid[level, pl.ds(HALO, rows), :] = field[level]
        grid[level, pl.ds(HALO + rows, HALO), :] = jnp.where(has_north, north_field[level], 0.0)
    for number in range(coef.shape[0]):
        raw[0, number, pl.ds(0, HALO), :] = jnp.where(has_south, south_coef[number], 0.0)
        raw[0, number, pl.ds(HALO, rows), :] = coef[number]
        raw[0, number, pl.ds(HALO + rows, HALO), :] = jnp.where(
            has_north, north_coef[number], 0.0
        )
    for pair in range(strips):
        first = grid[2 * pair]
        second = grid[min(2 * pair + 1, levels - 1)]
        grid[levels + pair] = strip(pair, first, second)
    for number in range(0, coef.shape[0], 2):
        pair = strips + number // 2
        for offset in range(2):
            plane = raw[0, number + offset]
            both = strip(pair, plane, plane)
            mirrored = turn(both, half)
            raw[1, number + offset] = jnp.where(
                upper_half, mirrored if offset == 0 else both, both if offset == 0 else mirrored
            )

    count = (tall - 2 * EDGE) // CHUNK

    def make_weights(step, carry):
        start = EDGE + step * CHUNK
        here = pl.ds(start, CHUNK)
        below = pl.ds(start - 1, CHUNK)
        above = pl.ds(start + 1, CHUNK)
        for kind in range(2):
            wet = raw[kind, 3, here, :]
            east = raw[kind, 0, here, :] * wet * turn(wet, -1)
            west = turn(east, 1)
            twist = 0.25 * raw[kind, 2, here, :] * wet
            north = raw[kind, 1, here, :] * wet * raw[kind, 3, above, :]
            south = raw[kind, 1, below, :] * raw[kind, 3, below, :] * wet
            keep = 1.0 - (east + west + north + south)
            for number, value in enumerate(
                (keep, north, south, west, turn(twist, 1), east, -turn(twist, -1))
            ):
                weights[kind, number, pl.ds(step * CHUNK, CHUNK), :] = value
        return carry

    lax.fori_loop(0, count, make_weights, 0)

    def sweep(source, target):
        def one_chunk(step, carry):
            start = EDGE + step * CHUNK
            here = pl.ds(start, CHUNK)
            below = pl.ds(start - 1, CHUNK)
            above = pl.ds(start + 1, CHUNK)
            own = pl.ds(step * CHUNK, CHUNK)
            for kind, planes in enumerate((range(levels), range(levels, levels + strips))):
                keep, north, south, to_left, twist_left, to_right, twist_right = (
                    weights[kind, number, own, :] for number in range(7)
                )
                for plane in planes:
                    centre = source[plane, here, :]
                    upper = source[plane, above, :]
                    lower = source[plane, below, :]
                    tilt = upper - lower
                    target[plane, here, :] = (
                        keep * centre
                        + (north * upper + south * lower)
                        + turn(to_left * centre + twist_left * tilt, -1)
                        + turn(to_right * centre + twist_right * tilt, 1)
                    )
            return carry

        lax.fori_loop(0, count, one_chunk, 0)

    def two_steps(number, carry):
        sweep(grid, other)
        sweep(other, grid)
        return carry

    lax.fori_loop(0, STEPS // 2, two_steps, 0)

    column = lane_ids((rows, lanes))
    inner = pl.ds(HALO, rows)
    for level in range(levels):
        edges = grid[levels + level // 2, inner, :]
        move = half * (level % 2)
        result = jnp.where(
            column < STEPS,
            turn(edges, -COLS - move),
            jnp.where(column >= lanes - STEPS, turn(edges, half + COLS - move), grid[level, inner, :]),
        )
        result = norm[level] * result
        out[level] = result
        turned[pl.ds(level, rows, stride=PAD), :] = result
    for level in range(levels, PAD):
        turned[pl.ds(level, rows, stride=PAD), :] = jnp.zeros((rows, lanes), jnp.float32)

    spots = corner_cells.shape[0] // 2
    lane8 = lane_ids((8, lanes))
    lane32 = lane_ids((PAD, lanes))

    def sample_tile(tile, carry):
        def sample_group(group, found):
            for u in range(8):
                spot = tile * lanes + group * 8 + u
                lower, upper = corner_masks(corner_weights, corner_cells, spot, spots, lane8)
                start = pl.multiple_of(corner_cells[spot] * PAD, PAD)
                low = turned[pl.ds(start, PAD), :].reshape(PAD // 8, 8, lanes)
                high = turned[pl.ds(start + PAD, PAD), :].reshape(PAD // 8, 8, lanes)
                total = jnp.sum((low * lower + high * upper).reshape(PAD, lanes), axis=1, keepdims=True)
                found = jnp.where(lane32 == group * 8 + u, total, found)
            return found

        found = lax.fori_loop(0, lanes // 8, sample_group, jnp.zeros((PAD, lanes), jnp.float32))
        square = jnp.concatenate([found, jnp.zeros((lanes - PAD, lanes), jnp.float32)], axis=0)
        sampled[pl.ds(pl.multiple_of(tile * lanes, lanes), lanes), :] = square.T
        return carry

    lax.fori_loop(0, spots // lanes, sample_tile, 0)


def diffuse(field, coef, norm, halos, corner_weights, corner_cells, n_lat):
    levels, rows, lanes = field.shape
    tall = rows + 2 * HALO
    whole = pl.BlockSpec(memory_space=pltpu.VMEM)
    scalars = pl.BlockSpec(memory_space=pltpu.SMEM)
    planes = levels + (levels + 1) // 2
    return pl.pallas_call(
        functools.partial(diffuse_kernel, n_lat),
        out_shape=(
            jax.ShapeDtypeStruct(field.shape, jnp.float32),
            jax.ShapeDtypeStruct((corner_cells.shape[0] // 2, lanes), jnp.float32),
        ),
        in_specs=[whole] * (3 + len(halos)) + [scalars] * 2,
        out_specs=(whole, whole),
        scratch_shapes=[
            pltpu.VMEM((planes, tall, lanes), jnp.float32),
            pltpu.VMEM((planes, tall, lanes), jnp.float32),
            pltpu.VMEM((2, coef.shape[0], tall, lanes), jnp.float32),
            pltpu.VMEM((2, 7, tall - 2 * EDGE, lanes), jnp.float32),
            pltpu.VMEM((rows * PAD, lanes), jnp.float32),
        ],
        compiler_params=pltpu.CompilerParams(vmem_limit_bytes=56 << 20),
    )(field, coef, norm, *halos, corner_weights, corner_cells)


def corner_masks(corner_weights, corner_cells, spot, spots, lane):
    column = corner_cells[spots + spot]
    here = lane == column
    beside = lane == column + 1
    lower = jnp.where(
        here, corner_weights[spot], jnp.where(beside, corner_weights[spots + spot], 0.0)
    )
    upper = jnp.where(
        here,
        corner_weights[2 * spots + spot],
        jnp.where(beside, corner_weights[3 * spots + spot], 0.0),
    )
    return lower, upper


def route_kernel(innovations, weights, place, owner_column, owner_row, ids, packet, slots, table):
    levels, count = innovations.shape
    total = packet.shape[0]
    same = owner_column[...] == owner_row[...]
    earlier = lax.broadcasted_iota(jnp.int32, (count, count), 0) < lax.broadcasted_iota(
        jnp.int32, (count, count), 1
    )
    rank = jnp.sum(jnp.where(jnp.logical_and(same, earlier), 1, 0), axis=0, keepdims=True)
    slot = owner_row[...] * CAPACITY + rank
    slots[...] = slot

    table[...] = jnp.zeros_like(table)
    table[pl.ds(0, levels), :] = innovations[...]
    table[pl.ds(levels, 4), :] = weights[...]
    table[pl.ds(levels + 4, 2), :] = place[...].astype(jnp.float32)
    flipped = jnp.concatenate(
        [table[:, pl.ds(start, LANES)].T for start in range(0, count, LANES)], axis=0
    )
    chosen = lax.broadcasted_iota(jnp.int32, (total, count), 0) == slot
    sent = jnp.dot(
        jnp.where(chosen, 1.0, 0.0),
        flipped,
        precision=lax.Precision.HIGHEST,
        preferred_element_type=jnp.float32,
    )
    lane = lane_ids((total, LANES))
    group = lax.broadcasted_iota(jnp.int32, (total, LANES), 0) // CAPACITY
    per_device = 2
    group = lax.rem(group, ids.shape[1] // per_device) * per_device
    numbers = jnp.concatenate(
        [ids[...].astype(jnp.float32), jnp.zeros((1, LANES - ids.shape[1]), jnp.float32)], axis=1
    )
    for t in range(per_device):
        number = jnp.sum(jnp.where(lane == group + t, numbers, 0.0), axis=1, keepdims=True)
        sent = jnp.where(lane == PAD + t, number, sent)
    packet[...] = sent


def route(innovations, weights, place, owners, ids, devices):
    whole = pl.BlockSpec(memory_space=pltpu.VMEM)
    count = innovations.shape[1]
    return pl.pallas_call(
        route_kernel,
        out_shape=(
            jax.ShapeDtypeStruct((devices * CAPACITY, LANES), jnp.float32),
            jax.ShapeDtypeStruct((1, count), jnp.int32),
        ),
        in_specs=[whole] * 6,
        out_specs=(whole, whole),
        scratch_shapes=[pltpu.VMEM((LANES, count), jnp.float32)],
        compiler_params=pltpu.CompilerParams(vmem_limit_bytes=32 << 20),
    )(innovations, weights, place, owners, owners.reshape(1, count), ids)


def spread_kernel(levels, corner_weights, corner_cells, packet, observed, first, second):
    total, lanes = packet.shape
    lane8 = lane_ids((8, lanes))
    is_level = lax.broadcasted_iota(jnp.int32, (PAD, lanes), 0) < levels
    parts = (first, second)
    for part in parts:
        part[...] = jnp.zeros_like(part)

    def spread_tile(tile, carry):
        start = pl.multiple_of(tile * lanes, lanes)
        values = jnp.where(is_level, packet[pl.ds(start, lanes), :].T[:PAD], 0.0)

        def spread_group(group, carry):
            moved = pltpu.roll(values, lax.rem(lanes - group * 8, lanes), 1)
            for u in range(8):
                spot = tile * lanes + group * 8 + u
                lower, upper = corner_masks(corner_weights, corner_cells, spot, total, lane8)
                value = jnp.broadcast_to(moved[:, u : u + 1], (PAD, lanes)).reshape(
                    PAD // 8, 8, lanes
                )
                added = jnp.concatenate(
                    [(value * lower).reshape(PAD, lanes), (value * upper).reshape(PAD, lanes)], axis=0
                )
                where = pl.ds(pl.multiple_of(corner_cells[spot] * PAD, PAD), 2 * PAD)
                part = parts[u % len(parts)]
                part[where, :] = part[where, :] + added
            return carry

        lax.fori_loop(0, lanes // 8, spread_group, 0)
        return carry

    lax.fori_loop(0, total // lanes, spread_tile, 0)
    observed[...] = first[...] + second[...]


def spread(corner_weights, corner_cells, packet, levels, rows):
    lanes = packet.shape[1]
    whole = pl.BlockSpec(memory_space=pltpu.VMEM)
    scalars = pl.BlockSpec(memory_space=pltpu.SMEM)
    return pl.pallas_call(
        functools.partial(spread_kernel, levels),
        out_shape=jax.ShapeDtypeStruct((rows * PAD, lanes), jnp.float32),
        in_specs=[scalars, scalars, whole],
        out_specs=whole,
        scratch_shapes=[pltpu.VMEM((rows * PAD, lanes), jnp.float32)] * 2,
        compiler_params=pltpu.CompilerParams(vmem_limit_bytes=40 << 20),
    )(corner_weights, corner_cells, packet)


def combine_kernel(ids, observed, tiles, norm, field):
    slots, levels, depth, lanes = tiles.shape

    def one_tile(slot, carry):
        row = pl.multiple_of(ids[slot] * depth, depth)
        rows = pl.ds(row, depth)
        for level in range(levels):
            seen = observed[pl.ds(row * PAD + level, depth, stride=PAD), :]
            field[level, rows, :] = norm[level, rows, :] * (seen + tiles[slot, level])
        return carry

    lax.fori_loop(0, slots, one_tile, 0)


def combine(ids, observed, tiles, norm):
    whole = pl.BlockSpec(memory_space=pltpu.VMEM)
    return pl.pallas_call(
        combine_kernel,
        out_shape=jax.ShapeDtypeStruct(norm.shape, jnp.float32),
        in_specs=[pl.BlockSpec(memory_space=pltpu.SMEM)] + [whole] * 3,
        out_specs=whole,
        compiler_params=pltpu.CompilerParams(vmem_limit_bytes=40 << 20),
    )(ids, observed, tiles, norm)


def collect_kernel(levels, returned, slots, out):
    total, lanes = returned.shape
    count = slots.shape[1]
    flipped = jnp.concatenate(
        [returned[pl.ds(start, lanes), :].T[:PAD] for start in range(0, total, lanes)], axis=1
    )
    chosen = lax.broadcasted_iota(jnp.int32, (total, count), 0) == slots[...]
    values = jnp.dot(
        flipped,
        jnp.where(chosen, 1.0, 0.0),
        precision=lax.Precision.HIGHEST,
        preferred_element_type=jnp.float32,
    )
    out[...] = values[:levels]


def collect(returned, slots, levels):
    whole = pl.BlockSpec(memory_space=pltpu.VMEM)
    return pl.pallas_call(
        functools.partial(collect_kernel, levels),
        out_shape=jax.ShapeDtypeStruct((levels, slots.shape[1]), jnp.float32),
        in_specs=[whole] * 2,
        out_specs=whole,
        compiler_params=pltpu.CompilerParams(vmem_limit_bytes=32 << 20),
    )(returned, slots)


def on_device(
    innovations,
    owners,
    prof_row,
    prof_col,
    interp_weights,
    model_tiles,
    model_ids,
    face_x,
    face_y,
    cross_term,
    wet_mask,
    norm_factor,
):
    levels, rows, lanes = norm_factor.shape
    n_lat = lax.axis_size("lat")
    n_lon = lax.axis_size("lon")
    devices = n_lat * n_lon
    both = ("lat", "lon")
    place = jnp.stack([prof_row, prof_col])
    packet, slots = route(innovations, interp_weights, place, owners, model_ids, devices)
    packet = lax.all_to_all(packet.reshape(devices, CAPACITY, LANES), both, 0, 0, tiled=True)
    tiles = lax.all_to_all(model_tiles, "lon", split_axis=1, concat_axis=1, tiled=True)
    tiles = jnp.transpose(tiles, (1, 0, 2, 3))
    same_lat = lax.dynamic_slice_in_dim(packet[:, 0], lax.axis_index("lat") * n_lon, n_lon, 0)
    ids = same_lat[:, PAD : PAD + 2].reshape(-1).astype(jnp.int32)
    packet = packet.reshape(devices * CAPACITY, LANES)
    corner_weights = packet[:, levels : levels + 4].T.reshape(-1)
    corner_cells = packet[:, levels + 4 : levels + 6].T.reshape(-1).astype(jnp.int32)
    observed = spread(corner_weights, corner_cells, packet, levels, rows)
    field = combine(ids, observed, tiles, norm_factor)
    coef = jnp.stack([face_x, face_y, cross_term, wet_mask.astype(jnp.float32)])
    halos = exchange(field, coef, n_lat, n_lon)
    smoothed, sampled = diffuse(
        field, coef, norm_factor, halos, corner_weights, corner_cells, n_lat
    )
    returned = lax.all_to_all(sampled.reshape(devices, CAPACITY, LANES), both, 0, 0, tiled=True)
    profile_values = collect(returned.reshape(devices * CAPACITY, LANES), slots, levels)
    return (smoothed, profile_values)


def solution(mesh):
    in_specs = (
        P(None, ("lat", "lon")),
        P(("lat", "lon"), None),
        P(("lat", "lon")),
        P(("lat", "lon")),
        P(None, ("lat", "lon")),
        P(None, ("lat", "lon"), None, None),
        P(None, ("lat", "lon")),
        P("lat", "lon"),
        P("lat", "lon"),
        P("lat", "lon"),
        P("lat", "lon"),
        P(None, "lat", "lon"),
    )
    out_specs = (P(None, "lat", "lon"), P(None, ("lat", "lon")))
    return jax.shard_map(
        on_device, mesh=mesh, in_specs=in_specs, out_specs=out_specs, check_vma=False
    )
```

time: 299 us -> 207 us (0.69)
  local copies, waits for them, and re-layouts: 92.7 us -> 19.7 us
  other arithmetic: 43.5 us -> 3.91 us
  Pallas kernels: 98.9 us -> 125 us
  starting transfers between devices: 27.6 us -> 16.1 us
  blocking collectives: 17.3 us -> 23.5 us
    gather x5 -> x0, local copies, waits for them, and re-layouts: 35.3 us -> none  [the longest x1 8.57 us: on_device(): flat_field[:, base_cell + lon_cells]]
    scatter-add x1 -> x0, other arithmetic: 29.1 us -> none  [on_device(): jnp.zeros((levels, lat_cells * lon_cells), jnp.float32).at[:, corner_cells]]
    pallas_call x1 -> x5, Pallas kernels: 76.7 us -> 102 us  [the longest x1 66.5 us: diffuse(): pl.pallas_call(functools.partial(diffuse_kernel, n_lat), out_shape=(jax.S...]
    reshape x2 -> x0, local copies, waits for them, and re-layouts: 21.4 us -> none  [the longest x1 11.3 us: on_device(): observed = observed.reshape(levels, lat_cells, lon_cells)]
    scatter x3 -> x0, local copies, waits for them, and re-layouts: 11.9 us -> none  [the longest x1 7.63 us: on_device(): increment = jnp.zeros_like(moved_tiles).at[:, moved_ids[0]].set(moved_tiles)]
    all_to_all x3 -> x1, starting transfers between devices: 23 us -> 11.5 us  [on_device(): lax.all_to_all(packet.reshape(devices, CAPACITY, LANES), both, 0, 0, tile...]
    all_to_all x3 -> x1, waiting for transfers between devices: 17.5 us -> 9.91 us  [on_device(): lax.all_to_all(packet.reshape(devices, CAPACITY, LANES), both, 0, 0, tile...]
    all_to_all x1, waiting for transfers between devices: 0.01 us -> 7.05 us  [on_device(): lax.all_to_all(model_tiles, 'lon', split_axis=1, concat_axis=1, tiled=True)]
  transfers between devices with their start and end apart: 4 -> 2, of which waited for: 2 -> 2; matrix products, arithmetic and copies ran while one was open for 22% -> 5% of each run, Pallas kernels for 0% -> 13%
where the time goes in v2:
time: 207 us; the launch traced here: 206 us
  Pallas kernels  125 us (60%)
  blocking collectives  23.5 us (11%)
  local copies, waits for them, and re-layouts  19.7 us (10%)
  waiting for transfers between devices  17 us (8%)
  starting transfers between devices  16.1 us (8%)
  other arithmetic  3.91 us (2%)
    pallas_call x1, Pallas kernels, diffuse(): pl.pallas_call(functools.partial(diffuse_kernel, n_lat), out_shape=(jax.S...  66.5 us
    pallas_call x1, Pallas kernels, spread(): pl.pallas_call(functools.partial(spread_kernel, levels), out_shape=jax.Sh...  26.2 us
    all_to_all x1, blocking collectives, on_device(): lax.all_to_all(sampled.reshape(devices, CAPACITY, LANES), both, 0, 0, til...  23.5 us
    pallas_call x1, Pallas kernels, exchange(): pl.pallas_call(functools.partial(exchange_kernel, n_lat, n_lon), out_shap...  22.7 us
    unnamed x50, local copies, waits for them, and re-layouts  16.9 us
    all_to_all x1, starting transfers between devices, on_device(): lax.all_to_all(packet.reshape(devices, CAPACITY, LANES), both, 0, 0, tile...  11.5 us
    all_to_all x1, waiting for transfers between devices, on_device(): lax.all_to_all(packet.reshape(devices, CAPACITY, LANES), both, 0, 0, tile...  9.91 us
    all_to_all x1, waiting for transfers between devices, on_device(): lax.all_to_all(model_tiles, 'lon', split_axis=1, concat_axis=1, tiled=True)  7.05 us
  transfers between devices with their start and end apart: 2, of which 2 were waited for; matrix products, arithmetic and copies ran while one was open for 5% of the time, Pallas kernels for 13%

profile of v2, /device:TPU:1, one launch (start us, length us, event | category | flops | bytes accessed | tf_op | source)
XLA Modules:
  0.0 206.1 jit_solution(937861274190449668)
XLA Ops:
  0.6 0.8 copy.16.owner_column
  1.5 0.7 pad_add_fusion.place
  2.2 0.8 copy-done.13
  3.0 0.7 copy-done.16
  3.7 0.7 copy-done.17
  4.4 0.7 copy-done.18
  5.0 3.1 %shard_map.131 = (f32[1024,128]{1,0:T(8,128)}, s32[1,512]{1,0:T(1,128)S(1)}) custom-call(f32[25,512]{1,0:T(8,128)S(1)} %copy-done.13, f32[4,512]{1,0:T(4,128)S(1)} %copy-done.17, s32[2,512]{1,0:T(2,128)S(1)} %pad_add_fusion.place, s32[512,1]{1,0:T(8,128)S(1)} %copy.16.owner_column, s32[1,512]{1,0:T(1,128)S(1)} %bitcast.34, s32[1,32]{1,0:T(1,128)S(1)} %copy-done.18), custom_call_target="tpu_custom_call" | custom-call | tf_op jit(solution)/shard_map/pallas_call | solution.py:402
  8.2 11.5 %all-to-all-start = ((f32[128,8,128]{2,1,0:T(8,128)}), f32[128,8,128]{2,1,0:T(8,128)S(1)}, u32[]{:S(2)}, u32[]{:S(2)}) async-start(f32[128,8,128]{2,1,0:T(8,128)} %bitcast.3), calls=%async_computation | async-start | bytes 1048576 | tf_op jit(solution)/shard_map/all_to_all | solution.py:537
  19.7 3.8 %copy.19 = f32[25,32,8,128]{3,2,0,1:T(8,128)} copy(f32[25,32,8,128]{3,2,1,0:T(8,128)} %param.17) | data formatting | bytes 6553600 | tf_op args[5]
  23.5 9.9 %all-to-all-done = f32[128,8,128]{2,1,0:T(8,128)S(1)} async-done(((f32[128,8,128]{2,1,0:T(8,128)}), f32[128,8,128]{2,1,0:T(8,128)S(1)}, u32[]{:S(2)}, u32[]{:S(2)}) %all-to-all-start) | async-done | bytes 524320 | tf_op jit(solution)/shard_map/all_to_all | solution.py:537
  33.4 4.6 %all-to-all-start.1 = ((f32[25,32,8,128]{3,2,0,1:T(8,128)}), f32[25,32,8,128]{3,2,0,1:T(8,128)}, u32[]{:S(2)}, u32[]{:S(2)}) async-start(f32[25,32,8,128]{3,2,0,1:T(8,128)} %copy.19), calls=%async_computation.1 | async-start | bytes 6553600 | tf_op jit(solution)/shard_map/all_to_all | solution.py:538
  38.1 0.0 copy-done.19
  38.1 0.0 copy-done.20
  38.1 0.0 copy-done.21
  38.1 0.0 copy-done.22
  38.1 0.9 pad_maximum_fusion.coef
  39.0 0.0 copy-done.4
  39.0 0.2 slice_bitcast_fusion
  39.2 0.2 copy.17
  39.4 2.2 %fusion = s32[2,1024]{0,1:T(8,128)} fusion(f32[1024,128]{1,0:T(8,128)} %bitcast.27), kind=kLoop, calls=%fused_computation.1 | loop fusion | flops 2048 | bytes 16384 | tf_op jit(solution)/shard_map/convert_element_type | solution.py:544
  41.6 1.2 copy.18
  42.9 1.1 slice.16
  44.0 0.1 slice_convert_fusion.1
  44.1 0.1 convert_element_type.16.ids
  44.2 0.0 copy-start.5
  44.2 1.0 copy-done.5
  45.2 26.2 %shard_map.132.observed = f32[8192,128]{1,0:T(8,128)S(1)} custom-call(f32[4096]{0:T(1024)S(1)} %bitcast.30, s32[2048]{0:T(1024)S(1)} %bitcast.32, f32[1024,128]{1,0:T(8,128)S(1)} %bitcast.28), custom_call_target="tpu_custom_call" | custom-call | tf_op jit(solution)/shard_map/pallas_call | solution.py:454
  71.4 0.0 copy-start.1
  71.4 1.9 copy-done.1
  73.4 7.1 %all-to-all-done.1 = f32[25,32,8,128]{3,2,0,1:T(8,128)} async-done(((f32[25,32,8,128]{3,2,0,1:T(8,128)}), f32[25,32,8,128]{3,2,0,1:T(8,128)}, u32[]{:S(2)}, u32[]{:S(2)}) %all-to-all-start.1) | async-done | bytes 3276832 | tf_op jit(solution)/shard_map/all_to_all | solution.py:538
  80.4 0.0 copy-done.3
  80.4 2.2 %copy-done.2 = f32[8192,128]{1,0:T(8,128)S(1)} copy-done((f32[8192,128]{1,0:T(8,128)S(1)}, f32[8192,128]{1,0:T(8,128)}, u32[]{:S(2)}) %copy-start.2) | copy-done | bytes 4194328
  82.6 4.4 %shard_map.133.field = f32[25,256,128]{2,1,0:T(8,128)S(1)} custom-call(s32[32]{0:T(128)S(1)} %convert_element_type.16.ids, f32[8192,128]{1,0:T(8,128)S(1)} %copy-done.2, f32[32,25,8,128]{3,2,1,0:T(8,128)} %bitcast.8.tiles, f32[25,256,128]{2,1,0:T(8,128)S(1)} %copy-done.3), custom_call_target="tpu_custom_call" | custom-call | tf_op jit(solution)/shard_map/pallas_call | solution.py:480
  87.1 0.0 copy-done.11
  87.1 0.0 copy-done.12
  87.1 0.0 copy-done.6
  87.1 0.0 copy-start
  87.1 22.7 %shard_map.134 = (f32[3,288,128]{2,1,0:T(8,128)S(1)}, f32[3,288,128]{2,1,0:T(8,128)S(1)}, f32[25,16,128]{2,1,0:T(8,128)S(1)}, f32[25,16,128]{2,1,0:T(8,128)S(1)}...) custom-call(f32[25,256,128]{2,1,0:T(8,128)S(1)} %shard_map.133.field, f32[4,256,128]{2,1,0:T(8,128)S(1)} %copy-done.6), custom_call_target="tpu_custom_call" | custom-call | tf_op jit(solution)/shard_map/pallas_call | solution.py:131
  109.8 0.0 copy-start.7
  109.8 0.8 copy-done.7
  110.6 0.8 copy-done.8
  111.4 0.7 copy-done.9
  112.0 0.7 copy-done.10
  112.7 0.6 copy-done.14
  113.3 0.6 copy-done.15
  113.9 66.5 %shard_map.135 = (f32[25,256,128]{2,1,0:T(8,128)}, f32[1024,128]{1,0:T(8,128)}) custom-call(f32[25,256,128]{2,1,0:T(8,128)} %copy-done, f32[4,256,128]{2,1,0:T(8,128)} %pad_maximum_fusion.coef, f32[25,256,128]{2,1,0:T(8,128)} %norm.3, f32[3,288,128]{2,1,0:T(8,128)} %copy-done.7, f32[3,288,128]{2,1,0:T(8,128)} %copy-done.8, f32[25,16,128]{2,1,0:T(8,128)} %copy-done.9, ...), custom_call_target="tpu_custom_call" | custom-call | tf_op jit(solution)/shard_map/pallas_call | solution.py:327
  180.5 23.5 %all_to_all.15 = f32[128,8,128]{2,1,0:T(8,128)S(1)} all-to-all(f32[128,8,128]{2,1,0:T(8,128)} %bitcast.35), channel_id=1, replica_groups=mesh['lat'=8,'lon'=16] {'lat','lon'}, dimensions={0} | all-to-all | bytes 1048576 | tf_op jit(solution)/shard_map/all_to_all | solution.py:552
  204.0 2.1 %shard_map.136 = f32[25,512]{1,0:T(8,128)} custom-call(f32[1024,128]{1,0:T(8,128)S(1)} %bitcast.29, s32[1,512]{1,0:T(1,128)S(1)} %get-tuple-element.21.slots), custom_call_target="tpu_custom_call" | custom-call | tf_op jit(solution)/shard_map/pallas_call | solution.py:507
  (24 shorter events, 0.1 us)
Async XLA Ops:
  2.2 0.8 copy-start.13
  3.0 0.7 copy-start.16
  3.7 0.7 copy-start.17
  4.4 0.7 copy-start.18
  8.2 25.3 %all-to-all-start = ((f32[128,8,128]{2,1,0:T(8,128)}), f32[128,8,128]{2,1,0:T(8,128)S(1)}, u32[]{:S(2)}, u32[]{:S(2)}) async-start(f32[128,8,128]{2,1,0:T(8,128)} %bitcast.3), calls=%async_computation | async-start | bytes 1048576 | tf_op jit(solution)/shard_map/all_to_all | solution.py:537
  23.5 14.5 %copy-start.19 = (s32[256,128]{1,0:T(8,128)S(1)}, s32[256,128]{1,0:T(8,128)}, u32[]{:S(2)}) copy-start(s32[256,128]{1,0:T(8,128)} %param.22) | copy-start | bytes 393220
  23.5 14.6 %copy-start.20 = (f32[256,128]{1,0:T(8,128)S(1)}, f32[256,128]{1,0:T(8,128)}, u32[]{:S(2)}) copy-start(f32[256,128]{1,0:T(8,128)} %param.21) | copy-start | bytes 393220
  23.5 14.6 %copy-start.21 = (f32[256,128]{1,0:T(8,128)S(1)}, f32[256,128]{1,0:T(8,128)}, u32[]{:S(2)}) copy-start(f32[256,128]{1,0:T(8,128)} %param.20) | copy-start | bytes 393220
  23.5 14.6 %copy-start.22 = (f32[256,128]{1,0:T(8,128)S(1)}, f32[256,128]{1,0:T(8,128)}, u32[]{:S(2)}) copy-start(f32[256,128]{1,0:T(8,128)} %param.19) | copy-start | bytes 393220
  33.4 5.6 %copy-start.4 = (f32[128,8,128]{2,1,0:T(8,128)}, f32[128,8,128]{2,1,0:T(8,128)S(1)}, u32[]{:S(2)}) copy-start(f32[128,8,128]{2,1,0:T(8,128)S(1)} %all-to-all-done) | copy-start | bytes 1572868
  33.4 47.0 %all-to-all-start.1 = ((f32[25,32,8,128]{3,2,0,1:T(8,128)}), f32[25,32,8,128]{3,2,0,1:T(8,128)}, u32[]{:S(2)}, u32[]{:S(2)}) async-start(f32[25,32,8,128]{3,2,0,1:T(8,128)} %copy.19), calls=%async_computation.1 | async-start | bytes 6553600 | tf_op jit(solution)/shard_map/all_to_all | solution.py:538
  39.4 41.0 %copy-start.3 = (f32[25,256,128]{2,1,0:T(8,128)S(1)}, f32[25,256,128]{2,1,0:T(8,128)}, u32[]{:S(2)}) copy-start(f32[25,256,128]{2,1,0:T(8,128)} %norm.3) | copy-start | bytes 9830404
  39.4 47.6 %copy-start.11 = (f32[1,8,4,128]{3,1,2,0:T(8,128)}, f32[1,8,4,128]{3,1,2,0:T(8,128)S(1)}, u32[]{:S(2)}) copy-start(f32[1,8,4,128]{3,1,2,0:T(8,128)S(1)} %copy.24) | copy-start | bytes 49156
  42.9 44.2 %copy-start.12 = (s32[1,8,2,128]{3,1,2,0:T(8,128)}, s32[1,8,2,128]{3,1,2,0:T(8,128)S(1)}, u32[]{:S(2)}) copy-start(s32[1,8,2,128]{3,1,2,0:T(8,128)S(1)} %copy.25) | copy-start | bytes 24580
  44.2 1.0 copy-start.5
  71.4 2.0 copy-start.1
  80.4 2.2 %copy-start.2 = (f32[8192,128]{1,0:T(8,128)S(1)}, f32[8192,128]{1,0:T(8,128)}, u32[]{:S(2)}) copy-start(f32[8192,128]{1,0:T(8,128)} %copy-done.1) | copy-start | bytes 12582916
  82.6 4.5 %copy-start.6 = (f32[4,256,128]{2,1,0:T(8,128)S(1)}, f32[4,256,128]{2,1,0:T(8,128)}, u32[]{:S(2)}) copy-start(f32[4,256,128]{2,1,0:T(8,128)} %pad_maximum_fusion.coef) | copy-start | bytes 1572868
  87.1 26.9 %copy-start = (f32[25,256,128]{2,1,0:T(8,128)}, f32[25,256,128]{2,1,0:T(8,128)S(1)}, u32[]{:S(2)}) copy-start(f32[25,256,128]{2,1,0:T(8,128)S(1)} %shard_map.133.field) | copy-start | bytes 9830404
  109.8 0.8 copy-start.7
  110.6 0.8 copy-start.8
  111.4 0.7 copy-start.9
  112.0 0.7 copy-start.10
  112.7 0.6 copy-start.14
  113.3 0.6 copy-start.15

commit v3 on v2

--- a/solution.py
+++ b/solution.py
@@ -10,6 +10,7 @@
 STEPS = 10
 CAPACITY = 8
 PAD = 32
+UNROLL = 32
 HALO = 16
 LANES = 128
 COLS = 12
@@ -165,6 +166,7 @@
     raw,
     weights,
     turned,
+    gathered,
 ):
     lat = lax.axis_index("lat")
     levels, rows, lanes = field.shape
@@ -294,28 +296,33 @@
     for level in range(levels, PAD):
         turned[pl.ds(level, rows, stride=PAD), :] = jnp.zeros((rows, lanes), jnp.float32)
 
-    spots = corner_cells.shape[0] // 2
     lane8 = lane_ids((8, lanes))
-    lane32 = lane_ids((PAD, lanes))
+    lane_pad = lane_ids((PAD, lanes))
+    per_row = lanes // PAD
 
     def sample_tile(tile, carry):
-        def sample_group(group, found):
-            for u in range(8):
-                spot = tile * lanes + group * 8 + u
-                lower, upper = corner_masks(corner_weights, corner_cells, spot, spots, lane8)
-                start = pl.multiple_of(corner_cells[spot] * PAD, PAD)
-                low = turned[pl.ds(start, PAD), :].reshape(PAD // 8, 8, lanes)
-                high = turned[pl.ds(start + PAD, PAD), :].reshape(PAD // 8, 8, lanes)
-                total = jnp.sum((low * lower + high * upper).reshape(PAD, lanes), axis=1, keepdims=True)
-                found = jnp.where(lane32 == group * 8 + u, total, found)
-            return found
-
-        found = lax.fori_loop(0, lanes // 8, sample_group, jnp.zeros((PAD, lanes), jnp.float32))
-        square = jnp.concatenate([found, jnp.zeros((lanes - PAD, lanes), jnp.float32)], axis=0)
-        sampled[pl.ds(pl.multiple_of(tile * lanes, lanes), lanes), :] = square.T
-        return carry
-
-    lax.fori_loop(0, spots // lanes, sample_tile, 0)
+        for q in range(per_row):
+            block = tile * per_row + q
+
+            def sample_group(group, found):
+                for u in range(UNROLL):
+                    spot = group * UNROLL + u
+                    row, lower, upper = corner_masks(corner_weights, corner_cells, block, spot, lane8)
+                    start = pl.multiple_of(row * PAD, PAD)
+                    low = turned[pl.ds(start, PAD), :].reshape(PAD // 8, 8, lanes)
+                    high = turned[pl.ds(start + PAD, PAD), :].reshape(PAD // 8, 8, lanes)
+                    mixed = (low * lower + high * upper).reshape(PAD, lanes)
+                    total = jnp.sum(mixed, axis=1, keepdims=True)
+                    found = jnp.where(lane_pad == spot, total, found)
+                return found
+
+            gathered[pl.ds(PAD * q, PAD), :] = lax.fori_loop(
+                0, lanes // UNROLL, sample_group, jnp.zeros((PAD, lanes), jnp.float32)
+            )
+        sampled[pl.ds(pl.multiple_of(tile * lanes, lanes), lanes), :] = gathered[...].T
+        return carry
+
+    lax.fori_loop(0, sampled.shape[0] // lanes, sample_tile, 0)
 
 
 def diffuse(field, coef, norm, halos, corner_weights, corner_cells, n_lat):
@@ -328,7 +335,7 @@
         functools.partial(diffuse_kernel, n_lat),
         out_shape=(
             jax.ShapeDtypeStruct(field.shape, jnp.float32),
-            jax.ShapeDtypeStruct((corner_cells.shape[0] // 2, lanes), jnp.float32),
+            jax.ShapeDtypeStruct((corner_cells.shape[0] * PAD, lanes), jnp.float32),
         ),
         in_specs=[whole] * (3 + len(halos)) + [scalars] * 2,
         out_specs=(whole, whole),
@@ -338,24 +345,26 @@
             pltpu.VMEM((2, coef.shape[0], tall, lanes), jnp.float32),
             pltpu.VMEM((2, 7, tall - 2 * EDGE, lanes), jnp.float32),
             pltpu.VMEM((rows * PAD, lanes), jnp.float32),
+            pltpu.VMEM((lanes, lanes), jnp.float32),
         ],
         compiler_params=pltpu.CompilerParams(vmem_limit_bytes=56 << 20),
     )(field, coef, norm, *halos, corner_weights, corner_cells)
 
 
-def corner_masks(corner_weights, corner_cells, spot, spots, lane):
-    column = corner_cells[spots + spot]
+def corner_masks(corner_weights, corner_cells, block, spot, lane):
+    column = corner_cells[block, 6, spot]
     here = lane == column
     beside = lane == column + 1
-    lower = jnp.where(
-        here, corner_weights[spot], jnp.where(beside, corner_weights[spots + spot], 0.0)
-    )
-    upper = jnp.where(
-        here,
-        corner_weights[2 * spots + spot],
-        jnp.where(beside, corner_weights[3 * spots + spot], 0.0),
-    )
-    return lower, upper
+    first, second, third, fourth = (corner_weights[block, 1 + c, spot] for c in range(4))
+    lower = jnp.where(here, first, jnp.where(beside, second, 0.0))
+    upper = jnp.where(here, third, jnp.where(beside, fourth, 0.0))
+    return corner_cells[block, 5, spot], lower, upper
+
+
+def one_hot_slots(slots, q, rows):
+    shape = (rows, slots.shape[1])
+    number = lax.broadcasted_iota(jnp.int32, shape, 0) * (LANES // PAD) + q
+    return jnp.where(number == slots, 1.0, 0.0)
 
 
 def route_kernel(innovations, weights, place, owner_column, owner_row, ids, packet, slots, table):
@@ -376,23 +385,28 @@
     flipped = jnp.concatenate(
         [table[:, pl.ds(start, LANES)].T for start in range(0, count, LANES)], axis=0
     )
-    chosen = lax.broadcasted_iota(jnp.int32, (total, count), 0) == slot
-    sent = jnp.dot(
-        jnp.where(chosen, 1.0, 0.0),
-        flipped,
-        precision=lax.Precision.HIGHEST,
-        preferred_element_type=jnp.float32,
-    )
+    sent = jnp.zeros((total, LANES), jnp.float32)
+    for q in range(LANES // PAD):
+        moved = pltpu.roll(flipped, PAD * q, 1) if q else flipped
+        sent += jnp.dot(
+            one_hot_slots(slot, q, total),
+            moved,
+            precision=lax.Precision.HIGHEST,
+            preferred_element_type=jnp.float32,
+        )
     lane = lane_ids((total, LANES))
-    group = lax.broadcasted_iota(jnp.int32, (total, LANES), 0) // CAPACITY
+    row = lax.broadcasted_iota(jnp.int32, (total, LANES), 0)
     per_device = 2
-    group = lax.rem(group, ids.shape[1] // per_device) * per_device
+    row_group = CAPACITY * PAD // LANES
+    group = lax.rem(row // row_group, ids.shape[1] // per_device) * per_device
+    first_row = lax.rem(row, row_group) == 0
     numbers = jnp.concatenate(
         [ids[...].astype(jnp.float32), jnp.zeros((1, LANES - ids.shape[1]), jnp.float32)], axis=1
     )
     for t in range(per_device):
         number = jnp.sum(jnp.where(lane == group + t, numbers, 0.0), axis=1, keepdims=True)
-        sent = jnp.where(lane == PAD + t, number, sent)
+        spare = jnp.logical_and(first_row, lane == PAD * (t + 1) - 1)
+        sent = jnp.where(spare, number, sent)
     packet[...] = sent
 
 
@@ -402,7 +416,7 @@
     return pl.pallas_call(
         route_kernel,
         out_shape=(
-            jax.ShapeDtypeStruct((devices * CAPACITY, LANES), jnp.float32),
+            jax.ShapeDtypeStruct((devices * CAPACITY * PAD // LANES, LANES), jnp.float32),
             jax.ShapeDtypeStruct((1, count), jnp.int32),
         ),
         in_specs=[whole] * 6,
@@ -412,60 +426,159 @@
     )(innovations, weights, place, owners, owners.reshape(1, count), ids)
 
 
-def spread_kernel(levels, corner_weights, corner_cells, packet, observed, first, second):
+def post_kernel(n_lat, n_lon, source, target, send_sem, recv_sem, local_sem):
+    lat = lax.axis_index("lat")
+    lon = lax.axis_index("lon")
+    me = lat * n_lon + lon
+    devices = n_lat * n_lon
+    barrier = pltpu.get_barrier_semaphore()
+
+    def there(step):
+        other = lax.rem(me + step, devices)
+        return other, (other // n_lon, lax.rem(other, n_lon))
+
+    def greet(step, carry):
+        pl.semaphore_signal(barrier, inc=1, device_id=there(step)[1], device_id_type=MESH)
+        return carry
+
+    def transfer(step):
+        other, device = there(step)
+        return pltpu.make_async_remote_copy(
+            src_ref=source.at[other],
+            dst_ref=target.at[me],
+            send_sem=send_sem.at[step],
+            recv_sem=recv_sem.at[step],
+            device_id=device,
+            device_id_type=MESH,
+        )
+
+    def send(step, carry):
+        transfer(step).start()
+        return carry
+
+    def arrive(step, carry):
+        transfer(step).wait()
+        return carry
+
+    own = pltpu.make_async_copy(source.at[me], target.at[me], local_sem)
+    own.start()
+    lax.fori_loop(1, devices, greet, 0)
+    pl.semaphore_wait(barrier, devices - 1)
+    lax.fori_loop(1, devices, send, 0)
+    lax.fori_loop(1, devices, arrive, 0)
+    own.wait()
+
+
+def post(packet, n_lat, n_lon, collective_id):
+    devices = n_lat * n_lon
+    whole = pl.BlockSpec(memory_space=pltpu.VMEM)
+    blocks = packet.reshape(devices, -1, LANES)
+    received = pl.pallas_call(
+        functools.partial(post_kernel, n_lat, n_lon),
+        out_shape=jax.ShapeDtypeStruct(blocks.shape, jnp.float32),
+        in_specs=[whole],
+        out_specs=whole,
+        scratch_shapes=[
+            pltpu.SemaphoreType.DMA((devices,)),
+            pltpu.SemaphoreType.DMA((devices,)),
+            pltpu.SemaphoreType.DMA,
+        ],
+        compiler_params=pltpu.CompilerParams(
+            collective_id=collective_id, has_side_effects=True, vmem_limit_bytes=16 << 20
+        ),
+    )(blocks)
+    return received.reshape(packet.shape)
+
+
+def spread_kernel(
+    levels, packet, observed, weights_out, cells_out, turned, other, weights, cells, sems
+):
     total, lanes = packet.shape
+    per_row = lanes // PAD
+    tiles = total // lanes
     lane8 = lane_ids((8, lanes))
+    for tile in range(tiles):
+        flipped = packet[pl.ds(tile * lanes, lanes), :].T
+        turned[pl.ds(tile * lanes, lanes), :] = flipped
+        for q in range(per_row):
+            last = flipped[PAD * (q + 1) - 8 : PAD * (q + 1)]
+            weights_out[tile * per_row + q] = last
+            cells_out[tile * per_row + q] = last.astype(jnp.int32)
+    copies = (
+        pltpu.make_async_copy(weights_out, weights, sems.at[0]),
+        pltpu.make_async_copy(cells_out, cells, sems.at[1]),
+    )
+    for copy in copies:
+        copy.start()
     is_level = lax.broadcasted_iota(jnp.int32, (PAD, lanes), 0) < levels
-    parts = (first, second)
+    parts = (observed, other)
     for part in parts:
         part[...] = jnp.zeros_like(part)
-
-    def spread_tile(tile, carry):
-        start = pl.multiple_of(tile * lanes, lanes)
-        values = jnp.where(is_level, packet[pl.ds(start, lanes), :].T[:PAD], 0.0)
+    for copy in copies:
+        copy.wait()
+
+    def spread_block(block, carry):
+        values = jnp.where(is_level, turned[pl.ds(pl.multiple_of(block * PAD, PAD), PAD), :], 0.0)
 
         def spread_group(group, carry):
-            moved = pltpu.roll(values, lax.rem(lanes - group * 8, lanes), 1)
-            for u in range(8):
-                spot = tile * lanes + group * 8 + u
-                lower, upper = corner_masks(corner_weights, corner_cells, spot, total, lane8)
+            moved = pltpu.roll(values, lax.rem(lanes - group * UNROLL, lanes), 1)
+            for u in range(UNROLL):
+                spot = group * UNROLL + u
+                row, lower, upper = corner_masks(weights, cells, block, spot, lane8)
                 value = jnp.broadcast_to(moved[:, u : u + 1], (PAD, lanes)).reshape(
                     PAD // 8, 8, lanes
                 )
                 added = jnp.concatenate(
                     [(value * lower).reshape(PAD, lanes), (value * upper).reshape(PAD, lanes)], axis=0
                 )
-                where = pl.ds(pl.multiple_of(corner_cells[spot] * PAD, PAD), 2 * PAD)
+                where = pl.ds(pl.multiple_of(row * PAD, PAD), 2 * PAD)
                 part = parts[u % len(parts)]
                 part[where, :] = part[where, :] + added
             return carry
 
-        lax.fori_loop(0, lanes // 8, spread_group, 0)
-        return carry
-
-    lax.fori_loop(0, total // lanes, spread_tile, 0)
-    observed[...] = first[...] + second[...]
-
-
-def spread(corner_weights, corner_cells, packet, levels, rows):
-    lanes = packet.shape[1]
+        lax.fori_loop(0, lanes // UNROLL, spread_group, 0)
+        return carry
+
+    lax.fori_loop(0, tiles * per_row, spread_block, 0)
+    observed[...] = observed[...] + other[...]
+
+
+def spread(packet, levels, rows):
+    total, lanes = packet.shape
     whole = pl.BlockSpec(memory_space=pltpu.VMEM)
-    scalars = pl.BlockSpec(memory_space=pltpu.SMEM)
+    blocks = total // PAD
     return pl.pallas_call(
         functools.partial(spread_kernel, levels),
-        out_shape=jax.ShapeDtypeStruct((rows * PAD, lanes), jnp.float32),
-        in_specs=[scalars, scalars, whole],
-        out_specs=whole,
-        scratch_shapes=[pltpu.VMEM((rows * PAD, lanes), jnp.float32)] * 2,
+        out_shape=(
+            jax.ShapeDtypeStruct((rows * PAD, lanes), jnp.float32),
+            jax.ShapeDtypeStruct((blocks, 8, lanes), jnp.float32),
+            jax.ShapeDtypeStruct((blocks, 8, lanes), jnp.int32),
+        ),
+        in_specs=[whole],
+        out_specs=(whole, whole, whole),
+        scratch_shapes=[
+            pltpu.VMEM(packet.shape, jnp.float32),
+            pltpu.VMEM((rows * PAD, lanes), jnp.float32),
+            pltpu.SMEM((blocks, 8, lanes), jnp.float32),
+            pltpu.SMEM((blocks, 8, lanes), jnp.int32),
+            pltpu.SemaphoreType.DMA((2,)),
+        ],
         compiler_params=pltpu.CompilerParams(vmem_limit_bytes=40 << 20),
-    )(corner_weights, corner_cells, packet)
-
-
-def combine_kernel(ids, observed, tiles, norm, field):
+    )(packet)
+
+
+def combine_kernel(cells, observed, tiles, norm, field):
     slots, levels, depth, lanes = tiles.shape
+    n_lon = lax.axis_size("lon")
+    per_device = slots // n_lon
+    per_row = lanes // PAD
+    row_group = CAPACITY * PAD // lanes
+    base = lax.axis_index("lat") * n_lon
 
     def one_tile(slot, carry):
-        row = pl.multiple_of(ids[slot] * depth, depth)
+        at = (base + slot // per_device) * row_group
+        block = (at // lanes) * per_row + lax.rem(slot, per_device)
+        row = pl.multiple_of(cells[block, 7, lax.rem(at, lanes)] * depth, depth)
         rows = pl.ds(row, depth)
         for level in range(levels):
             seen = observed[pl.ds(row * PAD + level, depth, stride=PAD), :]
@@ -475,7 +588,7 @@
     lax.fori_loop(0, slots, one_tile, 0)
 
 
-def combine(ids, observed, tiles, norm):
+def combine(cells, observed, tiles, norm):
     whole = pl.BlockSpec(memory_space=pltpu.VMEM)
     return pl.pallas_call(
         combine_kernel,
@@ -483,22 +596,22 @@
         in_specs=[pl.BlockSpec(memory_space=pltpu.SMEM)] + [whole] * 3,
         out_specs=whole,
         compiler_params=pltpu.CompilerParams(vmem_limit_bytes=40 << 20),
-    )(ids, observed, tiles, norm)
+    )(cells, observed, tiles, norm)
 
 
 def collect_kernel(levels, returned, slots, out):
     total, lanes = returned.shape
-    count = slots.shape[1]
     flipped = jnp.concatenate(
-        [returned[pl.ds(start, lanes), :].T[:PAD] for start in range(0, total, lanes)], axis=1
-    )
-    chosen = lax.broadcasted_iota(jnp.int32, (total, count), 0) == slots[...]
-    values = jnp.dot(
-        flipped,
-        jnp.where(chosen, 1.0, 0.0),
-        precision=lax.Precision.HIGHEST,
-        preferred_element_type=jnp.float32,
-    )
+        [returned[pl.ds(start, lanes), :].T for start in range(0, total, lanes)], axis=1
+    )
+    values = jnp.zeros((PAD, slots.shape[1]), jnp.float32)
+    for q in range(lanes // PAD):
+        values += jnp.dot(
+            flipped[PAD * q : PAD * (q + 1)],
+            one_hot_slots(slots[...], q, total),
+            precision=lax.Precision.HIGHEST,
+            preferred_element_type=jnp.float32,
+        )
     out[...] = values[:levels]
 
 
@@ -530,27 +643,20 @@
     levels, rows, lanes = norm_factor.shape
     n_lat = lax.axis_size("lat")
     n_lon = lax.axis_size("lon")
-    devices = n_lat * n_lon
-    both = ("lat", "lon")
-    place = jnp.stack([prof_row, prof_col])
-    packet, slots = route(innovations, interp_weights, place, owners, model_ids, devices)
-    packet = lax.all_to_all(packet.reshape(devices, CAPACITY, LANES), both, 0, 0, tiled=True)
     tiles = lax.all_to_all(model_tiles, "lon", split_axis=1, concat_axis=1, tiled=True)
     tiles = jnp.transpose(tiles, (1, 0, 2, 3))
-    same_lat = lax.dynamic_slice_in_dim(packet[:, 0], lax.axis_index("lat") * n_lon, n_lon, 0)
-    ids = same_lat[:, PAD : PAD + 2].reshape(-1).astype(jnp.int32)
-    packet = packet.reshape(devices * CAPACITY, LANES)
-    corner_weights = packet[:, levels : levels + 4].T.reshape(-1)
-    corner_cells = packet[:, levels + 4 : levels + 6].T.reshape(-1).astype(jnp.int32)
-    observed = spread(corner_weights, corner_cells, packet, levels, rows)
-    field = combine(ids, observed, tiles, norm_factor)
+    place = jnp.stack([prof_row, prof_col])
+    packet, slots = route(innovations, interp_weights, place, owners, model_ids, n_lat * n_lon)
+    packet = post(packet, n_lat, n_lon, 1)
+    observed, corner_weights, corner_cells = spread(packet, levels, rows)
+    field = combine(corner_cells, observed, tiles, norm_factor)
     coef = jnp.stack([face_x, face_y, cross_term, wet_mask.astype(jnp.float32)])
     halos = exchange(field, coef, n_lat, n_lon)
     smoothed, sampled = diffuse(
         field, coef, norm_factor, halos, corner_weights, corner_cells, n_lat
     )
-    returned = lax.all_to_all(sampled.reshape(devices, CAPACITY, LANES), both, 0, 0, tiled=True)
-    profile_values = collect(returned.reshape(devices * CAPACITY, LANES), slots, levels)
+    returned = post(sampled, n_lat, n_lon, 2)
+    profile_values = collect(returned, slots, levels)
     return (smoothed, profile_values)
 
 

time: 207 us -> 204 us (0.986)
  Pallas kernels: 125 us -> 173 us
  blocking collectives: 23.5 us -> 0 us
  waiting for transfers between devices: 17 us -> 0.01 us
  starting transfers between devices: 16.1 us -> 9.59 us
  local copies, waits for them, and re-layouts: 19.7 us -> 16.6 us
    pallas_call x1 -> x3, Pallas kernels: 26.2 us -> 80.3 us  [the longest x2 65.1 us: post(): pl.pallas_call(functools.partial(post_kernel, n_lat, n_lon), out_shape=ja...]
    all_to_all x1 -> x0, blocking collectives: 23.5 us -> none  [on_device(): lax.all_to_all(sampled.reshape(devices, CAPACITY, LANES), both, 0, 0, til...]
    all_to_all x1 -> x0, starting transfers between devices: 11.5 us -> none  [on_device(): lax.all_to_all(packet.reshape(devices, CAPACITY, LANES), both, 0, 0, tile...]
    all_to_all x1 -> x0, waiting for transfers between devices: 9.91 us -> none  [on_device(): lax.all_to_all(packet.reshape(devices, CAPACITY, LANES), both, 0, 0, tile...]
    all_to_all x1, waiting for transfers between devices: 7.05 us -> 0.01 us  [on_device(): lax.all_to_all(model_tiles, 'lon', split_axis=1, concat_axis=1, tiled=True)]
    all_to_all x1, starting transfers between devices: 4.61 us -> 9.59 us  [on_device(): lax.all_to_all(model_tiles, 'lon', split_axis=1, concat_axis=1, tiled=True)]
    pallas_call x1, Pallas kernels: 66.5 us -> 63.4 us  [diffuse(): pl.pallas_call(functools.partial(diffuse_kernel, n_lat), out_shape=(jax.S...]
    convert_element_type x2 -> x0, other arithmetic: 2.29 us -> none  [the longest x1 2.22 us: on_device(): packet[:, levels + 4:levels + 6].T.reshape(-1).astype(jnp.int32)]
  transfers between devices with their start and end apart: 2 -> 1, of which waited for: 2 -> 0; matrix products, arithmetic and copies ran while one was open for 5% -> 2% of each run, Pallas kernels for 13% -> 31%
where the time goes in v3:
time: 204 us
  Pallas kernels  173 us (85%)
  local copies, waits for them, and re-layouts  16.6 us (8%)
  starting transfers between devices  9.59 us (5%)
  other arithmetic  3.51 us (2%)
    pallas_call x2, Pallas kernels, post(): pl.pallas_call(functools.partial(post_kernel, n_lat, n_lon), out_shape=ja...  65.1 us
    pallas_call x1, Pallas kernels, diffuse(): pl.pallas_call(functools.partial(diffuse_kernel, n_lat), out_shape=(jax.S...  63.4 us
    pallas_call x1, Pallas kernels, exchange(): pl.pallas_call(functools.partial(exchange_kernel, n_lat, n_lon), out_shap...  21.3 us
    unnamed x40, local copies, waits for them, and re-layouts  16.6 us
    pallas_call x1, Pallas kernels, spread(): pl.pallas_call(functools.partial(spread_kernel, levels), out_shape=(jax.S...  15.2 us
    all_to_all x1, starting transfers between devices, on_device(): lax.all_to_all(model_tiles, 'lon', split_axis=1, concat_axis=1, tiled=True)  9.59 us
  transfers between devices with their start and end apart: 1, of which 0 were waited for; matrix products, arithmetic and copies ran while one was open for 2% of the time, Pallas kernels for 31%

profile of v3, /device:TPU:1, one launch (start us, length us, event | category | flops | bytes accessed | tf_op | source)
XLA Modules:
  0.0 203.8 jit_solution(11126578454852764661)
XLA Ops:
  0.6 3.8 %copy.15 = f32[25,32,8,128]{3,2,0,1:T(8,128)} copy(f32[25,32,8,128]{3,2,1,0:T(8,128)} %param.17) | data formatting | bytes 6553600 | tf_op args[5]
  4.5 0.0 copy-start.15
  4.5 0.0 copy-start.18
  4.5 0.0 copy-start.16
  4.5 9.6 %all-to-all-start = ((f32[25,32,8,128]{3,2,0,1:T(8,128)}), f32[25,32,8,128]{3,2,0,1:T(8,128)S(1)}, u32[]{:S(2)}, u32[]{:S(2)}) async-start(f32[25,32,8,128]{3,2,0,1:T(8,128)} %copy.15), calls=%async_computation | async-start | bytes 6553600 | tf_op jit(solution)/shard_map/all_to_all | solution.py:646
  14.1 0.0 copy-done.15
  14.1 0.1 copy.14.owner_column
  14.2 0.0 copy-done.18
  14.2 0.7 pad_add_fusion.place
  14.9 0.0 copy-done.16
  14.9 0.0 copy-start.11
  14.9 0.8 copy-done.11
  15.8 0.0 copy-start.17
  15.8 0.7 copy-done.17
  16.4 2.3 %shard_map.131 = (f32[256,128]{1,0:T(8,128)S(1)}, s32[1,512]{1,0:T(1,128)S(1)}) custom-call(f32[25,512]{1,0:T(8,128)S(1)} %copy-done.11, f32[4,512]{1,0:T(4,128)S(1)} %copy-done.16, s32[2,512]{1,0:T(2,128)S(1)} %pad_add_fusion.place, s32[512,1]{1,0:T(8,128)S(1)} %copy.14.owner_column, s32[1,512]{1,0:T(1,128)S(1)} %bitcast.18, s32[1,32]{1,0:T(1,128)S(1)} %copy-done.17), custom_call_target="tpu_custom_call" | custom-call | tf_op jit(solution)/shard_map/pallas_call | solution.py:416
  18.7 45.1 %shard_map.132 = f32[128,2,128]{2,1,0:T(2,128)S(1)} custom-call(f32[128,2,128]{2,1,0:T(2,128)S(1)} %bitcast.17), custom_call_target="tpu_custom_call" | custom-call | tf_op jit(solution)/shard_map/pallas_call | solution.py:476
  63.9 15.2 %shard_map.133 = (f32[8192,128]{1,0:T(8,128)S(1)}, f32[8,8,128]{2,1,0:T(8,128)S(1)}, s32[8,8,128]{2,1,0:T(8,128)S(1)}) custom-call(f32[256,128]{1,0:T(8,128)S(1)} %bitcast.14), custom_call_target="tpu_custom_call" | custom-call | tf_op jit(solution)/shard_map/pallas_call | solution.py:550
  79.0 0.0 copy-start.3
  79.0 1.9 copy-done.3
  81.0 0.0 copy-start.12
  81.0 0.0 copy-start.9
  81.0 0.9 convert_bitcast_fusion
  81.9 0.0 copy-done.12
  81.9 1.9 pad_maximum_fusion.coef
  83.8 0.0 all-to-all-done
  83.8 0.0 copy-start.1
  83.8 1.9 copy-done.1
  85.7 0.0 copy-start.4
  85.7 2.2 %copy-done.4 = f32[8192,128]{1,0:T(8,128)S(1)} copy-done((f32[8192,128]{1,0:T(8,128)S(1)}, f32[8192,128]{1,0:T(8,128)}, u32[]{:S(2)}) %copy-start.4) | copy-done | bytes 4194328
  87.9 0.0 copy-start.2
  87.9 4.0 %shard_map.134.field = f32[25,256,128]{2,1,0:T(8,128)S(1)} custom-call(s32[8,8,128]{2,1,0:T(8,128)S(1)} %get-tuple-element.16.cells.corner_cells, f32[8192,128]{1,0:T(8,128)S(1)} %copy-done.4, f32[32,25,8,128]{3,2,1,0:T(8,128)S(1)} %bitcast.13, f32[25,256,128]{2,1,0:T(8,128)S(1)} %copy-done.1), custom_call_target="tpu_custom_call" | custom-call | tf_op jit(solution)/shard_map/pallas_call | solution.py:593
  91.9 0.0 copy-done.9
  92.0 0.0 copy-done.2
  92.0 0.0 copy-start
  92.0 21.3 %shard_map.135 = (f32[3,288,128]{2,1,0:T(8,128)S(1)}, f32[3,288,128]{2,1,0:T(8,128)S(1)}, f32[25,16,128]{2,1,0:T(8,128)S(1)}, f32[25,16,128]{2,1,0:T(8,128)S(1)}...) custom-call(f32[25,256,128]{2,1,0:T(8,128)S(1)} %shard_map.134.field, f32[4,256,128]{2,1,0:T(8,128)S(1)} %copy-done.2), custom_call_target="tpu_custom_call" | custom-call | tf_op jit(solution)/shard_map/pallas_call | solution.py:132
  113.3 0.0 copy-start.5
  113.3 0.8 copy-done.5
  114.1 0.0 copy-start.6
  114.1 0.8 copy-done.6
  114.9 0.7 copy-done.7
  115.6 0.7 copy-done.8
  116.2 0.6 copy-done.13
  116.9 0.6 copy-done.14
  117.5 0.0 copy-done
  117.5 63.4 %shard_map.136 = (f32[25,256,128]{2,1,0:T(8,128)}, f32[256,128]{1,0:T(8,128)}) custom-call(f32[25,256,128]{2,1,0:T(8,128)} %copy-done, f32[4,256,128]{2,1,0:T(8,128)} %pad_maximum_fusion.coef, f32[25,256,128]{2,1,0:T(8,128)} %norm.3, f32[3,288,128]{2,1,0:T(8,128)} %copy-done.5, f32[3,288,128]{2,1,0:T(8,128)} %copy-done.6, f32[25,16,128]{2,1,0:T(8,128)} %copy-done.7, ...), custom_call_target="tpu_custom_call" | custom-call | tf_op jit(solution)/shard_map/pallas_call | solution.py:334
  180.8 0.9 copy-done.10
  181.7 20.0 %shard_map.137 = f32[128,2,128]{2,1,0:T(2,128)S(1)} custom-call(f32[128,2,128]{2,1,0:T(2,128)S(1)} %bitcast.16), custom_call_target="tpu_custom_call" | custom-call | tf_op jit(solution)/shard_map/pallas_call | solution.py:476
  201.8 2.1 %shard_map.138 = f32[25,512]{1,0:T(8,128)} custom-call(f32[256,128]{1,0:T(8,128)S(1)} %bitcast.15, s32[1,512]{1,0:T(1,128)S(1)} %get-tuple-element.27.slots), custom_call_target="tpu_custom_call" | custom-call | tf_op jit(solution)/shard_map/pallas_call | solution.py:620
  (5 shorter events, 0.0 us)
Async XLA Ops:
  4.5 9.6 %copy-start.15 = (s32[512,1]{0,1:T(1,128)S(1)}, s32[512,1]{0,1:T(1,128)}, u32[]{:S(2)}) copy-start(s32[512,1]{0,1:T(1,128)} %param.13) | copy-start | bytes 6148
  4.5 9.8 %copy-start.18 = (s32[512]{0:T(512)S(1)}, s32[512]{0:T(512)}, u32[]{:S(2)}) copy-start(s32[512]{0:T(512)} %param.15) | copy-start | bytes 6148
  4.5 10.5 %copy-start.16 = (f32[4,512]{1,0:T(4,128)S(1)}, f32[4,512]{1,0:T(4,128)}, u32[]{:S(2)}) copy-start(f32[4,512]{1,0:T(4,128)} %weights.1) | copy-start | bytes 24580
  4.5 79.3 %all-to-all-start = ((f32[25,32,8,128]{3,2,0,1:T(8,128)}), f32[25,32,8,128]{3,2,0,1:T(8,128)S(1)}, u32[]{:S(2)}, u32[]{:S(2)}) async-start(f32[25,32,8,128]{3,2,0,1:T(8,128)} %copy.15), calls=%async_computation | async-start | bytes 6553600 | tf_op jit(solution)/shard_map/all_to_all | solution.py:646
  14.9 0.8 copy-start.11
  15.8 0.7 copy-start.17
  79.0 1.9 copy-start.3
  81.0 0.9 copy-start.12
  81.0 11.0 %copy-start.9 = (s32[8,8,128]{2,1,0:T(8,128)}, s32[8,8,128]{2,1,0:T(8,128)S(1)}, u32[]{:S(2)}) copy-start(s32[8,8,128]{2,1,0:T(8,128)S(1)} %get-tuple-element.16.cells.corner_cells) | copy-start | bytes 98308
  83.8 1.9 copy-start.1
  85.7 2.2 %copy-start.4 = (f32[8192,128]{1,0:T(8,128)S(1)}, f32[8192,128]{1,0:T(8,128)}, u32[]{:S(2)}) copy-start(f32[8192,128]{1,0:T(8,128)} %copy-done.3) | copy-start | bytes 12582916
  87.9 4.0 %copy-start.2 = (f32[4,256,128]{2,1,0:T(8,128)S(1)}, f32[4,256,128]{2,1,0:T(8,128)}, u32[]{:S(2)}) copy-start(f32[4,256,128]{2,1,0:T(8,128)} %pad_maximum_fusion.coef) | copy-start | bytes 1572868
  92.0 25.5 %copy-start = (f32[25,256,128]{2,1,0:T(8,128)}, f32[25,256,128]{2,1,0:T(8,128)S(1)}, u32[]{:S(2)}) copy-start(f32[25,256,128]{2,1,0:T(8,128)S(1)} %shard_map.134.field) | copy-start | bytes 9830404
  113.3 0.8 copy-start.5
  114.1 0.8 copy-start.6
  114.9 0.7 copy-start.7
  115.6 0.7 copy-start.8
  116.2 0.6 copy-start.13
  116.9 0.6 copy-start.14
  180.8 0.9 copy-start.10

commit v4 on v3

--- a/solution.py
+++ b/solution.py
@@ -141,7 +141,7 @@
             pltpu.SemaphoreType.DMA((10,)),
         ],
         compiler_params=pltpu.CompilerParams(
-            collective_id=0, has_side_effects=True, vmem_limit_bytes=40 << 20
+            collective_id=0, has_side_effects=True, vmem_limit_bytes=8 << 20
         ),
     )(field, coef)
 
@@ -157,8 +157,9 @@
     north_field,
     south_coef,
     north_coef,
-    corner_weights,
-    corner_cells,
+    lower,
+    upper,
+    cells,
     out,
     sampled,
     grid,
@@ -296,8 +297,7 @@
     for level in range(levels, PAD):
         turned[pl.ds(level, rows, stride=PAD), :] = jnp.zeros((rows, lanes), jnp.float32)
 
-    lane8 = lane_ids((8, lanes))
-    lane_pad = lane_ids((PAD, lanes))
+    even = lane_ids((PAD, lanes)) % 2 == 0
     per_row = lanes // PAD
 
     def sample_tile(tile, carry):
@@ -305,19 +305,23 @@
             block = tile * per_row + q
 
             def sample_group(group, found):
+                found = list(found)
                 for u in range(UNROLL):
                     spot = group * UNROLL + u
-                    row, lower, upper = corner_masks(corner_weights, corner_cells, block, spot, lane8)
-                    start = pl.multiple_of(row * PAD, PAD)
+                    start = pl.multiple_of(cells[block, 5, spot], PAD)
                     low = turned[pl.ds(start, PAD), :].reshape(PAD // 8, 8, lanes)
                     high = turned[pl.ds(start + PAD, PAD), :].reshape(PAD // 8, 8, lanes)
-                    mixed = (low * lower + high * upper).reshape(PAD, lanes)
-                    total = jnp.sum(mixed, axis=1, keepdims=True)
-                    found = jnp.where(lane_pad == spot, total, found)
-                return found
-
-            gathered[pl.ds(PAD * q, PAD), :] = lax.fori_loop(
-                0, lanes // UNROLL, sample_group, jnp.zeros((PAD, lanes), jnp.float32)
+                    mixed = low * row_of(lower, block * lanes + spot) + high * row_of(
+                        upper, block * lanes + spot
+                    )
+                    move = (cells[block, 6, spot] + spot) & (lanes - 1)
+                    found[u % 2] = found[u % 2] + pltpu.roll(mixed.reshape(PAD, lanes), move, 1)
+                return tuple(found)
+
+            zeros = jnp.zeros((PAD, lanes), jnp.float32)
+            on_even, on_odd = lax.fori_loop(0, lanes // UNROLL, sample_group, (zeros, zeros))
+            gathered[pl.ds(PAD * q, PAD), :] = jnp.where(
+                even, on_even + turn(on_even, -1), on_odd + turn(on_odd, -1)
             )
         sampled[pl.ds(pl.multiple_of(tile * lanes, lanes), lanes), :] = gathered[...].T
         return carry
@@ -325,7 +329,11 @@
     lax.fori_loop(0, sampled.shape[0] // lanes, sample_tile, 0)
 
 
-def diffuse(field, coef, norm, halos, corner_weights, corner_cells, n_lat):
+def row_of(table, number):
+    return table[pl.ds(number, 8, stride=0), :]
+
+
+def diffuse(field, coef, norm, halos, lower, upper, cells, n_lat):
     levels, rows, lanes = field.shape
     tall = rows + 2 * HALO
     whole = pl.BlockSpec(memory_space=pltpu.VMEM)
@@ -335,9 +343,9 @@
         functools.partial(diffuse_kernel, n_lat),
         out_shape=(
             jax.ShapeDtypeStruct(field.shape, jnp.float32),
-            jax.ShapeDtypeStruct((corner_cells.shape[0] * PAD, lanes), jnp.float32),
+            jax.ShapeDtypeStruct((cells.shape[0] * PAD, lanes), jnp.float32),
         ),
-        in_specs=[whole] * (3 + len(halos)) + [scalars] * 2,
+        in_specs=[whole] * (5 + len(halos)) + [scalars],
         out_specs=(whole, whole),
         scratch_shapes=[
             pltpu.VMEM((planes, tall, lanes), jnp.float32),
@@ -347,18 +355,8 @@
             pltpu.VMEM((rows * PAD, lanes), jnp.float32),
             pltpu.VMEM((lanes, lanes), jnp.float32),
         ],
-        compiler_params=pltpu.CompilerParams(vmem_limit_bytes=56 << 20),
-    )(field, coef, norm, *halos, corner_weights, corner_cells)
-
-
-def corner_masks(corner_weights, corner_cells, block, spot, lane):
-    column = corner_cells[block, 6, spot]
-    here = lane == column
-    beside = lane == column + 1
-    first, second, third, fourth = (corner_weights[block, 1 + c, spot] for c in range(4))
-    lower = jnp.where(here, first, jnp.where(beside, second, 0.0))
-    upper = jnp.where(here, third, jnp.where(beside, fourth, 0.0))
-    return corner_cells[block, 5, spot], lower, upper
+        compiler_params=pltpu.CompilerParams(vmem_limit_bytes=30 << 20),
+    )(field, coef, norm, *halos, lower, upper, cells)
 
 
 def one_hot_slots(slots, q, rows):
@@ -422,100 +420,114 @@
         in_specs=[whole] * 6,
         out_specs=(whole, whole),
         scratch_shapes=[pltpu.VMEM((LANES, count), jnp.float32)],
-        compiler_params=pltpu.CompilerParams(vmem_limit_bytes=32 << 20),
+        compiler_params=pltpu.CompilerParams(vmem_limit_bytes=16 << 20),
     )(innovations, weights, place, owners, owners.reshape(1, count), ids)
 
 
-def post_kernel(n_lat, n_lon, source, target, send_sem, recv_sem, local_sem):
+def post_kernel(source, target, held, send_sem, recv_sem, local_sem):
+    n_lat, n_lon = source.shape[:2]
     lat = lax.axis_index("lat")
     lon = lax.axis_index("lon")
-    me = lat * n_lon + lon
-    devices = n_lat * n_lon
+    across = [lax.rem(lon + step, n_lon) for step in range(1, n_lon)]
+    along = [lax.rem(lat + step, n_lat) for step in range(1, n_lat)]
+
     barrier = pltpu.get_barrier_semaphore()
-
-    def there(step):
-        other = lax.rem(me + step, devices)
-        return other, (other // n_lon, lax.rem(other, n_lon))
-
-    def greet(step, carry):
-        pl.semaphore_signal(barrier, inc=1, device_id=there(step)[1], device_id_type=MESH)
-        return carry
-
-    def transfer(step):
-        other, device = there(step)
-        return pltpu.make_async_remote_copy(
-            src_ref=source.at[other],
-            dst_ref=target.at[me],
-            send_sem=send_sem.at[step],
-            recv_sem=recv_sem.at[step],
+    for other in across:
+        pl.semaphore_signal(barrier, inc=1, device_id=(lat, other), device_id_type=MESH)
+    for other in along:
+        pl.semaphore_signal(barrier, inc=1, device_id=(other, lon), device_id_type=MESH)
+    own = pltpu.make_async_copy(source.at[:, lon], held.at[:, lon], local_sem)
+    own.start()
+    pl.semaphore_wait(barrier, n_lon + n_lat - 2)
+
+    def push(here, there, number, device):
+        copy = pltpu.make_async_remote_copy(
+            src_ref=here,
+            dst_ref=there,
+            send_sem=send_sem.at[number],
+            recv_sem=recv_sem.at[number],
             device_id=device,
             device_id_type=MESH,
         )
-
-    def send(step, carry):
-        transfer(step).start()
-        return carry
-
-    def arrive(step, carry):
-        transfer(step).wait()
-        return carry
-
-    own = pltpu.make_async_copy(source.at[me], target.at[me], local_sem)
+        copy.start()
+        return copy
+
+    copies = [
+        push(source.at[:, other], held.at[:, lon], number, (lat, other))
+        for number, other in enumerate(across)
+    ]
+    own.wait()
+    for copy in copies:
+        copy.wait()
+    copies = [
+        push(held.at[other], target.at[lat], n_lon + number, (other, lon))
+        for number, other in enumerate(along)
+    ]
+    own = pltpu.make_async_copy(held.at[lat], target.at[lat], local_sem)
     own.start()
-    lax.fori_loop(1, devices, greet, 0)
-    pl.semaphore_wait(barrier, devices - 1)
-    lax.fori_loop(1, devices, send, 0)
-    lax.fori_loop(1, devices, arrive, 0)
     own.wait()
+    for copy in copies:
+        copy.wait()
 
 
 def post(packet, n_lat, n_lon, collective_id):
-    devices = n_lat * n_lon
     whole = pl.BlockSpec(memory_space=pltpu.VMEM)
-    blocks = packet.reshape(devices, -1, LANES)
+    blocks = packet.reshape(n_lat, n_lon, -1, LANES)
     received = pl.pallas_call(
-        functools.partial(post_kernel, n_lat, n_lon),
+        post_kernel,
         out_shape=jax.ShapeDtypeStruct(blocks.shape, jnp.float32),
         in_specs=[whole],
         out_specs=whole,
         scratch_shapes=[
-            pltpu.SemaphoreType.DMA((devices,)),
-            pltpu.SemaphoreType.DMA((devices,)),
+            pltpu.VMEM(blocks.shape, jnp.float32),
+            pltpu.SemaphoreType.DMA((n_lon + n_lat,)),
+            pltpu.SemaphoreType.DMA((n_lon + n_lat,)),
             pltpu.SemaphoreType.DMA,
         ],
         compiler_params=pltpu.CompilerParams(
-            collective_id=collective_id, has_side_effects=True, vmem_limit_bytes=16 << 20
+            collective_id=collective_id, has_side_effects=True, vmem_limit_bytes=4 << 20
         ),
     )(blocks)
     return received.reshape(packet.shape)
 
 
 def spread_kernel(
-    levels, packet, observed, weights_out, cells_out, turned, other, weights, cells, sems
+    levels, packet, observed, lower, upper, cells_out, turned, other, cells, sem
 ):
     total, lanes = packet.shape
     per_row = lanes // PAD
     tiles = total // lanes
-    lane8 = lane_ids((8, lanes))
+    level_lane = PAD - 8
+    sublane = lax.broadcasted_iota(jnp.int32, (8, lanes), 0)
     for tile in range(tiles):
         flipped = packet[pl.ds(tile * lanes, lanes), :].T
         turned[pl.ds(tile * lanes, lanes), :] = flipped
         for q in range(per_row):
-            last = flipped[PAD * (q + 1) - 8 : PAD * (q + 1)]
-            weights_out[tile * per_row + q] = last
-            cells_out[tile * per_row + q] = last.astype(jnp.int32)
-    copies = (
-        pltpu.make_async_copy(weights_out, weights, sems.at[0]),
-        pltpu.make_async_copy(cells_out, cells, sems.at[1]),
-    )
-    for copy in copies:
-        copy.start()
+            last = flipped[PAD * q + level_lane : PAD * (q + 1)].astype(jnp.int32)
+            last = jnp.where(sublane == 5, last * PAD, jnp.where(sublane == 6, lanes - last, last))
+            cells_out[tile * per_row + q] = last
+    copy = pltpu.make_async_copy(cells_out, cells, sem)
+    copy.start()
+
+    lane = lane_ids((lanes, lanes)).astype(jnp.float32)
+    for tile in range(tiles):
+        rows = packet[pl.ds(tile * lanes, lanes), :]
+        for q in range(per_row):
+            first, second, third, fourth, row, column = (
+                jnp.broadcast_to(rows[:, n : n + 1], (lanes, lanes))
+                for n in range(PAD * q + level_lane + 1, PAD * q + level_lane + 7)
+            )
+            here = lane == column
+            beside = lane == column + 1.0
+            block = pl.ds((tile * per_row + q) * lanes, lanes)
+            lower[block, :] = jnp.where(here, first, jnp.where(beside, second, 0.0))
+            upper[block, :] = jnp.where(here, third, jnp.where(beside, fourth, 0.0))
+
     is_level = lax.broadcasted_iota(jnp.int32, (PAD, lanes), 0) < levels
     parts = (observed, other)
     for part in parts:
         part[...] = jnp.zeros_like(part)
-    for copy in copies:
-        copy.wait()
+    copy.wait()
 
     def spread_block(block, carry):
         values = jnp.where(is_level, turned[pl.ds(pl.multiple_of(block * PAD, PAD), PAD), :], 0.0)
@@ -524,14 +536,17 @@
             moved = pltpu.roll(values, lax.rem(lanes - group * UNROLL, lanes), 1)
             for u in range(UNROLL):
                 spot = group * UNROLL + u
-                row, lower, upper = corner_masks(weights, cells, block, spot, lane8)
                 value = jnp.broadcast_to(moved[:, u : u + 1], (PAD, lanes)).reshape(
                     PAD // 8, 8, lanes
                 )
                 added = jnp.concatenate(
-                    [(value * lower).reshape(PAD, lanes), (value * upper).reshape(PAD, lanes)], axis=0
+                    [
+                        (value * row_of(table, block * lanes + spot)).reshape(PAD, lanes)
+                        for table in (lower, upper)
+                    ],
+                    axis=0,
                 )
-                where = pl.ds(pl.multiple_of(row * PAD, PAD), 2 * PAD)
+                where = pl.ds(pl.multiple_of(cells[block, 5, spot], PAD), 2 * PAD)
                 part = parts[u % len(parts)]
                 part[where, :] = part[where, :] + added
             return carry
@@ -547,23 +562,24 @@
     total, lanes = packet.shape
     whole = pl.BlockSpec(memory_space=pltpu.VMEM)
     blocks = total // PAD
+    masks = jax.ShapeDtypeStruct((blocks * lanes, lanes), jnp.float32)
     return pl.pallas_call(
         functools.partial(spread_kernel, levels),
         out_shape=(
             jax.ShapeDtypeStruct((rows * PAD, lanes), jnp.float32),
-            jax.ShapeDtypeStruct((blocks, 8, lanes), jnp.float32),
+            masks,
+            masks,
             jax.ShapeDtypeStruct((blocks, 8, lanes), jnp.int32),
         ),
         in_specs=[whole],
-        out_specs=(whole, whole, whole),
+        out_specs=(whole,) * 4,
         scratch_shapes=[
             pltpu.VMEM(packet.shape, jnp.float32),
             pltpu.VMEM((rows * PAD, lanes), jnp.float32),
-            pltpu.SMEM((blocks, 8, lanes), jnp.float32),
             pltpu.SMEM((blocks, 8, lanes), jnp.int32),
-            pltpu.SemaphoreType.DMA((2,)),
+            pltpu.SemaphoreType.DMA,
         ],
-        compiler_params=pltpu.CompilerParams(vmem_limit_bytes=40 << 20),
+        compiler_params=pltpu.CompilerParams(vmem_limit_bytes=12 << 20),
     )(packet)
 
 
@@ -595,7 +611,7 @@
         out_shape=jax.ShapeDtypeStruct(norm.shape, jnp.float32),
         in_specs=[pl.BlockSpec(memory_space=pltpu.SMEM)] + [whole] * 3,
         out_specs=whole,
-        compiler_params=pltpu.CompilerParams(vmem_limit_bytes=40 << 20),
+        compiler_params=pltpu.CompilerParams(vmem_limit_bytes=8 << 20),
     )(cells, observed, tiles, norm)
 
 
@@ -622,7 +638,7 @@
         out_shape=jax.ShapeDtypeStruct((levels, slots.shape[1]), jnp.float32),
         in_specs=[whole] * 2,
         out_specs=whole,
-        compiler_params=pltpu.CompilerParams(vmem_limit_bytes=32 << 20),
+        compiler_params=pltpu.CompilerParams(vmem_limit_bytes=16 << 20),
     )(returned, slots)
 
 
@@ -643,17 +659,17 @@
     levels, rows, lanes = norm_factor.shape
     n_lat = lax.axis_size("lat")
     n_lon = lax.axis_size("lon")
-    tiles = lax.all_to_all(model_tiles, "lon", split_axis=1, concat_axis=1, tiled=True)
-    tiles = jnp.transpose(tiles, (1, 0, 2, 3))
     place = jnp.stack([prof_row, prof_col])
     packet, slots = route(innovations, interp_weights, place, owners, model_ids, n_lat * n_lon)
     packet = post(packet, n_lat, n_lon, 1)
-    observed, corner_weights, corner_cells = spread(packet, levels, rows)
-    field = combine(corner_cells, observed, tiles, norm_factor)
+    tiles, packet = lax.optimization_barrier((jnp.transpose(model_tiles, (1, 0, 2, 3)), packet))
+    tiles = lax.all_to_all(tiles, "lon", split_axis=0, concat_axis=0, tiled=True)
+    observed, lower, upper, cells = spread(packet, levels, rows)
+    field = combine(cells, observed, tiles, norm_factor)
     coef = jnp.stack([face_x, face_y, cross_term, wet_mask.astype(jnp.float32)])
     halos = exchange(field, coef, n_lat, n_lon)
     smoothed, sampled = diffuse(
-        field, coef, norm_factor, halos, corner_weights, corner_cells, n_lat
+        field, coef, norm_factor, halos, lower, upper, cells, n_lat
     )
     returned = post(sampled, n_lat, n_lon, 2)
     profile_values = collect(returned, slots, levels)

time: 204 us -> 182 us (0.89)
  Pallas kernels: 173 us -> 133 us
  waiting for transfers between devices: 0.01 us -> 23.5 us
  local copies, waits for them, and re-layouts: 16.6 us -> 13.3 us
    pallas_call x2, Pallas kernels: 65.1 us -> 31.9 us  [post(): pl.pallas_call(post_kernel, out_shape=jax.ShapeDtypeStruct(blocks.shape,...]
    all_to_all x1, waiting for transfers between devices: 0.01 us -> 23.5 us  [on_device(): lax.all_to_all(tiles, 'lon', split_axis=0, concat_axis=0, tiled=True)]
    pallas_call x1, Pallas kernels: 63.4 us -> 56.2 us  [diffuse(): pl.pallas_call(functools.partial(diffuse_kernel, n_lat), out_shape=(jax.S...]
    unnamed x40 -> x26, local copies, waits for them, and re-layouts: 16.6 us -> 13.3 us
    pallas_call x1, Pallas kernels: 15.2 us -> 12.4 us  [spread(): pl.pallas_call(functools.partial(spread_kernel, levels), out_shape=(jax.S...]
  transfers between devices with their start and end apart: 1 -> 1, of which waited for: 0 -> 1; matrix products, arithmetic and copies ran while one was open for 2% -> 2% of each run, Pallas kernels for 31% -> 7%
where the time goes in v4:
time: 182 us
  Pallas kernels  133 us (73%)
  waiting for transfers between devices  23.5 us (13%)
  local copies, waits for them, and re-layouts  13.3 us (7%)
  starting transfers between devices  7.88 us (4%)
  other arithmetic  3.55 us (2%)
    pallas_call x1, Pallas kernels, diffuse(): pl.pallas_call(functools.partial(diffuse_kernel, n_lat), out_shape=(jax.S...  56.2 us
    pallas_call x2, Pallas kernels, post(): pl.pallas_call(post_kernel, out_shape=jax.ShapeDtypeStruct(blocks.shape,...  31.9 us
    all_to_all x1, waiting for transfers between devices, on_device(): lax.all_to_all(tiles, 'lon', split_axis=0, concat_axis=0, tiled=True)  23.5 us
    pallas_call x1, Pallas kernels, exchange(): pl.pallas_call(functools.partial(exchange_kernel, n_lat, n_lon), out_shap...  23.3 us
    unnamed x26, local copies, waits for them, and re-layouts  13.3 us
    pallas_call x1, Pallas kernels, spread(): pl.pallas_call(functools.partial(spread_kernel, levels), out_shape=(jax.S...  12.4 us
    all_to_all x1, starting transfers between devices, on_device(): lax.all_to_all(tiles, 'lon', split_axis=0, concat_axis=0, tiled=True)  7.88 us
    pallas_call x1, Pallas kernels, combine(): pl.pallas_call(combine_kernel, out_shape=jax.ShapeDtypeStruct(norm.shape,...  4.94 us
  transfers between devices with their start and end apart: 1, of which 1 were waited for; matrix products, arithmetic and copies ran while one was open for 2% of the time, Pallas kernels for 7%

profile of v4, /device:TPU:1, one launch (start us, length us, event | category | flops | bytes accessed | tf_op | source)
XLA Modules:
  0.0 182.0 jit_solution(7773956340696758805)
XLA Ops:
  0.6 0.8 copy.15.owner_column
  1.5 0.7 pad_add_fusion.place
  2.2 0.0 copy-start.8
  2.2 0.8 copy-done.8
  3.0 0.0 copy-start.9
  3.0 0.7 copy-done.9
  3.7 0.0 copy-start.10
  3.7 0.7 copy-done.10
  4.4 0.0 copy-start.11
  4.4 0.7 copy-done.11
  5.0 2.3 %shard_map.131 = (f32[256,128]{1,0:T(8,128)S(1)}, s32[1,512]{1,0:T(1,128)S(1)}) custom-call(f32[25,512]{1,0:T(8,128)S(1)} %copy-done.8, f32[4,512]{1,0:T(4,128)S(1)} %copy-done.10, s32[2,512]{1,0:T(2,128)S(1)} %pad_add_fusion.place, s32[512,1]{1,0:T(8,128)S(1)} %copy.15.owner_column, s32[1,512]{1,0:T(1,128)S(1)} %bitcast.19, s32[1,32]{1,0:T(1,128)S(1)} %copy-done.11), custom_call_target="tpu_custom_call" | custom-call | tf_op jit(solution)/shard_map/pallas_call | solution.py:414
  7.3 16.6 %shard_map.132 = f32[8,16,2,128]{3,2,1,0:T(2,128)S(1)} custom-call(f32[8,16,2,128]{3,2,1,0:T(2,128)S(1)} %bitcast.18), custom_call_target="tpu_custom_call" | custom-call | tf_op jit(solution)/shard_map/pallas_call | solution.py:476
  24.0 3.8 %copy.17 = f32[25,32,8,128]{3,2,0,1:T(8,128)} copy(f32[25,32,8,128]{3,2,1,0:T(8,128)} %param.17) | data formatting | bytes 6553600 | tf_op args[5]
  27.8 0.0 copy-start
  27.8 7.9 %all-to-all-start = ((f32[32,25,8,128]{3,2,1,0:T(8,128)}), f32[32,25,8,128]{3,2,1,0:T(8,128)}, u32[]{:S(2)}, u32[]{:S(2)}) async-start(f32[32,25,8,128]{3,2,1,0:T(8,128)} %bitcast.20), calls=%async_computation | async-start | bytes 6553600 | tf_op jit(solution)/shard_map/all_to_all | solution.py:666
  35.7 12.4 %shard_map.133 = (f32[8192,128]{1,0:T(8,128)S(1)}, f32[1024,128]{1,0:T(8,128)S(1)}, f32[1024,128]{1,0:T(8,128)S(1)}, s32[8,8,128]{2,1,0:T(8,128)S(1)}) custom-call(f32[256,128]{1,0:T(8,128)S(1)} %bitcast.15), custom_call_target="tpu_custom_call" | custom-call | tf_op jit(solution)/shard_map/pallas_call | solution.py:566
  48.1 0.0 copy-start.2
  48.1 2.0 %copy-done.2 = f32[8192,128]{1,0:T(8,128)} copy-done((f32[8192,128]{1,0:T(8,128)}, f32[8192,128]{1,0:T(8,128)S(1)}, u32[]{:S(2)}) %copy-start.2) | copy-done | bytes 4194328
  50.1 0.0 copy-start.4
  50.1 0.8 copy-done.4
  50.9 0.0 copy-start.6
  50.9 0.8 copy-done.6
  51.7 0.9 convert_bitcast_fusion
  52.6 1.9 %pad_maximum_fusion.coef = f32[4,256,128]{2,1,0:T(8,128)} fusion(f32[1,256,128]{2,1,0:T(8,128)S(1)} %convert_bitcast_fusion, f32[1,256,128]{2,1,0:T(8,128)} %bitcast.21, f32[1,256,128]{2,1,0:T(8,128)} %bitcast.22, f32[1,256,128]{2,1,0:T(8,128)} %bitcast.23), kind=kLoop, calls=%fused_computation.1 | loop fusion | flops 393216 | bytes 1048576 | tf_op jit(solution)/shard_map/stack | solution.py:669
  54.5 23.5 %all-to-all-done.tiles = f32[32,25,8,128]{3,2,1,0:T(8,128)} async-done(((f32[32,25,8,128]{3,2,1,0:T(8,128)}), f32[32,25,8,128]{3,2,1,0:T(8,128)}, u32[]{:S(2)}, u32[]{:S(2)}) %all-to-all-start) | async-done | bytes 3276832 | tf_op jit(solution)/shard_map/all_to_all | solution.py:666
  78.0 0.0 copy-done
  78.0 0.0 copy-start.3
  78.0 2.2 %copy-done.3 = f32[8192,128]{1,0:T(8,128)S(1)} copy-done((f32[8192,128]{1,0:T(8,128)S(1)}, f32[8192,128]{1,0:T(8,128)}, u32[]{:S(2)}) %copy-start.3) | copy-done | bytes 4194328
  80.2 0.0 copy-start.1
  80.2 4.9 %shard_map.134.field = f32[25,256,128]{2,1,0:T(8,128)S(1)} custom-call(s32[8,8,128]{2,1,0:T(8,128)S(1)} %get-tuple-element.20.cells, f32[8192,128]{1,0:T(8,128)S(1)} %copy-done.3, f32[32,25,8,128]{3,2,1,0:T(8,128)} %all-to-all-done.tiles, f32[25,256,128]{2,1,0:T(8,128)S(1)} %copy-done), custom_call_target="tpu_custom_call" | custom-call | tf_op jit(solution)/shard_map/pallas_call | solution.py:609
  85.1 0.0 copy-done.1
  85.1 0.0 copy-start.5
  85.2 0.0 copy-start.7
  85.2 23.3 %shard_map.135 = (f32[3,288,128]{2,1,0:T(8,128)S(1)}, f32[3,288,128]{2,1,0:T(8,128)S(1)}, f32[25,16,128]{2,1,0:T(8,128)S(1)}, f32[25,16,128]{2,1,0:T(8,128)S(1)}...) custom-call(f32[25,256,128]{2,1,0:T(8,128)S(1)} %shard_map.134.field, f32[4,256,128]{2,1,0:T(8,128)S(1)} %copy-done.1), custom_call_target="tpu_custom_call" | custom-call | tf_op jit(solution)/shard_map/pallas_call | solution.py:132
  108.5 0.0 copy-done.5
  108.5 0.0 copy-done.7
  108.5 56.2 %shard_map.136 = (f32[25,256,128]{2,1,0:T(8,128)}, f32[256,128]{1,0:T(8,128)S(1)}) custom-call(f32[25,256,128]{2,1,0:T(8,128)S(1)} %shard_map.134.field, f32[4,256,128]{2,1,0:T(8,128)S(1)} %copy-done.1, f32[25,256,128]{2,1,0:T(8,128)S(1)} %copy-done, f32[3,288,128]{2,1,0:T(8,128)S(1)} %get-tuple-element.23.west_cols, ...), custom_call_target="tpu_custom_call" | custom-call | tf_op jit(solution)/shard_map/pallas_call | solution.py:342
  164.7 15.2 %shard_map.137 = f32[8,16,2,128]{3,2,1,0:T(2,128)S(1)} custom-call(f32[8,16,2,128]{3,2,1,0:T(2,128)S(1)} %bitcast.17), custom_call_target="tpu_custom_call" | custom-call | tf_op jit(solution)/shard_map/pallas_call | solution.py:476
  179.9 2.1 %shard_map.138 = f32[25,512]{1,0:T(8,128)} custom-call(f32[256,128]{1,0:T(8,128)S(1)} %bitcast.16, s32[1,512]{1,0:T(1,128)S(1)} %get-tuple-element.33.slots), custom_call_target="tpu_custom_call" | custom-call | tf_op jit(solution)/shard_map/pallas_call | solution.py:636
Async XLA Ops:
  2.2 0.8 copy-start.8
  3.0 0.7 copy-start.9
  3.7 0.7 copy-start.10
  4.4 0.7 copy-start.11
  27.8 50.2 %copy-start = (f32[25,256,128]{2,1,0:T(8,128)S(1)}, f32[25,256,128]{2,1,0:T(8,128)}, u32[]{:S(2)}) copy-start(f32[25,256,128]{2,1,0:T(8,128)} %norm.3) | copy-start | bytes 9830404
  27.8 50.2 %all-to-all-start = ((f32[32,25,8,128]{3,2,1,0:T(8,128)}), f32[32,25,8,128]{3,2,1,0:T(8,128)}, u32[]{:S(2)}, u32[]{:S(2)}) async-start(f32[32,25,8,128]{3,2,1,0:T(8,128)} %bitcast.20), calls=%async_computation | async-start | bytes 6553600 | tf_op jit(solution)/shard_map/all_to_all | solution.py:666
  48.1 2.0 %copy-start.2 = (f32[8192,128]{1,0:T(8,128)}, f32[8192,128]{1,0:T(8,128)S(1)}, u32[]{:S(2)}) copy-start(f32[8192,128]{1,0:T(8,128)S(1)} %get-tuple-element.21.observed) | copy-start | bytes 12582916
  50.1 0.8 copy-start.4
  50.9 0.9 copy-start.6
  78.0 2.2 %copy-start.3 = (f32[8192,128]{1,0:T(8,128)S(1)}, f32[8192,128]{1,0:T(8,128)}, u32[]{:S(2)}) copy-start(f32[8192,128]{1,0:T(8,128)} %copy-done.2) | copy-start | bytes 12582916
  80.2 4.9 %copy-start.1 = (f32[4,256,128]{2,1,0:T(8,128)S(1)}, f32[4,256,128]{2,1,0:T(8,128)}, u32[]{:S(2)}) copy-start(f32[4,256,128]{2,1,0:T(8,128)} %pad_maximum_fusion.coef) | copy-start | bytes 1572868
  85.1 23.3 %copy-start.5 = (f32[1024,128]{1,0:T(8,128)S(1)}, f32[1024,128]{1,0:T(8,128)}, u32[]{:S(2)}) copy-start(f32[1024,128]{1,0:T(8,128)} %copy-done.4) | copy-start | bytes 1572868
  85.2 23.3 %copy-start.7 = (f32[1024,128]{1,0:T(8,128)S(1)}, f32[1024,128]{1,0:T(8,128)}, u32[]{:S(2)}) copy-start(f32[1024,128]{1,0:T(8,128)} %copy-done.6) | copy-start | bytes 1572868

commit v5 on v4

--- a/solution.py
+++ b/solution.py
@@ -14,7 +14,9 @@
 HALO = 16
 LANES = 128
 COLS = 12
-PAIRS = 5
+PAIRS = 6
+COEF_PAIRS = 5
+EARLY = 10
 CHUNK = 40
 EDGE = 4
 MESH = pl.DeviceIdType.MESH
@@ -24,29 +26,86 @@
     return lax.broadcasted_iota(jnp.int32, shape, len(shape) - 1)
 
 
-def exchange_kernel(
-    n_lat,
-    n_lon,
-    field,
-    coef,
-    west_cols,
-    east_cols,
-    south_field,
-    north_field,
-    south_coef,
-    north_coef,
-    pack_first,
-    pack_last,
-    send_sem,
-    recv_sem,
-):
+def within(lane, start, width):
+    start = start % LANES
+    return jnp.logical_and(lane >= start, lane < start + width)
+
+
+def turn(values, shift):
+    shift = shift % LANES
+    return pltpu.roll(values, shift, 1) if shift else values
+
+
+def packed_columns(plane_of, planes, rows, cols, first_pair, pairs):
+    lane = lane_ids((rows, LANES))
+    low = jnp.zeros((rows, LANES), jnp.float32)
+    high = jnp.zeros((rows, LANES), jnp.float32)
+    for k in range(pairs):
+        for half in range(2):
+            plane = 2 * (first_pair + k) + half
+            if plane >= planes:
+                continue
+            shift = cols * k + (LANES // 2) * half
+            values = turn(plane_of(plane), shift)
+            low = jnp.where(within(lane, shift, cols), values, low)
+            high = jnp.where(within(lane, LANES - cols + shift, cols), values, high)
+    return low, high
+
+
+def strip_plane(first, second, east, west, k, cols, inside):
+    half = LANES // 2
+    lane = lane_ids(first.shape)
+    upper_half = lane >= half
+    lane = lane % half
+    west_side = lane < half // 2
+    low = jnp.where(west_side, turn(first, COLS), turn(first, half - COLS))
+    high = jnp.where(west_side, turn(second, COLS + half), turn(second, -COLS))
+    own = jnp.where(upper_half, high, low)
+    east = jnp.where(
+        jnp.logical_and(inside, within(lane, half - COLS, cols)),
+        turn(east, half - COLS - cols * k),
+        0.0,
+    )
+    west = jnp.where(
+        jnp.logical_and(inside, within(lane, COLS - cols, cols)), turn(west, COLS - cols * k), east
+    )
+    return jnp.where(jnp.logical_and(lane >= COLS, lane < half - COLS), own, west)
+
+
+def inside_domain(shape, rows, has_south, has_north):
+    row = lax.broadcasted_iota(jnp.int32, shape, 0)
+    return jnp.logical_and(
+        jnp.logical_or(row >= HALO, has_south), jnp.logical_or(row < HALO + rows, has_north)
+    )
+
+
+def neighbours(n_lat, n_lon):
     lat = lax.axis_index("lat")
     lon = lax.axis_index("lon")
     up = lax.rem(lat + 1, n_lat)
     down = lax.rem(lat + n_lat - 1, n_lat)
     right = lax.rem(lon + 1, n_lon)
     left = lax.rem(lon + n_lon - 1, n_lon)
-    rows = field.shape[1]
+    return lat, lon, up, down, right, left
+
+
+def exchange_kernel(
+    n_lat,
+    n_lon,
+    field,
+    west_cols,
+    east_cols,
+    south_rows,
+    north_rows,
+    pack_first,
+    pack_last,
+    pack_low,
+    pack_high,
+    send_sem,
+    recv_sem,
+):
+    lat, lon, up, down, right, left = neighbours(n_lat, n_lon)
+    levels, rows = field.shape[:2]
 
     barrier = pltpu.get_barrier_semaphore()
     for there in (
@@ -60,7 +119,6 @@
         (down, left),
     ):
         pl.semaphore_signal(barrier, inc=1, device_id=there, device_id_type=MESH)
-    pl.semaphore_wait(barrier, 8)
 
     copies = []
 
@@ -77,38 +135,22 @@
         copy.start()
         copies.append(copy)
 
+    for level in range(levels):
+        at = pl.ds(STEPS * level, STEPS)
+        pack_high[at, :] = field[level, pl.ds(rows - STEPS, STEPS), :]
+        pack_low[at, :] = field[level, pl.ds(0, STEPS), :]
+    pl.semaphore_wait(barrier, 8)
+    send(pack_high, south_rows, (up, lon))
+    send(pack_low, north_rows, (down, lon))
+    for tile in range(pack_first.shape[0]):
+        low, high = packed_columns(
+            lambda plane: field[plane], levels, rows, STEPS, tile * PAIRS, PAIRS
+        )
+        pack_first[tile] = low
+        pack_last[tile] = high
+
     first = pl.ds(0, HALO)
     last = pl.ds(rows - HALO, HALO)
-    send(field.at[:, last, :], south_field, (up, lon))
-    send(field.at[:, first, :], north_field, (down, lon))
-    send(coef.at[:, last, :], south_coef, (up, lon))
-    send(coef.at[:, first, :], north_coef, (down, lon))
-
-    levels = field.shape[0]
-    planes = levels + (levels % 2) + coef.shape[0]
-    lane = lane_ids((rows, LANES))
-
-    def within(start):
-        start = start % LANES
-        return jnp.logical_and(lane >= start, lane < start + COLS)
-
-    for tile in range(pack_first.shape[0]):
-        low = jnp.zeros((rows, LANES), jnp.float32)
-        high = jnp.zeros((rows, LANES), jnp.float32)
-        for k in range(PAIRS):
-            for half in range(2):
-                plane = 2 * (tile * PAIRS + k) + half
-                if plane >= planes or levels <= plane < levels + (levels % 2):
-                    continue
-                values = field[plane] if plane < levels else coef[plane - planes + coef.shape[0]]
-                shift = COLS * k + (LANES // 2) * half
-                if shift:
-                    values = pltpu.roll(values, shift, 1)
-                low = jnp.where(within(shift), values, low)
-                high = jnp.where(within(LANES - COLS + shift), values, high)
-        pack_first[tile] = low
-        pack_last[tile] = high
-
     own = pl.ds(HALO, rows)
     above = pl.ds(HALO + rows, HALO)
     send(pack_last, west_cols.at[:, own, :], (lat, right))
@@ -121,111 +163,55 @@
         copy.wait()
 
 
-def exchange(field, coef, n_lat, n_lon):
+def exchange(field, n_lat, n_lon):
     levels, rows, lanes = field.shape
-    pairs = (levels + 1) // 2 + coef.shape[0] // 2
-    tiles = -(-pairs // PAIRS)
+    tiles = -(-((levels + 1) // 2) // PAIRS)
+    edge = -(-levels * STEPS // 8) * 8
     whole = pl.BlockSpec(memory_space=pltpu.VMEM)
     packed = jax.ShapeDtypeStruct((tiles, rows + 2 * HALO, lanes), jnp.float32)
-    edge_field = jax.ShapeDtypeStruct((levels, HALO, lanes), jnp.float32)
-    edge_coef = jax.ShapeDtypeStruct((coef.shape[0], HALO, lanes), jnp.float32)
+    edges = jax.ShapeDtypeStruct((edge, lanes), jnp.float32)
     return pl.pallas_call(
         functools.partial(exchange_kernel, n_lat, n_lon),
-        out_shape=(packed, packed, edge_field, edge_field, edge_coef, edge_coef),
-        in_specs=[whole] * 2,
-        out_specs=[whole] * 6,
+        out_shape=(packed, packed, edges, edges),
+        in_specs=[whole],
+        out_specs=[whole] * 4,
         scratch_shapes=[
             pltpu.VMEM((tiles, rows, lanes), jnp.float32),
             pltpu.VMEM((tiles, rows, lanes), jnp.float32),
-            pltpu.SemaphoreType.DMA((10,)),
-            pltpu.SemaphoreType.DMA((10,)),
+            pltpu.VMEM((edge, lanes), jnp.float32),
+            pltpu.VMEM((edge, lanes), jnp.float32),
+            pltpu.SemaphoreType.DMA((8,)),
+            pltpu.SemaphoreType.DMA((8,)),
         ],
         compiler_params=pltpu.CompilerParams(
             collective_id=0, has_side_effects=True, vmem_limit_bytes=8 << 20
         ),
-    )(field, coef)
-
-
-def diffuse_kernel(
-    n_lat,
-    field,
-    coef,
-    norm,
-    west_cols,
-    east_cols,
-    south_field,
-    north_field,
-    south_coef,
-    north_coef,
-    lower,
-    upper,
-    cells,
-    out,
-    sampled,
-    grid,
-    other,
-    raw,
-    weights,
-    turned,
-    gathered,
+    )(field)
+
+
+def prepare_kernel(
+    n_lat, coef, west_cols, east_cols, south_coef, north_coef, weights, raw
 ):
-    lat = lax.axis_index("lat")
-    levels, rows, lanes = field.shape
+    rows, lanes = coef.shape[1:]
     tall = rows + 2 * HALO
     half = lanes // 2
-    strips = (levels + 1) // 2
-    has_south = lat > 0
-    has_north = lat < n_lat - 1
-
-    lane = lane_ids((tall, lanes)) % half
+    has_south = lax.axis_index("lat") > 0
+    has_north = lax.axis_index("lat") < n_lat - 1
+    inside = inside_domain((tall, lanes), rows, has_south, has_north)
     upper_half = lane_ids((tall, lanes)) >= half
-    row = lax.broadcasted_iota(jnp.int32, (tall, lanes), 0)
-    inside = jnp.logical_and(
-        jnp.logical_or(row >= HALO, has_south), jnp.logical_or(row < HALO + rows, has_north)
-    )
-    west_side = lane < half // 2
-    from_west = lane < COLS
-    from_east = lane >= half - COLS
-
-    def turn(values, shift):
-        shift = shift % lanes
-        return pltpu.roll(values, shift, 1) if shift else values
-
-    def strip(pair, first, second):
-        tile, k = divmod(pair, PAIRS)
-        low = jnp.where(west_side, turn(first, COLS), turn(first, half - COLS))
-        high = jnp.where(west_side, turn(second, COLS + half), turn(second, -COLS))
-        own = jnp.where(upper_half, high, low)
-        east = turn(east_cols[tile], half - COLS - COLS * k)
-        west = turn(west_cols[tile], COLS - COLS * k)
-        halo = jnp.where(inside, jnp.where(from_east, east, west), 0.0)
-        return jnp.where(jnp.logical_or(from_east, from_west), halo, own)
-
-    for level in range(levels):
-        grid[level, pl.ds(0, HALO), :] = jnp.where(has_south, south_field[level], 0.0)
-        grid[level, pl.ds(HALO, rows), :] = field[level]
-        grid[level, pl.ds(HALO + rows, HALO), :] = jnp.where(has_north, north_field[level], 0.0)
-    for number in range(coef.shape[0]):
-        raw[0, number, pl.ds(0, HALO), :] = jnp.where(has_south, south_coef[number], 0.0)
-        raw[0, number, pl.ds(HALO, rows), :] = coef[number]
-        raw[0, number, pl.ds(HALO + rows, HALO), :] = jnp.where(
-            has_north, north_coef[number], 0.0
+    for n in range(coef.shape[0]):
+        plane = jnp.concatenate(
+            [
+                jnp.where(has_south, south_coef[n], 0.0),
+                coef[n],
+                jnp.where(has_north, north_coef[n], 0.0),
+            ],
+            axis=0,
         )
-    for pair in range(strips):
-        first = grid[2 * pair]
-        second = grid[min(2 * pair + 1, levels - 1)]
-        grid[levels + pair] = strip(pair, first, second)
-    for number in range(0, coef.shape[0], 2):
-        pair = strips + number // 2
-        for offset in range(2):
-            plane = raw[0, number + offset]
-            both = strip(pair, plane, plane)
-            mirrored = turn(both, half)
-            raw[1, number + offset] = jnp.where(
-                upper_half, mirrored if offset == 0 else both, both if offset == 0 else mirrored
-            )
-
-    count = (tall - 2 * EDGE) // CHUNK
+        raw[0, n] = plane
+        both = strip_plane(plane, plane, east_cols[...], west_cols[...], n // 2, COLS, inside)
+        mirrored = turn(both, half)
+        raw[1, n] = jnp.where(upper_half, *((mirrored, both) if n % 2 == 0 else (both, mirrored)))
 
     def make_weights(step, carry):
         start = EDGE + step * CHUNK
@@ -246,7 +232,70 @@
                 weights[kind, number, pl.ds(step * CHUNK, CHUNK), :] = value
         return carry
 
-    lax.fori_loop(0, count, make_weights, 0)
+    lax.fori_loop(0, (tall - 2 * EDGE) // CHUNK, make_weights, 0)
+
+
+def prepare(coef, halos, n_lat):
+    count, rows, lanes = coef.shape
+    tall = rows + 2 * HALO
+    whole = pl.BlockSpec(memory_space=pltpu.VMEM)
+    return pl.pallas_call(
+        functools.partial(prepare_kernel, n_lat),
+        out_shape=jax.ShapeDtypeStruct((2, 7, tall - 2 * EDGE, lanes), jnp.float32),
+        in_specs=[whole] * 5,
+        out_specs=whole,
+        scratch_shapes=[pltpu.VMEM((2, count, tall, lanes), jnp.float32)],
+        compiler_params=pltpu.CompilerParams(vmem_limit_bytes=8 << 20),
+    )(coef, *halos)
+
+
+def diffuse_kernel(
+    n_lat,
+    field,
+    norm,
+    west_cols,
+    east_cols,
+    south_rows,
+    north_rows,
+    weights,
+    lower,
+    upper,
+    cells,
+    out,
+    sampled,
+    grid,
+    other,
+    turned,
+    gathered,
+):
+    levels, rows, lanes = field.shape
+    tall = rows + 2 * HALO
+    half = lanes // 2
+    strips = (levels + 1) // 2
+    has_south = lax.axis_index("lat") > 0
+    has_north = lax.axis_index("lat") < n_lat - 1
+    inside = inside_domain((tall, lanes), rows, has_south, has_north)
+
+    for level in range(levels):
+        at = pl.ds(STEPS * level, STEPS)
+        grid[level, pl.ds(0, HALO), :] = jnp.zeros((HALO, lanes), jnp.float32)
+        grid[level, pl.ds(HALO + rows, HALO), :] = jnp.zeros((HALO, lanes), jnp.float32)
+        grid[level, pl.ds(HALO - STEPS, STEPS), :] = jnp.where(has_south, south_rows[at, :], 0.0)
+        grid[level, pl.ds(HALO, rows), :] = field[level]
+        grid[level, pl.ds(HALO + rows, STEPS), :] = jnp.where(has_north, north_rows[at, :], 0.0)
+    for pair in range(strips):
+        tile, k = divmod(pair, PAIRS)
+        grid[levels + pair] = strip_plane(
+            grid[2 * pair],
+            grid[min(2 * pair + 1, levels - 1)],
+            east_cols[tile],
+            west_cols[tile],
+            k,
+            STEPS,
+            inside,
+        )
+
+    count = (tall - 2 * EDGE) // CHUNK
 
     def sweep(source, target):
         def one_chunk(step, carry):
@@ -333,7 +382,7 @@
     return table[pl.ds(number, 8, stride=0), :]
 
 
-def diffuse(field, coef, norm, halos, lower, upper, cells, n_lat):
+def diffuse(field, norm, halos, weights, lower, upper, cells, n_lat):
     levels, rows, lanes = field.shape
     tall = rows + 2 * HALO
     whole = pl.BlockSpec(memory_space=pltpu.VMEM)
@@ -345,18 +394,16 @@
             jax.ShapeDtypeStruct(field.shape, jnp.float32),
             jax.ShapeDtypeStruct((cells.shape[0] * PAD, lanes), jnp.float32),
         ),
-        in_specs=[whole] * (5 + len(halos)) + [scalars],
+        in_specs=[whole] * 9 + [scalars],
         out_specs=(whole, whole),
         scratch_shapes=[
             pltpu.VMEM((planes, tall, lanes), jnp.float32),
             pltpu.VMEM((planes, tall, lanes), jnp.float32),
-            pltpu.VMEM((2, coef.shape[0], tall, lanes), jnp.float32),
-            pltpu.VMEM((2, 7, tall - 2 * EDGE, lanes), jnp.float32),
             pltpu.VMEM((rows * PAD, lanes), jnp.float32),
             pltpu.VMEM((lanes, lanes), jnp.float32),
         ],
-        compiler_params=pltpu.CompilerParams(vmem_limit_bytes=30 << 20),
-    )(field, coef, norm, *halos, lower, upper, cells)
+        compiler_params=pltpu.CompilerParams(vmem_limit_bytes=24 << 20),
+    )(field, norm, *halos, weights, lower, upper, cells)
 
 
 def one_hot_slots(slots, q, rows):
@@ -424,21 +471,42 @@
     )(innovations, weights, place, owners, owners.reshape(1, count), ids)
 
 
-def post_kernel(source, target, held, send_sem, recv_sem, local_sem):
+def post_kernel(has_coef, source, *refs):
+    if has_coef:
+        coef, tiles, target, west_cols, east_cols, south_coef, north_coef, late = refs[:8]
+        held, send_sem, recv_sem, local_sem, pack_first, pack_last, late_sem = refs[8:]
+    else:
+        target, held, send_sem, recv_sem, local_sem = refs
     n_lat, n_lon = source.shape[:2]
-    lat = lax.axis_index("lat")
-    lon = lax.axis_index("lon")
+    lat, lon, up, down, right, left = neighbours(n_lat, n_lon)
     across = [lax.rem(lon + step, n_lon) for step in range(1, n_lon)]
     along = [lax.rem(lat + step, n_lat) for step in range(1, n_lat)]
+    corners = [(up, right), (up, left), (down, right), (down, left)] if has_coef else []
 
     barrier = pltpu.get_barrier_semaphore()
     for other in across:
         pl.semaphore_signal(barrier, inc=1, device_id=(lat, other), device_id_type=MESH)
     for other in along:
         pl.semaphore_signal(barrier, inc=1, device_id=(other, lon), device_id_type=MESH)
+    for there in corners:
+        pl.semaphore_signal(barrier, inc=1, device_id=there, device_id_type=MESH)
     own = pltpu.make_async_copy(source.at[:, lon], held.at[:, lon], local_sem)
     own.start()
-    pl.semaphore_wait(barrier, n_lon + n_lat - 2)
+    moves = []
+    if has_coef:
+        for level in range(late.shape[1]):
+            move = pltpu.make_async_copy(
+                tiles.at[EARLY + level], late.at[:, level], late_sem.at[level]
+            )
+            move.start()
+            moves.append(move)
+        rows = coef.shape[1]
+        low, high = packed_columns(
+            lambda plane: coef[plane], coef.shape[0], rows, COLS, 0, COEF_PAIRS
+        )
+        pack_first[...] = low
+        pack_last[...] = high
+    pl.semaphore_wait(barrier, n_lon + n_lat - 2 + len(corners))
 
     def push(here, there, number, device):
         copy = pltpu.make_async_remote_copy(
@@ -456,6 +524,23 @@
         push(source.at[:, other], held.at[:, lon], number, (lat, other))
         for number, other in enumerate(across)
     ]
+    edges = []
+    if has_coef:
+        first = pl.ds(0, HALO)
+        last = pl.ds(rows - HALO, HALO)
+        middle = pl.ds(HALO, rows)
+        above = pl.ds(HALO + rows, HALO)
+        for here, there, device in (
+            (coef.at[:, last, :], south_coef, (up, lon)),
+            (coef.at[:, first, :], north_coef, (down, lon)),
+            (pack_last, west_cols.at[middle, :], (lat, right)),
+            (pack_first, east_cols.at[middle, :], (lat, left)),
+            (pack_last.at[last, :], west_cols.at[first, :], (up, right)),
+            (pack_first.at[last, :], east_cols.at[first, :], (up, left)),
+            (pack_last.at[first, :], west_cols.at[above, :], (down, right)),
+            (pack_first.at[first, :], east_cols.at[above, :], (down, left)),
+        ):
+            edges.append(push(here, there, n_lon + n_lat + len(edges), device))
     own.wait()
     for copy in copies:
         copy.wait()
@@ -466,33 +551,54 @@
     own = pltpu.make_async_copy(held.at[lat], target.at[lat], local_sem)
     own.start()
     own.wait()
-    for copy in copies:
+    for copy in copies + edges + moves:
         copy.wait()
 
 
-def post(packet, n_lat, n_lon, collective_id):
+def post(packet, n_lat, n_lon, collective_id, coef=None, tiles=None):
     whole = pl.BlockSpec(memory_space=pltpu.VMEM)
+    anywhere = pl.BlockSpec(memory_space=pl.ANY)
     blocks = packet.reshape(n_lat, n_lon, -1, LANES)
-    received = pl.pallas_call(
-        post_kernel,
-        out_shape=jax.ShapeDtypeStruct(blocks.shape, jnp.float32),
-        in_specs=[whole],
-        out_specs=whole,
-        scratch_shapes=[
-            pltpu.VMEM(blocks.shape, jnp.float32),
-            pltpu.SemaphoreType.DMA((n_lon + n_lat,)),
-            pltpu.SemaphoreType.DMA((n_lon + n_lat,)),
-            pltpu.SemaphoreType.DMA,
-        ],
+    has_coef = coef is not None
+    sems = n_lon + n_lat + 8 * has_coef
+    out_shape = [jax.ShapeDtypeStruct(blocks.shape, jnp.float32)]
+    scratch = [
+        pltpu.VMEM(blocks.shape, jnp.float32),
+        pltpu.SemaphoreType.DMA((sems,)),
+        pltpu.SemaphoreType.DMA((sems,)),
+        pltpu.SemaphoreType.DMA,
+    ]
+    operands, in_specs, out_specs = [blocks], [whole], [whole]
+    if has_coef:
+        count, rows, lanes = coef.shape
+        levels, slots, depth, _ = tiles.shape
+        packed = jax.ShapeDtypeStruct((rows + 2 * HALO, lanes), jnp.float32)
+        edge = jax.ShapeDtypeStruct((count, HALO, lanes), jnp.float32)
+        late = jax.ShapeDtypeStruct((slots, levels - EARLY, depth, lanes), jnp.float32)
+        out_shape += [packed, packed, edge, edge, late]
+        scratch += [
+            pltpu.VMEM((rows, lanes), jnp.float32),
+            pltpu.VMEM((rows, lanes), jnp.float32),
+            pltpu.SemaphoreType.DMA((levels - EARLY,)),
+        ]
+        operands += [coef, tiles]
+        in_specs += [whole, anywhere]
+        out_specs += [whole] * 4 + [anywhere]
+    received, *rest = pl.pallas_call(
+        functools.partial(post_kernel, has_coef),
+        out_shape=out_shape,
+        in_specs=in_specs,
+        out_specs=out_specs,
+        scratch_shapes=scratch,
         compiler_params=pltpu.CompilerParams(
             collective_id=collective_id, has_side_effects=True, vmem_limit_bytes=4 << 20
         ),
-    )(blocks)
-    return received.reshape(packet.shape)
+    )(*operands)
+    return (received.reshape(packet.shape), *rest)
 
 
 def spread_kernel(
-    levels, packet, observed, lower, upper, cells_out, turned, other, cells, sem
+    levels, packet, seen, lower, upper, cells_out, turned, observed, other, cells, sem
 ):
     total, lanes = packet.shape
     per_row = lanes // PAD
@@ -555,7 +661,10 @@
         return carry
 
     lax.fori_loop(0, tiles * per_row, spread_block, 0)
-    observed[...] = observed[...] + other[...]
+    rows = seen.shape[1]
+    for level in range(levels):
+        at = pl.ds(level, rows, stride=PAD)
+        seen[level] = observed[at, :] + other[at, :]
 
 
 def spread(packet, levels, rows):
@@ -566,7 +675,7 @@
     return pl.pallas_call(
         functools.partial(spread_kernel, levels),
         out_shape=(
-            jax.ShapeDtypeStruct((rows * PAD, lanes), jnp.float32),
+            jax.ShapeDtypeStruct((levels, rows, lanes), jnp.float32),
             masks,
             masks,
             jax.ShapeDtypeStruct((blocks, 8, lanes), jnp.int32),
@@ -576,6 +685,7 @@
         scratch_shapes=[
             pltpu.VMEM(packet.shape, jnp.float32),
             pltpu.VMEM((rows * PAD, lanes), jnp.float32),
+            pltpu.VMEM((rows * PAD, lanes), jnp.float32),
             pltpu.SMEM((blocks, 8, lanes), jnp.int32),
             pltpu.SemaphoreType.DMA,
         ],
@@ -583,8 +693,8 @@
     )(packet)
 
 
-def combine_kernel(cells, observed, tiles, norm, field):
-    slots, levels, depth, lanes = tiles.shape
+def combine_kernel(cells, seen, early, late, norm, field):
+    slots, _, depth, lanes = early.shape
     n_lon = lax.axis_size("lon")
     per_device = slots // n_lon
     per_row = lanes // PAD
@@ -594,25 +704,23 @@
     def one_tile(slot, carry):
         at = (base + slot // per_device) * row_group
         block = (at // lanes) * per_row + lax.rem(slot, per_device)
-        row = pl.multiple_of(cells[block, 7, lax.rem(at, lanes)] * depth, depth)
-        rows = pl.ds(row, depth)
-        for level in range(levels):
-            seen = observed[pl.ds(row * PAD + level, depth, stride=PAD), :]
-            field[level, rows, :] = norm[level, rows, :] * (seen + tiles[slot, level])
+        rows = pl.ds(pl.multiple_of(cells[block, 7, lax.rem(at, lanes)] * depth, depth), depth)
+        for part, tiles in ((pl.ds(0, early.shape[1]), early), (pl.ds(early.shape[1], late.shape[1]), late)):
+            field[part, rows, :] = norm[part, rows, :] * (seen[part, rows, :] + tiles[slot])
         return carry
 
     lax.fori_loop(0, slots, one_tile, 0)
 
 
-def combine(cells, observed, tiles, norm):
+def combine(cells, seen, early, late, norm):
     whole = pl.BlockSpec(memory_space=pltpu.VMEM)
     return pl.pallas_call(
         combine_kernel,
         out_shape=jax.ShapeDtypeStruct(norm.shape, jnp.float32),
-        in_specs=[pl.BlockSpec(memory_space=pltpu.SMEM)] + [whole] * 3,
+        in_specs=[pl.BlockSpec(memory_space=pltpu.SMEM)] + [whole] * 4,
         out_specs=whole,
         compiler_params=pltpu.CompilerParams(vmem_limit_bytes=8 << 20),
-    )(cells, observed, tiles, norm)
+    )(cells, seen, early, late, norm)
 
 
 def collect_kernel(levels, returned, slots, out):
@@ -659,19 +767,20 @@
     levels, rows, lanes = norm_factor.shape
     n_lat = lax.axis_size("lat")
     n_lon = lax.axis_size("lon")
+    early = lax.all_to_all(
+        jnp.transpose(model_tiles[:EARLY], (1, 0, 2, 3)), "lon", split_axis=0, concat_axis=0, tiled=True
+    )
+    coef = jnp.stack([face_x, face_y, cross_term, wet_mask.astype(jnp.float32)])
     place = jnp.stack([prof_row, prof_col])
     packet, slots = route(innovations, interp_weights, place, owners, model_ids, n_lat * n_lon)
-    packet = post(packet, n_lat, n_lon, 1)
-    tiles, packet = lax.optimization_barrier((jnp.transpose(model_tiles, (1, 0, 2, 3)), packet))
-    tiles = lax.all_to_all(tiles, "lon", split_axis=0, concat_axis=0, tiled=True)
-    observed, lower, upper, cells = spread(packet, levels, rows)
-    field = combine(cells, observed, tiles, norm_factor)
-    coef = jnp.stack([face_x, face_y, cross_term, wet_mask.astype(jnp.float32)])
-    halos = exchange(field, coef, n_lat, n_lon)
-    smoothed, sampled = diffuse(
-        field, coef, norm_factor, halos, lower, upper, cells, n_lat
-    )
-    returned = post(sampled, n_lat, n_lon, 2)
+    packet, *coef_halos, late = post(packet, n_lat, n_lon, 1, coef, model_tiles)
+    late = lax.all_to_all(late, "lon", split_axis=0, concat_axis=0, tiled=True)
+    seen, lower, upper, cells = spread(packet, levels, rows)
+    weights = prepare(coef, coef_halos, n_lat)
+    field = combine(cells, seen, early, late, norm_factor)
+    halos = exchange(field, n_lat, n_lon)
+    smoothed, sampled = diffuse(field, norm_factor, halos, weights, lower, upper, cells, n_lat)
+    (returned,) = post(sampled, n_lat, n_lon, 2)
     profile_values = collect(returned, slots, levels)
     return (smoothed, profile_values)
 

time: 182 us -> 171 us (0.940)
  waiting for transfers between devices: 23.5 us -> 0.01 us
  starting transfers between devices: 7.88 us -> 15.6 us
  local copies, waits for them, and re-layouts: 13.3 us -> 17 us
    all_to_all x1 -> x2, waiting for transfers between devices: 23.5 us -> 0.01 us  [the longest x1 0.01 us: on_device(): lax.all_to_all(jnp.transpose(model_tiles[:EARLY], (1, 0, 2, 3)), 'lon', s...]
    all_to_all x1 -> x2, starting transfers between devices: 7.88 us -> 15.6 us  [the longest x1 9.72 us: on_device(): lax.all_to_all(jnp.transpose(model_tiles[:EARLY], (1, 0, 2, 3)), 'lon', s...]
    pallas_call x1, Pallas kernels: 23.3 us -> 15.9 us  [exchange(): pl.pallas_call(functools.partial(exchange_kernel, n_lat, n_lon), out_shap...]
    pallas_call x2 -> x3, Pallas kernels: 31.9 us -> 38.1 us  [the longest x2 35.9 us: post(): pl.pallas_call(functools.partial(post_kernel, has_coef), out_shape=out_sh...]
    pallas_call x1, Pallas kernels: 12.4 us -> 18.2 us  [spread(): pl.pallas_call(functools.partial(spread_kernel, levels), out_shape=(jax.S...]
    pallas_call x1, Pallas kernels: 56.2 us -> 53.6 us  [diffuse(): pl.pallas_call(functools.partial(diffuse_kernel, n_lat), out_shape=(jax.S...]
    transpose x0 -> x1, local copies, waits for them, and re-layouts: none -> 2.48 us  [on_device(): jnp.transpose(model_tiles[:EARLY], (1, 0, 2, 3))]
    unnamed x26 -> x45, local copies, waits for them, and re-layouts: 13.3 us -> 14.5 us
  transfers between devices with their start and end apart: 1 -> 2, of which waited for: 1 -> 0; matrix products, arithmetic and copies ran while one was open for 2% -> 2% of each run, Pallas kernels for 7% -> 26%
where the time goes in v5:
time: 171 us; the launch traced here: 170 us
  Pallas kernels  134 us (78%)
  local copies, waits for them, and re-layouts  17 us (10%)
  starting transfers between devices  15.6 us (9%)
  other arithmetic  2.69 us (2%)
    pallas_call x1, Pallas kernels, diffuse(): pl.pallas_call(functools.partial(diffuse_kernel, n_lat), out_shape=(jax.S...  53.6 us
    pallas_call x2, Pallas kernels, post(): pl.pallas_call(functools.partial(post_kernel, has_coef), out_shape=out_sh...  35.9 us
    pallas_call x1, Pallas kernels, spread(): pl.pallas_call(functools.partial(spread_kernel, levels), out_shape=(jax.S...  18.2 us
    pallas_call x1, Pallas kernels, exchange(): pl.pallas_call(functools.partial(exchange_kernel, n_lat, n_lon), out_shap...  15.9 us
    unnamed x45, local copies, waits for them, and re-layouts  14.5 us
    all_to_all x1, starting transfers between devices, on_device(): lax.all_to_all(jnp.transpose(model_tiles[:EARLY], (1, 0, 2, 3)), 'lon', s...  9.72 us
    all_to_all x1, starting transfers between devices, on_device(): late = lax.all_to_all(late, 'lon', split_axis=0, concat_axis=0, tiled=True)  5.88 us
    pallas_call x1, Pallas kernels, combine(): pl.pallas_call(combine_kernel, out_shape=jax.ShapeDtypeStruct(norm.shape,...  3.82 us
  transfers between devices with their start and end apart: 2, of which 0 were waited for; matrix products, arithmetic and copies ran while one was open for 2% of the time, Pallas kernels for 26%

profile of v5, /device:TPU:1, one launch (start us, length us, event | category | flops | bytes accessed | tf_op | source)
XLA Modules:
  0.0 170.1 jit_solution(5383657245006124332)
XLA Ops:
  0.6 0.0 copy-start.18
  0.6 0.0 copy-start.21
  0.7 0.0 copy-start.19
  0.7 2.5 %copy_bitcast_fusion = f32[32,10,8,128]{3,2,1,0:T(8,128)} fusion(f32[25,32,8,128]{3,2,1,0:T(8,128)} %refs_1_.1), kind=kLoop, calls=%fused_computation | loop fusion | bytes 2621440 | tf_op jit(solution)/shard_map/transpose | solution.py:771
  3.1 9.7 %all-to-all-start = ((f32[32,10,8,128]{3,2,1,0:T(8,128)}), f32[32,10,8,128]{3,2,1,0:T(8,128)}, u32[]{:S(2)}, u32[]{:S(2)}) async-start(f32[32,10,8,128]{3,2,1,0:T(8,128)} %copy_bitcast_fusion), calls=%async_computation | async-start | bytes 2621440 | tf_op jit(solution)/shard_map/all_to_all | solution.py:770
  12.9 0.0 copy-done.18
  12.9 0.1 copy.14.owner_column
  13.0 0.0 copy-done.21
  13.0 0.7 pad_add_fusion.place
  13.7 0.0 copy-done.19
  13.7 0.0 copy-start.17
  13.7 0.8 copy-done.17
  14.6 0.7 copy-done.20
  15.2 2.3 %shard_map.131 = (f32[256,128]{1,0:T(8,128)S(1)}, s32[1,512]{1,0:T(1,128)S(1)}) custom-call(f32[25,512]{1,0:T(8,128)S(1)} %copy-done.17, f32[4,512]{1,0:T(4,128)S(1)} %copy-done.19, s32[2,512]{1,0:T(2,128)S(1)} %pad_add_fusion.place, s32[512,1]{1,0:T(8,128)S(1)} %copy.14.owner_column, s32[1,512]{1,0:T(1,128)S(1)} %bitcast.18, s32[1,32]{1,0:T(1,128)S(1)} %copy-done.20), custom_call_target="tpu_custom_call" | custom-call | tf_op jit(solution)/shard_map/pallas_call | solution.py:461
  17.5 0.9 convert_bitcast_fusion
  18.5 1.1 pad_maximum_fusion.refs_0_.coef
  19.5 0.0 copy-done.3
  19.5 21.3 %shard_map.132 = (f32[8,16,2,128]{3,2,1,0:T(2,128)S(1)}, f32[288,128]{1,0:T(8,128)S(1)}, f32[288,128]{1,0:T(8,128)S(1)}, f32[4,16,128]{2,1,0:T(8,128)S(1)}, f32[...) custom-call(f32[8,16,2,128]{3,2,1,0:T(2,128)S(1)} %bitcast.15, f32[4,256,128]{2,1,0:T(8,128)S(1)} %pad_maximum_fusion.refs_0_.coef, ...), custom_call_target="tpu_custom_call" | custom-call | tf_op jit(solution)/shard_map/pallas_call | solution.py:587
  40.8 0.0 copy-start.4
  40.8 0.8 copy-done.4
  41.6 1.3 copy-done.8
  42.9 0.7 copy-done.13
  43.6 0.7 copy-done.15
  44.2 0.0 all-to-all-done.early
  44.2 5.9 %all-to-all-start.1 = ((f32[32,15,8,128]{3,2,1,0:T(8,128)}), f32[32,15,8,128]{3,2,1,0:T(8,128)}, u32[]{:S(2)}, u32[]{:S(2)}) async-start(f32[32,15,8,128]{3,2,1,0:T(8,128)} %copy-done.8), calls=%async_computation.1 | async-start | bytes 3932160 | tf_op jit(solution)/shard_map/all_to_all | solution.py:777
  50.1 0.9 copy-done.16
  51.0 18.2 %shard_map.133 = (f32[25,256,128]{2,1,0:T(8,128)S(1)}, f32[1024,128]{1,0:T(8,128)S(1)}, f32[1024,128]{1,0:T(8,128)S(1)}, s32[8,8,128]{2,1,0:T(8,128)S(1)}) custom-call(f32[256,128]{1,0:T(8,128)S(1)} %bitcast.16), custom_call_target="tpu_custom_call" | custom-call | tf_op jit(solution)/shard_map/pallas_call | solution.py:675
  69.2 0.0 copy-start.6
  69.2 1.7 copy-done.6
  70.9 0.8 copy-done.9
  71.7 0.8 copy-done.11
  72.5 1.0 copy-done.5
  73.6 0.9 copy-done.14
  74.5 2.3 %shard_map.136.weights = f32[2,7,280,128]{3,2,1,0:T(8,128)S(1)} custom-call(f32[4,256,128]{2,1,0:T(8,128)S(1)} %copy-done.5, f32[288,128]{1,0:T(8,128)S(1)} %get-tuple-element.29.west_cols, f32[288,128]{1,0:T(8,128)S(1)} %copy-done.14, f32[4,16,128]{2,1,0:T(8,128)S(1)} %get-tuple-element.31.south_coef, f32[4,16,128]{2,1,0:T(8,128)S(1)} %get-tuple-element.32.north_coef), custom_call_target="tpu_custom_call" | custom-call | tf_op jit(solution)/shard_map/pallas_call | solution.py:242
  76.7 0.0 copy-start.1
  76.7 1.3 copy-done.1
  78.1 0.0 all-to-all-done.1.late
  78.1 0.0 copy-done
  78.1 1.9 %copy-done.7 = f32[25,256,128]{2,1,0:T(8,128)S(1)} copy-done((f32[25,256,128]{2,1,0:T(8,128)S(1)}, f32[25,256,128]{2,1,0:T(8,128)}, u32[]{:S(2)}) %copy-start.7) | copy-done | bytes 3276824
  80.0 3.8 %shard_map.134.field = f32[25,256,128]{2,1,0:T(8,128)S(1)} custom-call(s32[8,8,128]{2,1,0:T(8,128)S(1)} %get-tuple-element.22.cells, f32[25,256,128]{2,1,0:T(8,128)S(1)} %copy-done.7, f32[32,10,8,128]{3,2,1,0:T(8,128)} %all-to-all-done.early, f32[32,15,8,128]{3,2,1,0:T(8,128)} %all-to-all-done.1.late, f32[25,256,128]{2,1,0:T(8,128)S(1)} %copy-done), custom_call_target="tpu_custom_call" | custom-call | tf_op jit(solution)/shard_map/pallas_call | solution.py:717
  83.8 0.0 copy-start.2
  83.9 15.9 %shard_map.135 = (f32[3,288,128]{2,1,0:T(8,128)S(1)}, f32[3,288,128]{2,1,0:T(8,128)S(1)}, f32[256,128]{1,0:T(8,128)S(1)}, f32[256,128]{1,0:T(8,128)S(1)}) custom-call(f32[25,256,128]{2,1,0:T(8,128)S(1)} %shard_map.134.field), custom_call_target="tpu_custom_call" | custom-call | tf_op jit(solution)/shard_map/pallas_call | solution.py:173
  99.8 0.0 copy-done.2
  99.8 0.0 copy-done.10
  99.8 0.0 copy-done.12
  99.8 53.6 %shard_map.137 = (f32[25,256,128]{2,1,0:T(8,128)}, f32[256,128]{1,0:T(8,128)S(1)}) custom-call(f32[25,256,128]{2,1,0:T(8,128)S(1)} %shard_map.134.field, f32[25,256,128]{2,1,0:T(8,128)S(1)} %copy-done, f32[3,288,128]{2,1,0:T(8,128)S(1)} %get-tuple-element.25.west_cols, f32[3,288,128]{2,1,0:T(8,128)S(1)} %get-tuple-element.26.east_cols, ...), custom_call_target="tpu_custom_call" | custom-call | tf_op jit(solution)/shard_map/pallas_call | solution.py:391
  153.4 14.6 %shard_map.138 = f32[8,16,2,128]{3,2,1,0:T(2,128)S(1)} custom-call(f32[8,16,2,128]{3,2,1,0:T(2,128)S(1)} %bitcast.17), custom_call_target="tpu_custom_call" | custom-call | tf_op jit(solution)/shard_map/pallas_call | solution.py:587
  168.0 2.1 %shard_map.139 = f32[25,512]{1,0:T(8,128)} custom-call(f32[256,128]{1,0:T(8,128)S(1)} %bitcast.14, s32[1,512]{1,0:T(1,128)S(1)} %get-tuple-element.37.slots), custom_call_target="tpu_custom_call" | custom-call | tf_op jit(solution)/shard_map/pallas_call | solution.py:744
  (14 shorter events, 0.0 us)
Async XLA Ops:
  0.6 12.2 %copy-start.18 = (s32[512,1]{0,1:T(1,128)S(1)}, s32[512,1]{0,1:T(1,128)}, u32[]{:S(2)}) copy-start(s32[512,1]{0,1:T(1,128)} %param.13) | copy-start | bytes 6148
  0.6 12.4 %copy-start.21 = (s32[512]{0:T(512)S(1)}, s32[512]{0:T(512)}, u32[]{:S(2)}) copy-start(s32[512]{0:T(512)} %param.15) | copy-start | bytes 6148
  0.7 13.1 %copy-start.19 = (f32[4,512]{1,0:T(4,128)S(1)}, f32[4,512]{1,0:T(4,128)}, u32[]{:S(2)}) copy-start(f32[4,512]{1,0:T(4,128)} %weights.1) | copy-start | bytes 24580
  3.1 16.4 %copy-start.3 = (f32[25,32,8,128]{3,2,1,0:T(8,128)S(1)}, f32[25,32,8,128]{3,2,1,0:T(8,128)}, u32[]{:S(2)}) copy-start(f32[25,32,8,128]{3,2,1,0:T(8,128)} %refs_1_.1) | copy-start | bytes 9830404
  3.1 41.1 %all-to-all-start = ((f32[32,10,8,128]{3,2,1,0:T(8,128)}), f32[32,10,8,128]{3,2,1,0:T(8,128)}, u32[]{:S(2)}, u32[]{:S(2)}) async-start(f32[32,10,8,128]{3,2,1,0:T(8,128)} %copy_bitcast_fusion), calls=%async_computation | async-start | bytes 2621440 | tf_op jit(solution)/shard_map/all_to_all | solution.py:770
  13.7 0.8 copy-start.17
  14.6 0.7 copy-start.20
  40.8 0.8 copy-start.4
  41.6 1.3 copy-start.8
  42.9 0.7 copy-start.13
  43.6 0.7 copy-start.15
  44.2 33.8 %copy-start = (f32[25,256,128]{2,1,0:T(8,128)S(1)}, f32[25,256,128]{2,1,0:T(8,128)}, u32[]{:S(2)}) copy-start(f32[25,256,128]{2,1,0:T(8,128)} %norm.3) | copy-start | bytes 9830404
  44.2 33.8 %all-to-all-start.1 = ((f32[32,15,8,128]{3,2,1,0:T(8,128)}), f32[32,15,8,128]{3,2,1,0:T(8,128)}, u32[]{:S(2)}, u32[]{:S(2)}) async-start(f32[32,15,8,128]{3,2,1,0:T(8,128)} %copy-done.8), calls=%async_computation.1 | async-start | bytes 3932160 | tf_op jit(solution)/shard_map/all_to_all | solution.py:777
  50.1 0.9 copy-start.16
  69.2 1.7 %copy-start.6 = (f32[25,256,128]{2,1,0:T(8,128)}, f32[25,256,128]{2,1,0:T(8,128)S(1)}, u32[]{:S(2)}) copy-start(f32[25,256,128]{2,1,0:T(8,128)S(1)} %get-tuple-element.23.seen) | copy-start | bytes 9830404
  70.9 0.8 copy-start.9
  71.7 0.8 copy-start.11
  72.5 1.0 copy-start.5
  73.6 0.9 copy-start.14
  76.7 1.3 copy-start.1
  78.1 1.9 %copy-start.7 = (f32[25,256,128]{2,1,0:T(8,128)S(1)}, f32[25,256,128]{2,1,0:T(8,128)}, u32[]{:S(2)}) copy-start(f32[25,256,128]{2,1,0:T(8,128)} %copy-done.6) | copy-start | bytes 9830404
  83.8 16.0 %copy-start.2 = (f32[2,7,280,128]{3,2,1,0:T(8,128)S(1)}, f32[2,7,280,128]{3,2,1,0:T(8,128)}, u32[]{:S(2)}) copy-start(f32[2,7,280,128]{3,2,1,0:T(8,128)} %copy-done.1) | copy-start | bytes 6021124
  83.9 16.0 %copy-start.10 = (f32[1024,128]{1,0:T(8,128)S(1)}, f32[1024,128]{1,0:T(8,128)}, u32[]{:S(2)}) copy-start(f32[1024,128]{1,0:T(8,128)} %copy-done.9) | copy-start | bytes 1572868
  83.9 16.0 %copy-start.12 = (f32[1024,128]{1,0:T(8,128)S(1)}, f32[1024,128]{1,0:T(8,128)}, u32[]{:S(2)}) copy-start(f32[1024,128]{1,0:T(8,128)} %copy-done.11) | copy-start | bytes 1572868

commit v6 on v5

--- a/solution.py
+++ b/solution.py
@@ -10,13 +10,17 @@
 STEPS = 10
 CAPACITY = 8
 PAD = 32
+DEEP = 40
 UNROLL = 32
+BIG = 62 << 20
+PARTS = 2
 HALO = 16
 LANES = 128
 COLS = 12
 PAIRS = 6
 COEF_PAIRS = 5
 EARLY = 10
+BATCH = 5
 CHUNK = 40
 EDGE = 4
 MESH = pl.DeviceIdType.MESH
@@ -92,38 +96,38 @@
 def exchange_kernel(
     n_lat,
     n_lon,
-    field,
+    packs,
     west_cols,
     east_cols,
     south_rows,
     north_rows,
-    pack_first,
-    pack_last,
-    pack_low,
-    pack_high,
     send_sem,
     recv_sem,
 ):
     lat, lon, up, down, right, left = neighbours(n_lat, n_lon)
-    levels, rows = field.shape[:2]
-
+    tiles, rows = packs.shape[0] // 2 - 1, packs.shape[1]
+    pack_first, pack_last = packs.at[pl.ds(0, tiles)], packs.at[pl.ds(tiles, tiles)]
+    pack_low, pack_high = packs.at[2 * tiles], packs.at[2 * tiles + 1]
+    first = pl.ds(0, HALO)
+    last = pl.ds(rows - HALO, HALO)
+    own = pl.ds(HALO, rows)
+    above = pl.ds(HALO + rows, HALO)
+    sends = (
+        (pack_high, south_rows, (up, lon)),
+        (pack_low, north_rows, (down, lon)),
+        (pack_last, west_cols.at[:, own, :], (lat, right)),
+        (pack_first, east_cols.at[:, own, :], (lat, left)),
+        (pack_last.at[:, last, :], west_cols.at[:, first, :], (up, right)),
+        (pack_first.at[:, last, :], east_cols.at[:, first, :], (up, left)),
+        (pack_last.at[:, first, :], west_cols.at[:, above, :], (down, right)),
+        (pack_first.at[:, first, :], east_cols.at[:, above, :], (down, left)),
+    )
     barrier = pltpu.get_barrier_semaphore()
-    for there in (
-        (lat, right),
-        (lat, left),
-        (up, lon),
-        (down, lon),
-        (up, right),
-        (up, left),
-        (down, right),
-        (down, left),
-    ):
+    for _, _, there in sends:
         pl.semaphore_signal(barrier, inc=1, device_id=there, device_id_type=MESH)
-
+    pl.semaphore_wait(barrier, len(sends))
     copies = []
-
-    def send(source, target, there):
-        number = len(copies)
+    for number, (source, target, there) in enumerate(sends):
         copy = pltpu.make_async_remote_copy(
             src_ref=source,
             dst_ref=target,
@@ -134,63 +138,29 @@
         )
         copy.start()
         copies.append(copy)
-
-    for level in range(levels):
-        at = pl.ds(STEPS * level, STEPS)
-        pack_high[at, :] = field[level, pl.ds(rows - STEPS, STEPS), :]
-        pack_low[at, :] = field[level, pl.ds(0, STEPS), :]
-    pl.semaphore_wait(barrier, 8)
-    send(pack_high, south_rows, (up, lon))
-    send(pack_low, north_rows, (down, lon))
-    for tile in range(pack_first.shape[0]):
-        low, high = packed_columns(
-            lambda plane: field[plane], levels, rows, STEPS, tile * PAIRS, PAIRS
-        )
-        pack_first[tile] = low
-        pack_last[tile] = high
-
-    first = pl.ds(0, HALO)
-    last = pl.ds(rows - HALO, HALO)
-    own = pl.ds(HALO, rows)
-    above = pl.ds(HALO + rows, HALO)
-    send(pack_last, west_cols.at[:, own, :], (lat, right))
-    send(pack_first, east_cols.at[:, own, :], (lat, left))
-    send(pack_last.at[:, last, :], west_cols.at[:, first, :], (up, right))
-    send(pack_first.at[:, last, :], east_cols.at[:, first, :], (up, left))
-    send(pack_last.at[:, first, :], west_cols.at[:, above, :], (down, right))
-    send(pack_first.at[:, first, :], east_cols.at[:, above, :], (down, left))
     for copy in copies:
         copy.wait()
 
 
-def exchange(field, n_lat, n_lon):
-    levels, rows, lanes = field.shape
-    tiles = -(-((levels + 1) // 2) // PAIRS)
-    edge = -(-levels * STEPS // 8) * 8
-    whole = pl.BlockSpec(memory_space=pltpu.VMEM)
-    packed = jax.ShapeDtypeStruct((tiles, rows + 2 * HALO, lanes), jnp.float32)
-    edges = jax.ShapeDtypeStruct((edge, lanes), jnp.float32)
+def exchange(packs, n_lat, n_lon):
+    count, rows, lanes = packs.shape
+    anywhere = pl.BlockSpec(memory_space=pl.ANY)
+    packed = jax.ShapeDtypeStruct((count // 2 - 1, rows + 2 * HALO, lanes), jnp.float32)
+    edges = jax.ShapeDtypeStruct((rows, lanes), jnp.float32)
     return pl.pallas_call(
         functools.partial(exchange_kernel, n_lat, n_lon),
         out_shape=(packed, packed, edges, edges),
-        in_specs=[whole],
-        out_specs=[whole] * 4,
-        scratch_shapes=[
-            pltpu.VMEM((tiles, rows, lanes), jnp.float32),
-            pltpu.VMEM((tiles, rows, lanes), jnp.float32),
-            pltpu.VMEM((edge, lanes), jnp.float32),
-            pltpu.VMEM((edge, lanes), jnp.float32),
-            pltpu.SemaphoreType.DMA((8,)),
-            pltpu.SemaphoreType.DMA((8,)),
-        ],
+        in_specs=[anywhere],
+        out_specs=[anywhere] * 4,
+        scratch_shapes=[pltpu.SemaphoreType.DMA((8,)), pltpu.SemaphoreType.DMA((8,))],
         compiler_params=pltpu.CompilerParams(
-            collective_id=0, has_side_effects=True, vmem_limit_bytes=8 << 20
+            collective_id=0, has_side_effects=True, vmem_limit_bytes=BIG
         ),
-    )(field)
+    )(packs)
 
 
 def prepare_kernel(
-    n_lat, coef, west_cols, east_cols, south_coef, north_coef, weights, raw
+    n_lat, coef, west_cols, east_cols, south_coef, north_coef, weights_out, weights, raw, sem
 ):
     rows, lanes = coef.shape[1:]
     tall = rows + 2 * HALO
@@ -233,6 +203,9 @@
         return carry
 
     lax.fori_loop(0, (tall - 2 * EDGE) // CHUNK, make_weights, 0)
+    copy = pltpu.make_async_copy(weights, weights_out, sem)
+    copy.start()
+    copy.wait()
 
 
 def prepare(coef, halos, n_lat):
@@ -243,23 +216,27 @@
         functools.partial(prepare_kernel, n_lat),
         out_shape=jax.ShapeDtypeStruct((2, 7, tall - 2 * EDGE, lanes), jnp.float32),
         in_specs=[whole] * 5,
-        out_specs=whole,
-        scratch_shapes=[pltpu.VMEM((2, count, tall, lanes), jnp.float32)],
-        compiler_params=pltpu.CompilerParams(vmem_limit_bytes=8 << 20),
+        out_specs=pl.BlockSpec(memory_space=pltpu.HBM),
+        scratch_shapes=[
+            pltpu.VMEM((2, 7, tall - 2 * EDGE, lanes), jnp.float32),
+            pltpu.VMEM((2, count, tall, lanes), jnp.float32),
+            pltpu.SemaphoreType.DMA,
+        ],
+        compiler_params=pltpu.CompilerParams(vmem_limit_bytes=BIG),
     )(coef, *halos)
 
 
 def diffuse_kernel(
     n_lat,
     field,
-    norm,
+    norm_far,
+    weights_far,
+    lower_far,
+    upper_far,
     west_cols,
     east_cols,
     south_rows,
     north_rows,
-    weights,
-    lower,
-    upper,
     cells,
     out,
     sampled,
@@ -267,6 +244,12 @@
     other,
     turned,
     gathered,
+    norm,
+    weights,
+    lower,
+    upper,
+    sems,
+    out_sems,
 ):
     levels, rows, lanes = field.shape
     tall = rows + 2 * HALO
@@ -276,13 +259,28 @@
     has_north = lax.axis_index("lat") < n_lat - 1
     inside = inside_domain((tall, lanes), rows, has_south, has_north)
 
+    near = grid.at[pl.ds(0, levels), pl.ds(HALO, rows), :]
+    copies = [
+        pltpu.make_async_copy(far, here, sems.at[number])
+        for number, (far, here) in enumerate(
+            (
+                (field, near),
+                (weights_far, weights),
+                (norm_far, norm),
+                (lower_far, lower),
+                (upper_far, upper),
+            )
+        )
+    ]
+    for copy in copies:
+        copy.start()
     for level in range(levels):
         at = pl.ds(STEPS * level, STEPS)
         grid[level, pl.ds(0, HALO), :] = jnp.zeros((HALO, lanes), jnp.float32)
         grid[level, pl.ds(HALO + rows, HALO), :] = jnp.zeros((HALO, lanes), jnp.float32)
         grid[level, pl.ds(HALO - STEPS, STEPS), :] = jnp.where(has_south, south_rows[at, :], 0.0)
-        grid[level, pl.ds(HALO, rows), :] = field[level]
         grid[level, pl.ds(HALO + rows, STEPS), :] = jnp.where(has_north, north_rows[at, :], 0.0)
+    copies[0].wait()
     for pair in range(strips):
         tile, k = divmod(pair, PAIRS)
         grid[levels + pair] = strip_plane(
@@ -323,6 +321,8 @@
 
         lax.fori_loop(0, count, one_chunk, 0)
 
+    copies[1].wait()
+
     def two_steps(number, carry):
         sweep(grid, other)
         sweep(other, grid)
@@ -330,6 +330,9 @@
 
     lax.fori_loop(0, STEPS // 2, two_steps, 0)
 
+    for copy in copies[2:]:
+        copy.wait()
+    moves = []
     column = lane_ids((rows, lanes))
     inner = pl.ds(HALO, rows)
     for level in range(levels):
@@ -341,10 +344,13 @@
             jnp.where(column >= lanes - STEPS, turn(edges, half + COLS - move), grid[level, inner, :]),
         )
         result = norm[level] * result
-        out[level] = result
-        turned[pl.ds(level, rows, stride=PAD), :] = result
+        norm[level] = result
+        move = pltpu.make_async_copy(norm.at[level], out.at[level], out_sems.at[level])
+        move.start()
+        moves.append(move)
+        turned[pl.ds(level, rows, stride=DEEP), :] = result
     for level in range(levels, PAD):
-        turned[pl.ds(level, rows, stride=PAD), :] = jnp.zeros((rows, lanes), jnp.float32)
+        turned[pl.ds(level, rows, stride=DEEP), :] = jnp.zeros((rows, lanes), jnp.float32)
 
     even = lane_ids((PAD, lanes)) % 2 == 0
     per_row = lanes // PAD
@@ -357,9 +363,9 @@
                 found = list(found)
                 for u in range(UNROLL):
                     spot = group * UNROLL + u
-                    start = pl.multiple_of(cells[block, 5, spot], PAD)
+                    start = pl.multiple_of(cells[block, 5, spot], 8)
                     low = turned[pl.ds(start, PAD), :].reshape(PAD // 8, 8, lanes)
-                    high = turned[pl.ds(start + PAD, PAD), :].reshape(PAD // 8, 8, lanes)
+                    high = turned[pl.ds(start + DEEP, PAD), :].reshape(PAD // 8, 8, lanes)
                     mixed = low * row_of(lower, block * lanes + spot) + high * row_of(
                         upper, block * lanes + spot
                     )
@@ -376,6 +382,8 @@
         return carry
 
     lax.fori_loop(0, sampled.shape[0] // lanes, sample_tile, 0)
+    for move in moves:
+        move.wait()
 
 
 def row_of(table, number):
@@ -388,22 +396,29 @@
     whole = pl.BlockSpec(memory_space=pltpu.VMEM)
     scalars = pl.BlockSpec(memory_space=pltpu.SMEM)
     planes = levels + (levels + 1) // 2
+    anywhere = pl.BlockSpec(memory_space=pl.ANY)
     return pl.pallas_call(
         functools.partial(diffuse_kernel, n_lat),
         out_shape=(
             jax.ShapeDtypeStruct(field.shape, jnp.float32),
             jax.ShapeDtypeStruct((cells.shape[0] * PAD, lanes), jnp.float32),
         ),
-        in_specs=[whole] * 9 + [scalars],
-        out_specs=(whole, whole),
+        in_specs=[anywhere] * 5 + [whole] * 4 + [scalars],
+        out_specs=(anywhere, whole),
         scratch_shapes=[
             pltpu.VMEM((planes, tall, lanes), jnp.float32),
             pltpu.VMEM((planes, tall, lanes), jnp.float32),
-            pltpu.VMEM((rows * PAD, lanes), jnp.float32),
+            pltpu.VMEM((rows * DEEP, lanes), jnp.float32),
             pltpu.VMEM((lanes, lanes), jnp.float32),
+            pltpu.VMEM(norm.shape, jnp.float32),
+            pltpu.VMEM(weights.shape, jnp.float32),
+            pltpu.VMEM(lower.shape, jnp.float32),
+            pltpu.VMEM(upper.shape, jnp.float32),
+            pltpu.SemaphoreType.DMA((5,)),
+            pltpu.SemaphoreType.DMA((levels,)),
         ],
-        compiler_params=pltpu.CompilerParams(vmem_limit_bytes=24 << 20),
-    )(field, norm, *halos, weights, lower, upper, cells)
+        compiler_params=pltpu.CompilerParams(vmem_limit_bytes=BIG),
+    )(field, norm, weights, lower, upper, *halos, cells)
 
 
 def one_hot_slots(slots, q, rows):
@@ -467,7 +482,7 @@
         in_specs=[whole] * 6,
         out_specs=(whole, whole),
         scratch_shapes=[pltpu.VMEM((LANES, count), jnp.float32)],
-        compiler_params=pltpu.CompilerParams(vmem_limit_bytes=16 << 20),
+        compiler_params=pltpu.CompilerParams(vmem_limit_bytes=BIG),
     )(innovations, weights, place, owners, owners.reshape(1, count), ids)
 
 
@@ -558,6 +573,7 @@
 def post(packet, n_lat, n_lon, collective_id, coef=None, tiles=None):
     whole = pl.BlockSpec(memory_space=pltpu.VMEM)
     anywhere = pl.BlockSpec(memory_space=pl.ANY)
+    outside = pl.BlockSpec(memory_space=pltpu.HBM)
     blocks = packet.reshape(n_lat, n_lon, -1, LANES)
     has_coef = coef is not None
     sems = n_lon + n_lat + 8 * has_coef
@@ -568,7 +584,7 @@
         pltpu.SemaphoreType.DMA((sems,)),
         pltpu.SemaphoreType.DMA,
     ]
-    operands, in_specs, out_specs = [blocks], [whole], [whole]
+    operands, in_specs, out_specs = [blocks], [whole], [outside if has_coef else whole]
     if has_coef:
         count, rows, lanes = coef.shape
         levels, slots, depth, _ = tiles.shape
@@ -583,7 +599,7 @@
         ]
         operands += [coef, tiles]
         in_specs += [whole, anywhere]
-        out_specs += [whole] * 4 + [anywhere]
+        out_specs += [outside] * 5
     received, *rest = pl.pallas_call(
         functools.partial(post_kernel, has_coef),
         out_shape=out_shape,
@@ -591,14 +607,26 @@
         out_specs=out_specs,
         scratch_shapes=scratch,
         compiler_params=pltpu.CompilerParams(
-            collective_id=collective_id, has_side_effects=True, vmem_limit_bytes=4 << 20
+            collective_id=collective_id, has_side_effects=True, vmem_limit_bytes=BIG if has_coef else 4 << 20
         ),
     )(*operands)
     return (received.reshape(packet.shape), *rest)
 
 
 def spread_kernel(
-    levels, packet, seen, lower, upper, cells_out, turned, observed, other, cells, sem
+    levels,
+    packet,
+    seen_out,
+    lower_out,
+    upper_out,
+    cells_out,
+    seen,
+    lower,
+    upper,
+    turned,
+    cells,
+    sem,
+    *parts,
 ):
     total, lanes = packet.shape
     per_row = lanes // PAD
@@ -610,9 +638,9 @@
         turned[pl.ds(tile * lanes, lanes), :] = flipped
         for q in range(per_row):
             last = flipped[PAD * q + level_lane : PAD * (q + 1)].astype(jnp.int32)
-            last = jnp.where(sublane == 5, last * PAD, jnp.where(sublane == 6, lanes - last, last))
+            last = jnp.where(sublane == 5, last * DEEP, jnp.where(sublane == 6, lanes - last, last))
             cells_out[tile * per_row + q] = last
-    copy = pltpu.make_async_copy(cells_out, cells, sem)
+    copy = pltpu.make_async_copy(cells_out, cells, sem.at[0])
     copy.start()
 
     lane = lane_ids((lanes, lanes)).astype(jnp.float32)
@@ -630,7 +658,12 @@
             upper[block, :] = jnp.where(here, third, jnp.where(beside, fourth, 0.0))
 
     is_level = lax.broadcasted_iota(jnp.int32, (PAD, lanes), 0) < levels
-    parts = (observed, other)
+    tables = (
+        pltpu.make_async_copy(lower, lower_out, sem.at[1]),
+        pltpu.make_async_copy(upper, upper_out, sem.at[2]),
+    )
+    for table in tables:
+        table.start()
     for part in parts:
         part[...] = jnp.zeros_like(part)
     copy.wait()
@@ -645,16 +678,11 @@
                 value = jnp.broadcast_to(moved[:, u : u + 1], (PAD, lanes)).reshape(
                     PAD // 8, 8, lanes
                 )
-                added = jnp.concatenate(
-                    [
-                        (value * row_of(table, block * lanes + spot)).reshape(PAD, lanes)
-                        for table in (lower, upper)
-                    ],
-                    axis=0,
-                )
-                where = pl.ds(pl.multiple_of(cells[block, 5, spot], PAD), 2 * PAD)
                 part = parts[u % len(parts)]
-                part[where, :] = part[where, :] + added
+                for table, offset in ((lower, 0), (upper, DEEP)):
+                    start = pl.multiple_of(cells[block, 5, spot] + offset, 8)
+                    added = (value * row_of(table, block * lanes + spot)).reshape(PAD, lanes)
+                    part[pl.ds(start, PAD), :] = part[pl.ds(start, PAD), :] + added
             return carry
 
         lax.fori_loop(0, lanes // UNROLL, spread_group, 0)
@@ -662,15 +690,25 @@
 
     lax.fori_loop(0, tiles * per_row, spread_block, 0)
     rows = seen.shape[1]
+    moves = list(tables)
     for level in range(levels):
-        at = pl.ds(level, rows, stride=PAD)
-        seen[level] = observed[at, :] + other[at, :]
+        at = pl.ds(level, rows, stride=DEEP)
+        total = parts[0][at, :]
+        for part in parts[1:]:
+            total = total + part[at, :]
+        seen[level] = total
+        move = pltpu.make_async_copy(seen.at[level], seen_out.at[level], sem.at[3 + level])
+        move.start()
+        moves.append(move)
+    for move in moves:
+        move.wait()
 
 
 def spread(packet, levels, rows):
     total, lanes = packet.shape
     whole = pl.BlockSpec(memory_space=pltpu.VMEM)
     blocks = total // PAD
+    outside = pl.BlockSpec(memory_space=pltpu.HBM)
     masks = jax.ShapeDtypeStruct((blocks * lanes, lanes), jnp.float32)
     return pl.pallas_call(
         functools.partial(spread_kernel, levels),
@@ -681,45 +719,114 @@
             jax.ShapeDtypeStruct((blocks, 8, lanes), jnp.int32),
         ),
         in_specs=[whole],
-        out_specs=(whole,) * 4,
+        out_specs=(outside,) * 3 + (whole,),
         scratch_shapes=[
+            pltpu.VMEM((levels, rows, lanes), jnp.float32),
+            pltpu.VMEM(masks.shape, jnp.float32),
+            pltpu.VMEM(masks.shape, jnp.float32),
             pltpu.VMEM(packet.shape, jnp.float32),
-            pltpu.VMEM((rows * PAD, lanes), jnp.float32),
-            pltpu.VMEM((rows * PAD, lanes), jnp.float32),
             pltpu.SMEM((blocks, 8, lanes), jnp.int32),
-            pltpu.SemaphoreType.DMA,
-        ],
-        compiler_params=pltpu.CompilerParams(vmem_limit_bytes=12 << 20),
+            pltpu.SemaphoreType.DMA((3 + levels,)),
+        ]
+        + [pltpu.VMEM((rows * DEEP, lanes), jnp.float32)] * PARTS,
+        compiler_params=pltpu.CompilerParams(vmem_limit_bytes=BIG),
     )(packet)
 
 
-def combine_kernel(cells, seen, early, late, norm, field):
+def combine_kernel(
+    cells,
+    seen,
+    early,
+    late,
+    norm,
+    field_out,
+    packs_out,
+    field,
+    packs,
+    seen_in,
+    tiles_in,
+    norm_in,
+    sems,
+    out_sems,
+):
     slots, _, depth, lanes = early.shape
+    levels = norm.shape[0]
     n_lon = lax.axis_size("lon")
     per_device = slots // n_lon
     per_row = lanes // PAD
     row_group = CAPACITY * PAD // lanes
     base = lax.axis_index("lat") * n_lon
-
-    def one_tile(slot, carry):
-        at = (base + slot // per_device) * row_group
-        block = (at // lanes) * per_row + lax.rem(slot, per_device)
-        rows = pl.ds(pl.multiple_of(cells[block, 7, lax.rem(at, lanes)] * depth, depth), depth)
-        for part, tiles in ((pl.ds(0, early.shape[1]), early), (pl.ds(early.shape[1], late.shape[1]), late)):
-            field[part, rows, :] = norm[part, rows, :] * (seen[part, rows, :] + tiles[slot])
-        return carry
-
-    lax.fori_loop(0, slots, one_tile, 0)
+    batches = []
+    for number, start in enumerate(range(0, levels, BATCH)):
+        part = pl.ds(start, BATCH)
+        tiles = early.at[:, part] if start < EARLY else late.at[:, pl.ds(start - EARLY, BATCH)]
+        copies = (
+            pltpu.make_async_copy(seen.at[part], seen_in.at[part], sems.at[number, 0]),
+            pltpu.make_async_copy(tiles, tiles_in.at[:, part], sems.at[number, 1]),
+            pltpu.make_async_copy(norm.at[part], norm_in.at[part], sems.at[number, 2]),
+        )
+        for copy in copies:
+            copy.start()
+        batches.append((part, copies))
+
+    moves = []
+
+    def send_out(here, there):
+        move = pltpu.make_async_copy(here, there, out_sems.at[len(moves)])
+        move.start()
+        moves.append(move)
+
+    for part, copies in batches:
+        for copy in copies:
+            copy.wait()
+
+        def one_tile(slot, carry):
+            at = (base + slot // per_device) * row_group
+            block = (at // lanes) * per_row + lax.rem(slot, per_device)
+            rows = pl.ds(pl.multiple_of(cells[block, 7, lax.rem(at, lanes)] * depth, depth), depth)
+            field[part, rows, :] = norm_in[part, rows, :] * (
+                seen_in[part, rows, :] + tiles_in[slot, part]
+            )
+            return carry
+
+        lax.fori_loop(0, slots, one_tile, 0, unroll=4)
+        send_out(field.at[part], field_out.at[part])
+
+    rows = field.shape[1]
+    tiles = packs.shape[0] // 2 - 1
+    for level in range(levels):
+        at = pl.ds(STEPS * level, STEPS)
+        packs[2 * tiles, at, :] = field[level, pl.ds(0, STEPS), :]
+        packs[2 * tiles + 1, at, :] = field[level, pl.ds(rows - STEPS, STEPS), :]
+    for tile in range(tiles):
+        packs[tile], packs[tiles + tile] = packed_columns(
+            lambda plane: field[plane], levels, rows, STEPS, tile * PAIRS, PAIRS
+        )
+    send_out(packs, packs_out)
+    for move in moves:
+        move.wait()
 
 
 def combine(cells, seen, early, late, norm):
-    whole = pl.BlockSpec(memory_space=pltpu.VMEM)
+    anywhere = pl.BlockSpec(memory_space=pl.ANY)
+    levels, rows, lanes = norm.shape
+    tiles = (early.shape[0], levels) + early.shape[2:]
+    packs = -(-((levels + 1) // 2) // PAIRS)
+    outs = [norm.shape, (2 * packs + 2, rows, lanes)]
     return pl.pallas_call(
         combine_kernel,
-        out_shape=jax.ShapeDtypeStruct(norm.shape, jnp.float32),
-        in_specs=[pl.BlockSpec(memory_space=pltpu.SMEM)] + [whole] * 4,
-        out_specs=whole,
-        compiler_params=pltpu.CompilerParams(vmem_limit_bytes=8 << 20),
+        out_shape=[jax.ShapeDtypeStruct(shape, jnp.float32) for shape in outs],
+        in_specs=[pl.BlockSpec(memory_space=pltpu.SMEM)] + [anywhere] * 4,
+        out_specs=[anywhere] * 2,
+        scratch_shapes=[pltpu.VMEM(shape, jnp.float32) for shape in outs]
+        + [
+            pltpu.VMEM(seen.shape, jnp.float32),
+            pltpu.VMEM(tiles, jnp.float32),
+            pltpu.VMEM(norm.shape, jnp.float32),
+            pltpu.SemaphoreType.DMA((levels // BATCH, 3)),
+            pltpu.SemaphoreType.DMA((levels // BATCH + 1,)),
+        ],
+        compiler_params=pltpu.CompilerParams(vmem_limit_bytes=59 << 20),
     )(cells, seen, early, late, norm)
 
 
@@ -746,7 +853,7 @@
         out_shape=jax.ShapeDtypeStruct((levels, slots.shape[1]), jnp.float32),
         in_specs=[whole] * 2,
         out_specs=whole,
-        compiler_params=pltpu.CompilerParams(vmem_limit_bytes=16 << 20),
+        compiler_params=pltpu.CompilerParams(vmem_limit_bytes=8 << 20),
     )(returned, slots)
 
 
@@ -777,8 +884,8 @@
     late = lax.all_to_all(late, "lon", split_axis=0, concat_axis=0, tiled=True)
     seen, lower, upper, cells = spread(packet, levels, rows)
     weights = prepare(coef, coef_halos, n_lat)
-    field = combine(cells, seen, early, late, norm_factor)
-    halos = exchange(field, n_lat, n_lon)
+    field, packs = combine(cells, seen, early, late, norm_factor)
+    halos = exchange(packs, n_lat, n_lon)
     smoothed, sampled = diffuse(field, norm_factor, halos, weights, lower, upper, cells, n_lat)
     (returned,) = post(sampled, n_lat, n_lon, 2)
     profile_values = collect(returned, slots, levels)

time: 171 us -> 214 us (1.25)
  Pallas kernels: 134 us -> 182 us
  local copies, waits for them, and re-layouts: 17 us -> 6.7 us
  waiting for transfers between devices: 0.01 us -> 6.15 us
    pallas_call x2, Pallas kernels: 35.9 us -> 77.9 us  [post(): pl.pallas_call(functools.partial(post_kernel, has_coef), out_shape=out_sh...]
    unnamed x45 -> x23, local copies, waits for them, and re-layouts: 14.5 us -> 4.24 us
    all_to_all x1, waiting for transfers between devices: 0.01 us -> 6.15 us  [on_device(): late = lax.all_to_all(late, 'lon', split_axis=0, concat_axis=0, tiled=True)]
    pallas_call x1, Pallas kernels: 3.82 us -> 8.39 us  [combine(): pl.pallas_call(combine_kernel, out_shape=[jax.ShapeDtypeStruct(shape, jnp...]
    pallas_call x1, Pallas kernels: 2.25 us -> 4.73 us  [prepare(): pl.pallas_call(functools.partial(prepare_kernel, n_lat), out_shape=jax.Sh...]
  transfers between devices with their start and end apart: 2 -> 2, of which waited for: 0 -> 1; matrix products, arithmetic and copies ran while one was open for 2% -> 1% of each run, Pallas kernels for 26% -> 41%
where the time goes in v6:
time: 214 us
  Pallas kernels  182 us (85%)
  starting transfers between devices  16.8 us (8%)
  local copies, waits for them, and re-layouts  6.7 us (3%)
  waiting for transfers between devices  6.15 us (3%)
    pallas_call x2, Pallas kernels, post(): pl.pallas_call(functools.partial(post_kernel, has_coef), out_shape=out_sh...  77.9 us
    pallas_call x1, Pallas kernels, diffuse(): pl.pallas_call(functools.partial(diffuse_kernel, n_lat), out_shape=(jax.S...  51.9 us
    pallas_call x1, Pallas kernels, exchange(): pl.pallas_call(functools.partial(exchange_kernel, n_lat, n_lon), out_shap...  16.5 us
    pallas_call x1, Pallas kernels, spread(): pl.pallas_call(functools.partial(spread_kernel, levels), out_shape=(jax.S...  16.2 us
    all_to_all x1, starting transfers between devices, on_device(): lax.all_to_all(jnp.transpose(model_tiles[:EARLY], (1, 0, 2, 3)), 'lon', s...  9.6 us
    pallas_call x1, Pallas kernels, combine(): pl.pallas_call(combine_kernel, out_shape=[jax.ShapeDtypeStruct(shape, jnp...  8.39 us
    all_to_all x1, starting transfers between devices, on_device(): late = lax.all_to_all(late, 'lon', split_axis=0, concat_axis=0, tiled=True)  7.23 us
    all_to_all x1, waiting for transfers between devices, on_device(): late = lax.all_to_all(late, 'lon', split_axis=0, concat_axis=0, tiled=True)  6.15 us
  transfers between devices with their start and end apart: 2, of which 1 were waited for; matrix products, arithmetic and copies ran while one was open for 1% of the time, Pallas kernels for 41%

profile of v6, /device:TPU:1, one launch (start us, length us, event | category | flops | bytes accessed | tf_op | source)
XLA Modules:
  0.0 213.6 jit_solution(14972806246835364697)
XLA Ops:
  0.6 0.0 copy-start.8
  0.6 2.5 %copy_bitcast_fusion = f32[32,10,8,128]{3,2,1,0:T(8,128)} fusion(f32[25,32,8,128]{3,2,1,0:T(8,128)} %refs_1_.1), kind=kLoop, calls=%fused_computation | loop fusion | bytes 2621440 | tf_op jit(solution)/shard_map/transpose | solution.py:878
  3.1 0.0 copy-start.9
  3.1 0.0 copy-start.10
  3.1 0.0 copy-start.4
  3.1 0.0 copy-start.5
  3.1 0.0 copy-start.6
  3.1 0.0 copy-start.7
  3.1 9.6 %all-to-all-start = ((f32[32,10,8,128]{3,2,1,0:T(8,128)}), f32[32,10,8,128]{3,2,1,0:T(8,128)S(1)}, u32[]{:S(2)}, u32[]{:S(2)}) async-start(f32[32,10,8,128]{3,2,1,0:T(8,128)} %copy_bitcast_fusion), calls=%async_computation | async-start | bytes 2621440 | tf_op jit(solution)/shard_map/all_to_all | solution.py:877
  12.7 0.0 copy-done.8
  12.8 0.9 copy.14.owner_column
  13.6 0.0 copy-done.9
  13.6 0.0 copy-done.10
  13.6 0.6 pad_add_fusion.place
  14.2 3.9 %shard_map.131 = (f32[256,128]{1,0:T(8,128)}, s32[1,512]{1,0:T(1,128)}) custom-call(f32[25,512]{1,0:T(8,128)} %innovations.1, f32[4,512]{1,0:T(4,128)} %weights.1, s32[2,512]{1,0:T(2,128)} %pad_add_fusion.place, s32[512,1]{1,0:T(8,128)} %copy.14.owner_column, s32[1,512]{1,0:T(1,128)} %bitcast.21, s32[1,32]{1,0:T(1,128)} %ids.1), custom_call_target="tpu_custom_call" | custom-call | tf_op jit(solution)/shard_map/pallas_call | solution.py:476
  18.1 0.0 copy-done.4
  18.1 0.0 copy-done.5
  18.2 0.0 copy-done.6
  18.2 0.0 copy-done.7
  18.2 0.9 pad_maximum_fusion.refs_0_.coef
  19.1 62.6 %shard_map.132 = (f32[8,16,2,128]{3,2,1,0:T(2,128)}, f32[288,128]{1,0:T(8,128)}, f32[288,128]{1,0:T(8,128)}, f32[4,16,128]{2,1,0:T(8,128)}, f32[4,16,128]{2,1,0:T(8,128)}, /*index=5*/f32[32,15,8,128]{3,2,1,0:T(8,128)}) custom-call(f32[8,16,2,128]{3,2,1,0:T(2,128)} %bitcast.16, f32[4,256,128]{2,1,0:T(8,128)} %pad_maximum_fusion.refs_0_.coef, ...), custom_call_target="tpu_custom_call" | custom-call | tf_op jit(solution)/shard_map/pallas_call | solution.py:603
  81.7 0.0 all-to-all-done.early
  81.7 0.0 copy-start.3
  81.7 1.1 copy-done.3
  82.9 7.2 %all-to-all-start.1 = ((f32[32,15,8,128]{3,2,1,0:T(8,128)}), f32[32,15,8,128]{3,2,1,0:T(8,128)S(1)}, u32[]{:S(2)}, u32[]{:S(2)}) async-start(f32[32,15,8,128]{3,2,1,0:T(8,128)} %get-tuple-element.26), calls=%async_computation.1 | async-start | bytes 3932160 | tf_op jit(solution)/shard_map/all_to_all | solution.py:884
  90.1 16.2 %shard_map.133 = (f32[25,256,128]{2,1,0:T(8,128)}, f32[1024,128]{1,0:T(8,128)}, f32[1024,128]{1,0:T(8,128)}, s32[8,8,128]{2,1,0:T(8,128)}) custom-call(f32[256,128]{1,0:T(8,128)} %bitcast.17), custom_call_target="tpu_custom_call" | custom-call | tf_op jit(solution)/shard_map/pallas_call | solution.py:713
  106.3 4.7 %shard_map.135.weights_far = f32[2,7,280,128]{3,2,1,0:T(8,128)} custom-call(f32[4,256,128]{2,1,0:T(8,128)} %pad_maximum_fusion.refs_0_.coef, f32[288,128]{1,0:T(8,128)} %get-tuple-element.28.west_cols, f32[288,128]{1,0:T(8,128)} %get-tuple-element.29.east_cols, f32[4,16,128]{2,1,0:T(8,128)} %get-tuple-element.30.south_coef, ...), custom_call_target="tpu_custom_call" | custom-call | tf_op jit(solution)/shard_map/pallas_call | solution.py:215
  111.0 6.2 %all-to-all-done.1.late = f32[32,15,8,128]{3,2,1,0:T(8,128)S(1)} async-done(((f32[32,15,8,128]{3,2,1,0:T(8,128)}), f32[32,15,8,128]{3,2,1,0:T(8,128)S(1)}, u32[]{:S(2)}, u32[]{:S(2)}) %all-to-all-start.1) | async-done | bytes 1966112 | tf_op jit(solution)/shard_map/all_to_all | solution.py:884
  117.2 0.0 copy-start.2
  117.2 1.3 copy-done.2
  118.4 8.4 %shard_map.134 = (f32[25,256,128]{2,1,0:T(8,128)}, f32[8,256,128]{2,1,0:T(8,128)}) custom-call(s32[8,8,128]{2,1,0:T(8,128)} %get-tuple-element.24.cells, f32[25,256,128]{2,1,0:T(8,128)} %get-tuple-element.25.seen, f32[32,10,8,128]{3,2,1,0:T(8,128)} %copy-done.3, f32[32,15,8,128]{3,2,1,0:T(8,128)} %copy-done.2, f32[25,256,128]{2,1,0:T(8,128)} %norm_far.1), custom_call_target="tpu_custom_call" | custom-call | tf_op jit(solution)/shard_map/pallas_call | solution.py:816
  126.9 16.5 %shard_map.136 = (f32[3,288,128]{2,1,0:T(8,128)}, f32[3,288,128]{2,1,0:T(8,128)}, f32[256,128]{1,0:T(8,128)}, f32[256,128]{1,0:T(8,128)}) custom-call(f32[8,256,128]{2,1,0:T(8,128)} %get-tuple-element.34.packs), custom_call_target="tpu_custom_call" | custom-call | tf_op jit(solution)/shard_map/pallas_call | solution.py:150
  143.3 0.0 copy-start.1
  143.3 51.9 %shard_map.137 = (f32[25,256,128]{2,1,0:T(8,128)}, f32[256,128]{1,0:T(8,128)}) custom-call(f32[25,256,128]{2,1,0:T(8,128)} %get-tuple-element.27.field, f32[25,256,128]{2,1,0:T(8,128)} %norm_far.1, f32[2,7,280,128]{3,2,1,0:T(8,128)} %shard_map.135.weights_far, f32[1024,128]{1,0:T(8,128)} %get-tuple-element.32.lower_far, ...), custom_call_target="tpu_custom_call" | custom-call | tf_op jit(solution)/shard_map/pallas_call | solution.py:400
  195.3 0.0 copy-start
  195.3 0.9 copy-done
  196.2 15.3 %shard_map.138 = f32[8,16,2,128]{3,2,1,0:T(2,128)S(1)} custom-call(f32[8,16,2,128]{3,2,1,0:T(2,128)S(1)} %bitcast.15), custom_call_target="tpu_custom_call" | custom-call | tf_op jit(solution)/shard_map/pallas_call | solution.py:603
  211.5 0.0 copy-done.1
  211.5 2.1 shard_map.139
  (1 shorter events, 0.0 us)
Async XLA Ops:
  0.6 12.1 %copy-start.8 = (s32[512,1]{0,1:T(1,128)S(1)}, s32[512,1]{0,1:T(1,128)}, u32[]{:S(2)}) copy-start(s32[512,1]{0,1:T(1,128)} %param.13) | copy-start | bytes 6148
  3.1 10.5 %copy-start.9 = (s32[512]{0:T(512)S(1)}, s32[512]{0:T(512)}, u32[]{:S(2)}) copy-start(s32[512]{0:T(512)} %param.15) | copy-start | bytes 6148
  3.1 10.5 %copy-start.10 = (s32[512]{0:T(512)S(1)}, s32[512]{0:T(512)}, u32[]{:S(2)}) copy-start(s32[512]{0:T(512)} %param.14) | copy-start | bytes 6148
  3.1 15.0 %copy-start.4 = (s32[256,128]{1,0:T(8,128)S(1)}, s32[256,128]{1,0:T(8,128)}, u32[]{:S(2)}) copy-start(s32[256,128]{1,0:T(8,128)} %param.22) | copy-start | bytes 393220
  3.1 15.0 %copy-start.5 = (f32[256,128]{1,0:T(8,128)S(1)}, f32[256,128]{1,0:T(8,128)}, u32[]{:S(2)}) copy-start(f32[256,128]{1,0:T(8,128)} %param.21) | copy-start | bytes 393220
  3.1 15.0 %copy-start.6 = (f32[256,128]{1,0:T(8,128)S(1)}, f32[256,128]{1,0:T(8,128)}, u32[]{:S(2)}) copy-start(f32[256,128]{1,0:T(8,128)} %param.20) | copy-start | bytes 393220
  3.1 15.0 %copy-start.7 = (f32[256,128]{1,0:T(8,128)S(1)}, f32[256,128]{1,0:T(8,128)}, u32[]{:S(2)}) copy-start(f32[256,128]{1,0:T(8,128)} %param.19) | copy-start | bytes 393220
  3.1 78.5 %all-to-all-start = ((f32[32,10,8,128]{3,2,1,0:T(8,128)}), f32[32,10,8,128]{3,2,1,0:T(8,128)S(1)}, u32[]{:S(2)}, u32[]{:S(2)}) async-start(f32[32,10,8,128]{3,2,1,0:T(8,128)} %copy_bitcast_fusion), calls=%async_computation | async-start | bytes 2621440 | tf_op jit(solution)/shard_map/all_to_all | solution.py:877
  81.7 1.2 copy-start.3
  82.9 34.3 %all-to-all-start.1 = ((f32[32,15,8,128]{3,2,1,0:T(8,128)}), f32[32,15,8,128]{3,2,1,0:T(8,128)S(1)}, u32[]{:S(2)}, u32[]{:S(2)}) async-start(f32[32,15,8,128]{3,2,1,0:T(8,128)} %get-tuple-element.26), calls=%async_computation.1 | async-start | bytes 3932160 | tf_op jit(solution)/shard_map/all_to_all | solution.py:884
  117.2 1.3 copy-start.2
  143.3 68.2 %copy-start.1 = (s32[1,512]{1,0:T(1,128)S(1)}, s32[1,512]{1,0:T(1,128)}, u32[]{:S(2)}) copy-start(s32[1,512]{1,0:T(1,128)} %get-tuple-element.41.slots) | copy-start | bytes 6148
  195.3 0.9 copy-start

commit v7 on v5

--- a/solution.py
+++ b/solution.py
@@ -10,7 +10,9 @@
 STEPS = 10
 CAPACITY = 8
 PAD = 32
+DEEP = 40
 UNROLL = 32
+BIG = 62 << 20
 HALO = 16
 LANES = 128
 COLS = 12
@@ -245,7 +247,7 @@
         in_specs=[whole] * 5,
         out_specs=whole,
         scratch_shapes=[pltpu.VMEM((2, count, tall, lanes), jnp.float32)],
-        compiler_params=pltpu.CompilerParams(vmem_limit_bytes=8 << 20),
+        compiler_params=pltpu.CompilerParams(vmem_limit_bytes=4 << 20),
     )(coef, *halos)
 
 
@@ -342,9 +344,9 @@
         )
         result = norm[level] * result
         out[level] = result
-        turned[pl.ds(level, rows, stride=PAD), :] = result
+        turned[pl.ds(level, rows, stride=DEEP), :] = result
     for level in range(levels, PAD):
-        turned[pl.ds(level, rows, stride=PAD), :] = jnp.zeros((rows, lanes), jnp.float32)
+        turned[pl.ds(level, rows, stride=DEEP), :] = jnp.zeros((rows, lanes), jnp.float32)
 
     even = lane_ids((PAD, lanes)) % 2 == 0
     per_row = lanes // PAD
@@ -357,9 +359,9 @@
                 found = list(found)
                 for u in range(UNROLL):
                     spot = group * UNROLL + u
-                    start = pl.multiple_of(cells[block, 5, spot], PAD)
+                    start = pl.multiple_of(cells[block, 5, spot], 8)
                     low = turned[pl.ds(start, PAD), :].reshape(PAD // 8, 8, lanes)
-                    high = turned[pl.ds(start + PAD, PAD), :].reshape(PAD // 8, 8, lanes)
+                    high = turned[pl.ds(start + DEEP, PAD), :].reshape(PAD // 8, 8, lanes)
                     mixed = low * row_of(lower, block * lanes + spot) + high * row_of(
                         upper, block * lanes + spot
                     )
@@ -399,7 +401,7 @@
         scratch_shapes=[
             pltpu.VMEM((planes, tall, lanes), jnp.float32),
             pltpu.VMEM((planes, tall, lanes), jnp.float32),
-            pltpu.VMEM((rows * PAD, lanes), jnp.float32),
+            pltpu.VMEM((rows * DEEP, lanes), jnp.float32),
             pltpu.VMEM((lanes, lanes), jnp.float32),
         ],
         compiler_params=pltpu.CompilerParams(vmem_limit_bytes=24 << 20),
@@ -467,14 +469,14 @@
         in_specs=[whole] * 6,
         out_specs=(whole, whole),
         scratch_shapes=[pltpu.VMEM((LANES, count), jnp.float32)],
-        compiler_params=pltpu.CompilerParams(vmem_limit_bytes=16 << 20),
+        compiler_params=pltpu.CompilerParams(vmem_limit_bytes=BIG),
     )(innovations, weights, place, owners, owners.reshape(1, count), ids)
 
 
 def post_kernel(has_coef, source, *refs):
     if has_coef:
         coef, tiles, target, west_cols, east_cols, south_coef, north_coef, late = refs[:8]
-        held, send_sem, recv_sem, local_sem, pack_first, pack_last, late_sem = refs[8:]
+        held, send_sem, recv_sem, local_sem, pack_first, pack_last, staged, late_sem = refs[8:]
     else:
         target, held, send_sem, recv_sem, local_sem = refs
     n_lat, n_lon = source.shape[:2]
@@ -494,12 +496,9 @@
     own.start()
     moves = []
     if has_coef:
-        for level in range(late.shape[1]):
-            move = pltpu.make_async_copy(
-                tiles.at[EARLY + level], late.at[:, level], late_sem.at[level]
-            )
-            move.start()
-            moves.append(move)
+        count = late.shape[1]
+        stage = pltpu.make_async_copy(tiles.at[pl.ds(EARLY, count)], staged, late_sem.at[count])
+        stage.start()
         rows = coef.shape[1]
         low, high = packed_columns(
             lambda plane: coef[plane], coef.shape[0], rows, COLS, 0, COEF_PAIRS
@@ -541,6 +540,12 @@
             (pack_first.at[first, :], east_cols.at[above, :], (down, left)),
         ):
             edges.append(push(here, there, n_lon + n_lat + len(edges), device))
+    if has_coef:
+        stage.wait()
+        for level in range(count):
+            move = pltpu.make_async_copy(staged.at[level], late.at[:, level], late_sem.at[level])
+            move.start()
+            moves.append(move)
     own.wait()
     for copy in copies:
         copy.wait()
@@ -558,6 +563,7 @@
 def post(packet, n_lat, n_lon, collective_id, coef=None, tiles=None):
     whole = pl.BlockSpec(memory_space=pltpu.VMEM)
     anywhere = pl.BlockSpec(memory_space=pl.ANY)
+    outside = pl.BlockSpec(memory_space=pltpu.HBM)
     blocks = packet.reshape(n_lat, n_lon, -1, LANES)
     has_coef = coef is not None
     sems = n_lon + n_lat + 8 * has_coef
@@ -568,7 +574,7 @@
         pltpu.SemaphoreType.DMA((sems,)),
         pltpu.SemaphoreType.DMA,
     ]
-    operands, in_specs, out_specs = [blocks], [whole], [whole]
+    operands, in_specs, out_specs = [blocks], [whole], [outside if has_coef else whole]
     if has_coef:
         count, rows, lanes = coef.shape
         levels, slots, depth, _ = tiles.shape
@@ -579,11 +585,12 @@
         scratch += [
             pltpu.VMEM((rows, lanes), jnp.float32),
             pltpu.VMEM((rows, lanes), jnp.float32),
-            pltpu.SemaphoreType.DMA((levels - EARLY,)),
+            pltpu.VMEM((levels - EARLY, slots, depth, lanes), jnp.float32),
+            pltpu.SemaphoreType.DMA((levels - EARLY + 1,)),
         ]
         operands += [coef, tiles]
         in_specs += [whole, anywhere]
-        out_specs += [whole] * 4 + [anywhere]
+        out_specs += [outside] * 5
     received, *rest = pl.pallas_call(
         functools.partial(post_kernel, has_coef),
         out_shape=out_shape,
@@ -591,7 +598,7 @@
         out_specs=out_specs,
         scratch_shapes=scratch,
         compiler_params=pltpu.CompilerParams(
-            collective_id=collective_id, has_side_effects=True, vmem_limit_bytes=4 << 20
+            collective_id=collective_id, has_side_effects=True, vmem_limit_bytes=BIG if has_coef else 4 << 20
         ),
     )(*operands)
     return (received.reshape(packet.shape), *rest)
@@ -610,7 +617,7 @@
         turned[pl.ds(tile * lanes, lanes), :] = flipped
         for q in range(per_row):
             last = flipped[PAD * q + level_lane : PAD * (q + 1)].astype(jnp.int32)
-            last = jnp.where(sublane == 5, last * PAD, jnp.where(sublane == 6, lanes - last, last))
+            last = jnp.where(sublane == 5, last * DEEP, jnp.where(sublane == 6, lanes - last, last))
             cells_out[tile * per_row + q] = last
     copy = pltpu.make_async_copy(cells_out, cells, sem)
     copy.start()
@@ -645,16 +652,11 @@
                 value = jnp.broadcast_to(moved[:, u : u + 1], (PAD, lanes)).reshape(
                     PAD // 8, 8, lanes
                 )
-                added = jnp.concatenate(
-                    [
-                        (value * row_of(table, block * lanes + spot)).reshape(PAD, lanes)
-                        for table in (lower, upper)
-                    ],
-                    axis=0,
-                )
-                where = pl.ds(pl.multiple_of(cells[block, 5, spot], PAD), 2 * PAD)
                 part = parts[u % len(parts)]
-                part[where, :] = part[where, :] + added
+                for table, offset in ((lower, 0), (upper, DEEP)):
+                    start = pl.multiple_of(cells[block, 5, spot] + offset, 8)
+                    added = (value * row_of(table, block * lanes + spot)).reshape(PAD, lanes)
+                    part[pl.ds(start, PAD), :] = part[pl.ds(start, PAD), :] + added
             return carry
 
         lax.fori_loop(0, lanes // UNROLL, spread_group, 0)
@@ -663,7 +665,7 @@
     lax.fori_loop(0, tiles * per_row, spread_block, 0)
     rows = seen.shape[1]
     for level in range(levels):
-        at = pl.ds(level, rows, stride=PAD)
+        at = pl.ds(level, rows, stride=DEEP)
         seen[level] = observed[at, :] + other[at, :]
 
 
@@ -684,12 +686,12 @@
         out_specs=(whole,) * 4,
         scratch_shapes=[
             pltpu.VMEM(packet.shape, jnp.float32),
-            pltpu.VMEM((rows * PAD, lanes), jnp.float32),
-            pltpu.VMEM((rows * PAD, lanes), jnp.float32),
+            pltpu.VMEM((rows * DEEP, lanes), jnp.float32),
+            pltpu.VMEM((rows * DEEP, lanes), jnp.float32),
             pltpu.SMEM((blocks, 8, lanes), jnp.int32),
             pltpu.SemaphoreType.DMA,
         ],
-        compiler_params=pltpu.CompilerParams(vmem_limit_bytes=12 << 20),
+        compiler_params=pltpu.CompilerParams(vmem_limit_bytes=20 << 20),
     )(packet)
 
 
@@ -746,7 +748,7 @@
         out_shape=jax.ShapeDtypeStruct((levels, slots.shape[1]), jnp.float32),
         in_specs=[whole] * 2,
         out_specs=whole,
-        compiler_params=pltpu.CompilerParams(vmem_limit_bytes=16 << 20),
+        compiler_params=pltpu.CompilerParams(vmem_limit_bytes=8 << 20),
     )(returned, slots)
 
 

time: 171 us -> 165 us (0.965)
  Pallas kernels: 134 us -> 127 us
  waiting for transfers between devices: 0.01 us -> 3.93 us
  local copies, waits for them, and re-layouts: 17 us -> 15.2 us
    pallas_call x1, Pallas kernels: 18.2 us -> 13.4 us  [spread(): pl.pallas_call(functools.partial(spread_kernel, levels), out_shape=(jax.S...]
    all_to_all x1, waiting for transfers between devices: 0.01 us -> 3.93 us  [on_device(): late = lax.all_to_all(late, 'lon', split_axis=0, concat_axis=0, tiled=True)]
    pallas_call x1, Pallas kernels: 53.6 us -> 50.4 us  [diffuse(): pl.pallas_call(functools.partial(diffuse_kernel, n_lat), out_shape=(jax.S...]
    unnamed x45 -> x51, local copies, waits for them, and re-layouts: 14.5 us -> 12.7 us
  transfers between devices with their start and end apart: 2 -> 2, of which waited for: 0 -> 1; matrix products, arithmetic and copies ran while one was open for 2% -> 1% of each run, Pallas kernels for 26% -> 25%
where the time goes in v7:
time: 165 us; the launch traced here: 164 us
  Pallas kernels  127 us (77%)
  starting transfers between devices  15.5 us (9%)
  local copies, waits for them, and re-layouts  15.2 us (9%)
  waiting for transfers between devices  3.93 us (2%)
    pallas_call x1, Pallas kernels, diffuse(): pl.pallas_call(functools.partial(diffuse_kernel, n_lat), out_shape=(jax.S...  50.4 us
    pallas_call x2, Pallas kernels, post(): pl.pallas_call(functools.partial(post_kernel, has_coef), out_shape=out_sh...  36.7 us
    pallas_call x1, Pallas kernels, exchange(): pl.pallas_call(functools.partial(exchange_kernel, n_lat, n_lon), out_shap...  15.4 us
    pallas_call x1, Pallas kernels, spread(): pl.pallas_call(functools.partial(spread_kernel, levels), out_shape=(jax.S...  13.4 us
    unnamed x51, local copies, waits for them, and re-layouts  12.7 us
    all_to_all x1, starting transfers between devices, on_device(): lax.all_to_all(jnp.transpose(model_tiles[:EARLY], (1, 0, 2, 3)), 'lon', s...  9.6 us
    all_to_all x1, starting transfers between devices, on_device(): late = lax.all_to_all(late, 'lon', split_axis=0, concat_axis=0, tiled=True)  5.89 us
    all_to_all x1, waiting for transfers between devices, on_device(): late = lax.all_to_all(late, 'lon', split_axis=0, concat_axis=0, tiled=True)  3.93 us
  transfers between devices with their start and end apart: 2, of which 1 were waited for; matrix products, arithmetic and copies ran while one was open for 1% of the time, Pallas kernels for 25%

profile of v7, /device:TPU:1, one launch (start us, length us, event | category | flops | bytes accessed | tf_op | source)
XLA Modules:
  0.0 164.2 jit_solution(6221428564831709768)
XLA Ops:
  0.6 0.0 copy-start.22
  0.6 2.5 %copy_bitcast_fusion = f32[32,10,8,128]{3,2,1,0:T(8,128)} fusion(f32[25,32,8,128]{3,2,1,0:T(8,128)} %refs_1_.1), kind=kLoop, calls=%fused_computation | loop fusion | bytes 2621440 | tf_op jit(solution)/shard_map/transpose | solution.py:773
  3.1 0.0 copy-start.20
  3.1 0.0 copy-start.21
  3.1 9.6 %all-to-all-start = ((f32[32,10,8,128]{3,2,1,0:T(8,128)}), f32[32,10,8,128]{3,2,1,0:T(8,128)S(1)}, u32[]{:S(2)}, u32[]{:S(2)}) async-start(f32[32,10,8,128]{3,2,1,0:T(8,128)} %copy_bitcast_fusion), calls=%async_computation | async-start | bytes 2621440 | tf_op jit(solution)/shard_map/all_to_all | solution.py:772
  12.7 0.0 copy-done.22
  12.8 0.8 copy.14.owner_column
  13.6 0.0 copy-done.23
  13.6 0.0 copy-done.24
  13.6 0.6 pad_add_fusion.place
  14.2 3.9 %shard_map.131 = (f32[256,128]{1,0:T(8,128)}, s32[1,512]{1,0:T(1,128)}) custom-call(f32[25,512]{1,0:T(8,128)} %innovations.1, f32[4,512]{1,0:T(4,128)} %weights.1, s32[2,512]{1,0:T(2,128)} %pad_add_fusion.place, s32[512,1]{1,0:T(8,128)} %copy.14.owner_column, s32[1,512]{1,0:T(1,128)} %bitcast.21, s32[1,32]{1,0:T(1,128)} %ids.1), custom_call_target="tpu_custom_call" | custom-call | tf_op jit(solution)/shard_map/pallas_call | solution.py:463
  18.1 0.0 copy-done.18
  18.1 0.0 copy-done.19
  18.2 0.0 copy-done.20
  18.2 0.0 copy-done.21
  18.2 0.8 pad_maximum_fusion.refs_0_.coef
  19.0 21.8 %shard_map.132 = (f32[8,16,2,128]{3,2,1,0:T(2,128)}, f32[288,128]{1,0:T(8,128)}, f32[288,128]{1,0:T(8,128)}, f32[4,16,128]{2,1,0:T(8,128)}, f32[4,16,128]{2,1,0:T(8,128)}, /*index=5*/f32[32,15,8,128]{3,2,1,0:T(8,128)}) custom-call(f32[8,16,2,128]{3,2,1,0:T(2,128)} %bitcast.17, f32[4,256,128]{2,1,0:T(8,128)} %pad_maximum_fusion.refs_0_.coef, ...), custom_call_target="tpu_custom_call" | custom-call | tf_op jit(solution)/shard_map/pallas_call | solution.py:594
  40.8 0.0 all-to-all-done.early
  40.8 0.0 copy-start.3
  40.8 1.0 copy-done.3
  41.9 5.9 %all-to-all-start.1 = ((f32[32,15,8,128]{3,2,1,0:T(8,128)}), f32[32,15,8,128]{3,2,1,0:T(8,128)}, u32[]{:S(2)}, u32[]{:S(2)}) async-start(f32[32,15,8,128]{3,2,1,0:T(8,128)} %get-tuple-element.24), calls=%async_computation.1 | async-start | bytes 3932160 | tf_op jit(solution)/shard_map/all_to_all | solution.py:779
  47.8 0.9 copy-done.14
  48.7 13.4 %shard_map.133 = (f32[25,256,128]{2,1,0:T(8,128)S(1)}, f32[1024,128]{1,0:T(8,128)S(1)}, f32[1024,128]{1,0:T(8,128)S(1)}, s32[8,8,128]{2,1,0:T(8,128)S(1)}) custom-call(f32[256,128]{1,0:T(8,128)S(1)} %bitcast.15), custom_call_target="tpu_custom_call" | custom-call | tf_op jit(solution)/shard_map/pallas_call | solution.py:677
  62.1 0.0 copy-start.6
  62.1 1.7 %copy-done.6 = f32[25,256,128]{2,1,0:T(8,128)} copy-done((f32[25,256,128]{2,1,0:T(8,128)}, f32[25,256,128]{2,1,0:T(8,128)S(1)}, u32[]{:S(2)}) %copy-start.6) | copy-done | bytes 3276824
  63.8 0.8 copy-done.8
  64.7 0.9 copy-done.10
  65.5 0.0 copy-done.12
  65.5 0.0 copy-done.15
  65.5 0.0 copy-done.16
  65.5 1.0 copy-done.5
  66.6 0.9 copy-done.13
  67.5 2.2 %shard_map.136.weights = f32[2,7,280,128]{3,2,1,0:T(8,128)S(1)} custom-call(f32[4,256,128]{2,1,0:T(8,128)S(1)} %copy-done.5, f32[288,128]{1,0:T(8,128)S(1)} %copy-done.12, f32[288,128]{1,0:T(8,128)S(1)} %copy-done.13, f32[4,16,128]{2,1,0:T(8,128)S(1)} %copy-done.15, f32[4,16,128]{2,1,0:T(8,128)S(1)} %copy-done.16), custom_call_target="tpu_custom_call" | custom-call | tf_op jit(solution)/shard_map/pallas_call | solution.py:244
  69.7 0.0 copy-start.1
  69.7 1.3 copy-done.1
  71.0 3.9 %all-to-all-done.1.late = f32[32,15,8,128]{3,2,1,0:T(8,128)} async-done(((f32[32,15,8,128]{3,2,1,0:T(8,128)}), f32[32,15,8,128]{3,2,1,0:T(8,128)}, u32[]{:S(2)}, u32[]{:S(2)}) %all-to-all-start.1) | async-done | bytes 1966112 | tf_op jit(solution)/shard_map/all_to_all | solution.py:779
  75.0 1.3 copy-done.4
  76.3 1.9 %copy-done.7 = f32[25,256,128]{2,1,0:T(8,128)S(1)} copy-done((f32[25,256,128]{2,1,0:T(8,128)S(1)}, f32[25,256,128]{2,1,0:T(8,128)}, u32[]{:S(2)}) %copy-start.7) | copy-done | bytes 3276824
  78.2 3.2 %shard_map.134.field = f32[25,256,128]{2,1,0:T(8,128)S(1)} custom-call(s32[8,8,128]{2,1,0:T(8,128)S(1)} %get-tuple-element.22.cells, f32[25,256,128]{2,1,0:T(8,128)S(1)} %copy-done.7, f32[32,10,8,128]{3,2,1,0:T(8,128)S(1)} %copy-done.4, f32[32,15,8,128]{3,2,1,0:T(8,128)} %all-to-all-done.1.late, f32[25,256,128]{2,1,0:T(8,128)S(1)} %copy-done), custom_call_target="tpu_custom_call" | custom-call | tf_op jit(solution)/shard_map/pallas_call | solution.py:719
  81.4 15.4 %shard_map.135 = (f32[3,288,128]{2,1,0:T(8,128)S(1)}, f32[3,288,128]{2,1,0:T(8,128)S(1)}, f32[256,128]{1,0:T(8,128)S(1)}, f32[256,128]{1,0:T(8,128)S(1)}) custom-call(f32[25,256,128]{2,1,0:T(8,128)S(1)} %shard_map.134.field), custom_call_target="tpu_custom_call" | custom-call | tf_op jit(solution)/shard_map/pallas_call | solution.py:175
  96.8 0.0 copy-done.2
  96.9 0.0 copy-done.9
  96.9 0.0 copy-done.11
  96.9 0.0 copy-start.17
  96.9 50.4 %shard_map.137 = (f32[25,256,128]{2,1,0:T(8,128)}, f32[256,128]{1,0:T(8,128)S(1)}) custom-call(f32[25,256,128]{2,1,0:T(8,128)S(1)} %shard_map.134.field, f32[25,256,128]{2,1,0:T(8,128)S(1)} %copy-done, f32[3,288,128]{2,1,0:T(8,128)S(1)} %get-tuple-element.25.west_cols, f32[3,288,128]{2,1,0:T(8,128)S(1)} %get-tuple-element.26.east_cols, ...), custom_call_target="tpu_custom_call" | custom-call | tf_op jit(solution)/shard_map/pallas_call | solution.py:393
  147.3 14.9 %shard_map.138 = f32[8,16,2,128]{3,2,1,0:T(2,128)S(1)} custom-call(f32[8,16,2,128]{3,2,1,0:T(2,128)S(1)} %bitcast.16), custom_call_target="tpu_custom_call" | custom-call | tf_op jit(solution)/shard_map/pallas_call | solution.py:594
  162.2 0.0 copy-done.17
  162.2 2.1 %shard_map.139 = f32[25,512]{1,0:T(8,128)} custom-call(f32[256,128]{1,0:T(8,128)S(1)} %bitcast.14, s32[1,512]{1,0:T(1,128)S(1)} %copy-done.17), custom_call_target="tpu_custom_call" | custom-call | tf_op jit(solution)/shard_map/pallas_call | solution.py:746
  (20 shorter events, 0.0 us)
Async XLA Ops:
  0.6 12.1 %copy-start.22 = (s32[512,1]{0,1:T(1,128)S(1)}, s32[512,1]{0,1:T(1,128)}, u32[]{:S(2)}) copy-start(s32[512,1]{0,1:T(1,128)} %param.13) | copy-start | bytes 6148
  3.1 10.5 %copy-start.23 = (s32[512]{0:T(512)S(1)}, s32[512]{0:T(512)}, u32[]{:S(2)}) copy-start(s32[512]{0:T(512)} %param.15) | copy-start | bytes 6148
  3.1 10.5 %copy-start.24 = (s32[512]{0:T(512)S(1)}, s32[512]{0:T(512)}, u32[]{:S(2)}) copy-start(s32[512]{0:T(512)} %param.14) | copy-start | bytes 6148
  3.1 15.0 %copy-start.18 = (s32[256,128]{1,0:T(8,128)S(1)}, s32[256,128]{1,0:T(8,128)}, u32[]{:S(2)}) copy-start(s32[256,128]{1,0:T(8,128)} %param.22) | copy-start | bytes 393220
  3.1 15.0 %copy-start.19 = (f32[256,128]{1,0:T(8,128)S(1)}, f32[256,128]{1,0:T(8,128)}, u32[]{:S(2)}) copy-start(f32[256,128]{1,0:T(8,128)} %param.21) | copy-start | bytes 393220
  3.1 15.0 %copy-start.20 = (f32[256,128]{1,0:T(8,128)S(1)}, f32[256,128]{1,0:T(8,128)}, u32[]{:S(2)}) copy-start(f32[256,128]{1,0:T(8,128)} %param.20) | copy-start | bytes 393220
  3.1 15.0 %copy-start.21 = (f32[256,128]{1,0:T(8,128)S(1)}, f32[256,128]{1,0:T(8,128)}, u32[]{:S(2)}) copy-start(f32[256,128]{1,0:T(8,128)} %param.19) | copy-start | bytes 393220
  3.1 37.7 %all-to-all-start = ((f32[32,10,8,128]{3,2,1,0:T(8,128)}), f32[32,10,8,128]{3,2,1,0:T(8,128)S(1)}, u32[]{:S(2)}, u32[]{:S(2)}) async-start(f32[32,10,8,128]{3,2,1,0:T(8,128)} %copy_bitcast_fusion), calls=%async_computation | async-start | bytes 2621440 | tf_op jit(solution)/shard_map/all_to_all | solution.py:772
  40.8 1.1 copy-start.3
  41.9 23.6 %copy-start.12 = (f32[288,128]{1,0:T(8,128)S(1)}, f32[288,128]{1,0:T(8,128)}, u32[]{:S(2)}) copy-start(f32[288,128]{1,0:T(8,128)} %get-tuple-element.29.west_cols) | copy-start | bytes 442372
  41.9 23.6 %copy-start.15 = (f32[4,16,128]{2,1,0:T(8,128)S(1)}, f32[4,16,128]{2,1,0:T(8,128)}, u32[]{:S(2)}) copy-start(f32[4,16,128]{2,1,0:T(8,128)} %get-tuple-element.31.south_coef) | copy-start | bytes 98308
  41.9 23.6 %copy-start.16 = (f32[4,16,128]{2,1,0:T(8,128)S(1)}, f32[4,16,128]{2,1,0:T(8,128)}, u32[]{:S(2)}) copy-start(f32[4,16,128]{2,1,0:T(8,128)} %get-tuple-element.32.north_coef) | copy-start | bytes 98308
  41.9 33.1 %copy-start = (f32[25,256,128]{2,1,0:T(8,128)S(1)}, f32[25,256,128]{2,1,0:T(8,128)}, u32[]{:S(2)}) copy-start(f32[25,256,128]{2,1,0:T(8,128)} %norm.3) | copy-start | bytes 9830404
  41.9 33.1 %all-to-all-start.1 = ((f32[32,15,8,128]{3,2,1,0:T(8,128)}), f32[32,15,8,128]{3,2,1,0:T(8,128)}, u32[]{:S(2)}, u32[]{:S(2)}) async-start(f32[32,15,8,128]{3,2,1,0:T(8,128)} %get-tuple-element.24), calls=%async_computation.1 | async-start | bytes 3932160 | tf_op jit(solution)/shard_map/all_to_all | solution.py:779
  47.8 0.9 copy-start.14
  62.1 1.7 %copy-start.6 = (f32[25,256,128]{2,1,0:T(8,128)}, f32[25,256,128]{2,1,0:T(8,128)S(1)}, u32[]{:S(2)}) copy-start(f32[25,256,128]{2,1,0:T(8,128)S(1)} %get-tuple-element.23.seen) | copy-start | bytes 9830404
  63.8 0.8 copy-start.8
  64.7 0.9 copy-start.10
  65.5 1.0 copy-start.5
  66.6 0.9 copy-start.13
  69.7 1.3 copy-start.1
  75.0 1.3 copy-start.4
  76.3 1.9 %copy-start.7 = (f32[25,256,128]{2,1,0:T(8,128)S(1)}, f32[25,256,128]{2,1,0:T(8,128)}, u32[]{:S(2)}) copy-start(f32[25,256,128]{2,1,0:T(8,128)} %copy-done.6) | copy-start | bytes 9830404
  81.4 15.4 %copy-start.2 = (f32[2,7,280,128]{3,2,1,0:T(8,128)S(1)}, f32[2,7,280,128]{3,2,1,0:T(8,128)}, u32[]{:S(2)}) copy-start(f32[2,7,280,128]{3,2,1,0:T(8,128)} %copy-done.1) | copy-start | bytes 6021124
  81.4 15.4 %copy-start.9 = (f32[1024,128]{1,0:T(8,128)S(1)}, f32[1024,128]{1,0:T(8,128)}, u32[]{:S(2)}) copy-start(f32[1024,128]{1,0:T(8,128)} %copy-done.8) | copy-start | bytes 1572868
  81.4 15.4 %copy-start.11 = (f32[1024,128]{1,0:T(8,128)S(1)}, f32[1024,128]{1,0:T(8,128)}, u32[]{:S(2)}) copy-start(f32[1024,128]{1,0:T(8,128)} %copy-done.10) | copy-start | bytes 1572868
  96.9 65.3 %copy-start.17 = (s32[1,512]{1,0:T(1,128)S(1)}, s32[1,512]{1,0:T(1,128)}, u32[]{:S(2)}) copy-start(s32[1,512]{1,0:T(1,128)} %get-tuple-element.37.slots) | copy-start | bytes 6148

commit v8 on v7

--- a/solution.py
+++ b/solution.py
@@ -19,6 +19,7 @@
 PAIRS = 6
 COEF_PAIRS = 5
 EARLY = 10
+MIDDLE = 5
 CHUNK = 40
 EDGE = 4
 MESH = pl.DeviceIdType.MESH
@@ -191,7 +192,7 @@
     )(field)
 
 
-def prepare_kernel(
+def step_coefficients(
     n_lat, coef, west_cols, east_cols, south_coef, north_coef, weights, raw
 ):
     rows, lanes = coef.shape[1:]
@@ -235,20 +236,6 @@
         return carry
 
     lax.fori_loop(0, (tall - 2 * EDGE) // CHUNK, make_weights, 0)
-
-
-def prepare(coef, halos, n_lat):
-    count, rows, lanes = coef.shape
-    tall = rows + 2 * HALO
-    whole = pl.BlockSpec(memory_space=pltpu.VMEM)
-    return pl.pallas_call(
-        functools.partial(prepare_kernel, n_lat),
-        out_shape=jax.ShapeDtypeStruct((2, 7, tall - 2 * EDGE, lanes), jnp.float32),
-        in_specs=[whole] * 5,
-        out_specs=whole,
-        scratch_shapes=[pltpu.VMEM((2, count, tall, lanes), jnp.float32)],
-        compiler_params=pltpu.CompilerParams(vmem_limit_bytes=4 << 20),
-    )(coef, *halos)
 
 
 def diffuse_kernel(
@@ -475,8 +462,9 @@
 
 def post_kernel(has_coef, source, *refs):
     if has_coef:
-        coef, tiles, target, west_cols, east_cols, south_coef, north_coef, late = refs[:8]
-        held, send_sem, recv_sem, local_sem, pack_first, pack_last, staged, late_sem = refs[8:]
+        coef, tiles, target, weights_out, middle, late = refs[:6]
+        held, send_sem, recv_sem, local_sem, pack_first, pack_last, staged, late_sem = refs[6:14]
+        west_cols, east_cols, south_coef, north_coef, weights, raw = refs[14:]
     else:
         target, held, send_sem, recv_sem, local_sem = refs
     n_lat, n_lon = source.shape[:2]
@@ -497,7 +485,9 @@
     moves = []
     if has_coef:
         count = late.shape[1]
-        stage = pltpu.make_async_copy(tiles.at[pl.ds(EARLY, count)], staged, late_sem.at[count])
+        stage = pltpu.make_async_copy(
+            tiles.at[pl.ds(EARLY, MIDDLE + count)], staged, late_sem.at[count]
+        )
         stage.start()
         rows = coef.shape[1]
         low, high = packed_columns(
@@ -527,13 +517,13 @@
     if has_coef:
         first = pl.ds(0, HALO)
         last = pl.ds(rows - HALO, HALO)
-        middle = pl.ds(HALO, rows)
+        within_rows = pl.ds(HALO, rows)
         above = pl.ds(HALO + rows, HALO)
         for here, there, device in (
             (coef.at[:, last, :], south_coef, (up, lon)),
             (coef.at[:, first, :], north_coef, (down, lon)),
-            (pack_last, west_cols.at[middle, :], (lat, right)),
-            (pack_first, east_cols.at[middle, :], (lat, left)),
+            (pack_last, west_cols.at[within_rows, :], (lat, right)),
+            (pack_first, east_cols.at[within_rows, :], (lat, left)),
             (pack_last.at[last, :], west_cols.at[first, :], (up, right)),
             (pack_first.at[last, :], east_cols.at[first, :], (up, left)),
             (pack_last.at[first, :], west_cols.at[above, :], (down, right)),
@@ -543,7 +533,9 @@
     if has_coef:
         stage.wait()
         for level in range(count):
-            move = pltpu.make_async_copy(staged.at[level], late.at[:, level], late_sem.at[level])
+            move = pltpu.make_async_copy(
+                staged.at[MIDDLE + level], late.at[:, level], late_sem.at[level]
+            )
             move.start()
             moves.append(move)
     own.wait()
@@ -555,8 +547,33 @@
     ]
     own = pltpu.make_async_copy(held.at[lat], target.at[lat], local_sem)
     own.start()
+    if has_coef:
+        per_device = middle.shape[2]
+        levels = pl.ds(0, MIDDLE)
+        mine = pltpu.make_async_copy(
+            staged.at[levels, pl.ds(per_device * lon, per_device)],
+            middle.at[lon],
+            late_sem.at[count + 1],
+        )
+        mine.start()
+        moves.append(mine)
+        for number, other in enumerate(across):
+            copies.append(
+                push(
+                    staged.at[levels, pl.ds(per_device * other, per_device)],
+                    middle.at[lon],
+                    n_lon + n_lat + 8 + number,
+                    (lat, other),
+                )
+            )
+        for copy in edges:
+            copy.wait()
+        step_coefficients(n_lat, coef, west_cols, east_cols, south_coef, north_coef, weights, raw)
+        move = pltpu.make_async_copy(weights, weights_out, late_sem.at[count + 2])
+        move.start()
+        moves.append(move)
     own.wait()
-    for copy in copies + edges + moves:
+    for copy in copies + moves:
         copy.wait()
 
 
@@ -566,7 +583,7 @@
     outside = pl.BlockSpec(memory_space=pltpu.HBM)
     blocks = packet.reshape(n_lat, n_lon, -1, LANES)
     has_coef = coef is not None
-    sems = n_lon + n_lat + 8 * has_coef
+    sems = n_lon + n_lat + (8 + n_lon) * has_coef
     out_shape = [jax.ShapeDtypeStruct(blocks.shape, jnp.float32)]
     scratch = [
         pltpu.VMEM(blocks.shape, jnp.float32),
@@ -578,19 +595,32 @@
     if has_coef:
         count, rows, lanes = coef.shape
         levels, slots, depth, _ = tiles.shape
-        packed = jax.ShapeDtypeStruct((rows + 2 * HALO, lanes), jnp.float32)
-        edge = jax.ShapeDtypeStruct((count, HALO, lanes), jnp.float32)
-        late = jax.ShapeDtypeStruct((slots, levels - EARLY, depth, lanes), jnp.float32)
-        out_shape += [packed, packed, edge, edge, late]
+        tall = rows + 2 * HALO
+        table = (2, 7, tall - 2 * EDGE, lanes)
+        later = levels - EARLY - MIDDLE
+        out_shape += [
+            jax.ShapeDtypeStruct(shape, jnp.float32)
+            for shape in (
+                table,
+                (n_lon, MIDDLE, slots // n_lon, depth, lanes),
+                (slots, later, depth, lanes),
+            )
+        ]
         scratch += [
             pltpu.VMEM((rows, lanes), jnp.float32),
             pltpu.VMEM((rows, lanes), jnp.float32),
-            pltpu.VMEM((levels - EARLY, slots, depth, lanes), jnp.float32),
-            pltpu.SemaphoreType.DMA((levels - EARLY + 1,)),
+            pltpu.VMEM((MIDDLE + later, slots, depth, lanes), jnp.float32),
+            pltpu.SemaphoreType.DMA((later + 3,)),
+            pltpu.VMEM((tall, lanes), jnp.float32),
+            pltpu.VMEM((tall, lanes), jnp.float32),
+            pltpu.VMEM((count, HALO, lanes), jnp.float32),
+            pltpu.VMEM((count, HALO, lanes), jnp.float32),
+            pltpu.VMEM(table, jnp.float32),
+            pltpu.VMEM((2, count, tall, lanes), jnp.float32),
         ]
         operands += [coef, tiles]
         in_specs += [whole, anywhere]
-        out_specs += [outside] * 5
+        out_specs += [outside] * 3
     received, *rest = pl.pallas_call(
         functools.partial(post_kernel, has_coef),
         out_shape=out_shape,
@@ -695,7 +725,7 @@
     )(packet)
 
 
-def combine_kernel(cells, seen, early, late, norm, field):
+def combine_kernel(cells, seen, early, middle, late, norm, field):
     slots, _, depth, lanes = early.shape
     n_lon = lax.axis_size("lon")
     per_device = slots // n_lon
@@ -707,22 +737,29 @@
         at = (base + slot // per_device) * row_group
         block = (at // lanes) * per_row + lax.rem(slot, per_device)
         rows = pl.ds(pl.multiple_of(cells[block, 7, lax.rem(at, lanes)] * depth, depth), depth)
-        for part, tiles in ((pl.ds(0, early.shape[1]), early), (pl.ds(early.shape[1], late.shape[1]), late)):
-            field[part, rows, :] = norm[part, rows, :] * (seen[part, rows, :] + tiles[slot])
+        start = 0
+        for tiles in (
+            early[slot],
+            middle[slot // per_device, :, lax.rem(slot, per_device)],
+            late[slot],
+        ):
+            part = pl.ds(start, tiles.shape[0])
+            start += tiles.shape[0]
+            field[part, rows, :] = norm[part, rows, :] * (seen[part, rows, :] + tiles)
         return carry
 
     lax.fori_loop(0, slots, one_tile, 0)
 
 
-def combine(cells, seen, early, late, norm):
+def combine(cells, seen, early, middle, late, norm):
     whole = pl.BlockSpec(memory_space=pltpu.VMEM)
     return pl.pallas_call(
         combine_kernel,
         out_shape=jax.ShapeDtypeStruct(norm.shape, jnp.float32),
-        in_specs=[pl.BlockSpec(memory_space=pltpu.SMEM)] + [whole] * 4,
+        in_specs=[pl.BlockSpec(memory_space=pltpu.SMEM)] + [whole] * 5,
         out_specs=whole,
         compiler_params=pltpu.CompilerParams(vmem_limit_bytes=8 << 20),
-    )(cells, seen, early, late, norm)
+    )(cells, seen, early, middle, late, norm)
 
 
 def collect_kernel(levels, returned, slots, out):
@@ -775,11 +812,10 @@
     coef = jnp.stack([face_x, face_y, cross_term, wet_mask.astype(jnp.float32)])
     place = jnp.stack([prof_row, prof_col])
     packet, slots = route(innovations, interp_weights, place, owners, model_ids, n_lat * n_lon)
-    packet, *coef_halos, late = post(packet, n_lat, n_lon, 1, coef, model_tiles)
+    packet, weights, middle, late = post(packet, n_lat, n_lon, 1, coef, model_tiles)
     late = lax.all_to_all(late, "lon", split_axis=0, concat_axis=0, tiled=True)
     seen, lower, upper, cells = spread(packet, levels, rows)
-    weights = prepare(coef, coef_halos, n_lat)
-    field = combine(cells, seen, early, late, norm_factor)
+    field = combine(cells, seen, early, middle, late, norm_factor)
     halos = exchange(field, n_lat, n_lon)
     smoothed, sampled = diffuse(field, norm_factor, halos, weights, lower, upper, cells, n_lat)
     (returned,) = post(sampled, n_lat, n_lon, 2)

time: 165 us -> 164 us (level)
  local copies, waits for them, and re-layouts: 15.2 us -> 10.5 us
  Pallas kernels: 127 us -> 130 us
  starting transfers between devices: 15.5 us -> 17.4 us
    unnamed x51 -> x39, local copies, waits for them, and re-layouts: 12.7 us -> 8.07 us
    pallas_call x2, Pallas kernels: 36.7 us -> 40.9 us  [post(): pl.pallas_call(functools.partial(post_kernel, has_coef), out_shape=out_sh...]
    pallas_call x1 -> x0, Pallas kernels: 2.24 us -> none  [prepare(): pl.pallas_call(functools.partial(prepare_kernel, n_lat), out_shape=jax.Sh...]
    all_to_all x1, starting transfers between devices: 5.89 us -> 7.78 us  [on_device(): late = lax.all_to_all(late, 'lon', split_axis=0, concat_axis=0, tiled=True)]
  transfers between devices with their start and end apart: 2 -> 2, of which waited for: 1 -> 1; matrix products, arithmetic and copies ran while one was open for 1% -> 1% of each run, Pallas kernels for 25% -> 27%
where the time goes in v8:
time: 164 us; the launch traced here: 163 us
  Pallas kernels  130 us (79%)
  starting transfers between devices  17.4 us (11%)
  local copies, waits for them, and re-layouts  10.5 us (6%)
  waiting for transfers between devices  3.29 us (2%)
    pallas_call x1, Pallas kernels, diffuse(): pl.pallas_call(functools.partial(diffuse_kernel, n_lat), out_shape=(jax.S...  50.4 us
    pallas_call x2, Pallas kernels, post(): pl.pallas_call(functools.partial(post_kernel, has_coef), out_shape=out_sh...  40.9 us
    pallas_call x1, Pallas kernels, exchange(): pl.pallas_call(functools.partial(exchange_kernel, n_lat, n_lon), out_shap...  16.3 us
    pallas_call x1, Pallas kernels, spread(): pl.pallas_call(functools.partial(spread_kernel, levels), out_shape=(jax.S...  13.4 us
    all_to_all x1, starting transfers between devices, on_device(): lax.all_to_all(jnp.transpose(model_tiles[:EARLY], (1, 0, 2, 3)), 'lon', s...  9.6 us
    unnamed x39, local copies, waits for them, and re-layouts  8.07 us
    all_to_all x1, starting transfers between devices, on_device(): late = lax.all_to_all(late, 'lon', split_axis=0, concat_axis=0, tiled=True)  7.78 us
    pallas_call x1, Pallas kernels, route(): pl.pallas_call(route_kernel, out_shape=(jax.ShapeDtypeStruct((devices * C...  3.93 us
  transfers between devices with their start and end apart: 2, of which 1 were waited for; matrix products, arithmetic and copies ran while one was open for 1% of the time, Pallas kernels for 27%

profile of v8, /device:TPU:1, one launch (start us, length us, event | category | flops | bytes accessed | tf_op | source)
XLA Modules:
  0.0 163.3 jit_solution(5472471614752514552)
XLA Ops:
  0.6 0.0 copy-start.16
  0.6 2.5 %copy_bitcast_fusion = f32[32,10,8,128]{3,2,1,0:T(8,128)} fusion(f32[25,32,8,128]{3,2,1,0:T(8,128)} %refs_1_.1), kind=kLoop, calls=%fused_computation | loop fusion | bytes 2621440 | tf_op jit(solution)/shard_map/transpose | solution.py:810
  3.1 0.0 copy-start.17
  3.1 0.0 copy-start.18
  3.1 0.0 copy-start.12
  3.1 0.0 copy-start.13
  3.1 0.0 copy-start.14
  3.1 0.0 copy-start.15
  3.1 9.6 %all-to-all-start = ((f32[32,10,8,128]{3,2,1,0:T(8,128)}), f32[32,10,8,128]{3,2,1,0:T(8,128)S(1)}, u32[]{:S(2)}, u32[]{:S(2)}) async-start(f32[32,10,8,128]{3,2,1,0:T(8,128)} %copy_bitcast_fusion), calls=%async_computation | async-start | bytes 2621440 | tf_op jit(solution)/shard_map/all_to_all | solution.py:809
  12.7 0.0 copy-done.16
  12.8 0.9 copy.14.owner_column
  13.6 0.0 copy-done.17
  13.6 0.0 copy-done.18
  13.6 0.6 pad_add_fusion.place
  14.2 3.9 %shard_map.131 = (f32[256,128]{1,0:T(8,128)}, s32[1,512]{1,0:T(1,128)}) custom-call(f32[25,512]{1,0:T(8,128)} %innovations.1, f32[4,512]{1,0:T(4,128)} %weights.1, s32[2,512]{1,0:T(2,128)} %pad_add_fusion.place, s32[512,1]{1,0:T(8,128)} %copy.14.owner_column, s32[1,512]{1,0:T(1,128)} %bitcast.21, s32[1,32]{1,0:T(1,128)} %ids.1), custom_call_target="tpu_custom_call" | custom-call | tf_op jit(solution)/shard_map/pallas_call | solution.py:450
  18.1 0.0 copy-done.12
  18.2 0.0 copy-done.13
  18.2 0.0 copy-done.14
  18.2 0.0 copy-done.15
  18.2 0.9 pad_maximum_fusion.refs_0_
  19.0 27.2 %shard_map.132 = (f32[8,16,2,128]{3,2,1,0:T(2,128)}, f32[2,7,280,128]{3,2,1,0:T(8,128)}, f32[16,5,2,8,128]{4,3,2,1,0:T(8,128)}, f32[32,10,8,128]{3,2,1,0:T(8,128)}) custom-call(f32[8,16,2,128]{3,2,1,0:T(2,128)} %bitcast.17, f32[4,256,128]{2,1,0:T(8,128)} %pad_maximum_fusion.refs_0_, f32[25,32,8,128]{3,2,1,0:T(8,128)} %refs_1_.1), custom_call_target="tpu_custom_call" | custom-call | tf_op jit(solution)/shard_map/pallas_call | solution.py:624
  46.3 0.0 copy-start.10
  46.3 0.0 copy-start.5
  46.3 0.0 all-to-all-done.early
  46.3 7.8 %all-to-all-start.1 = ((f32[32,10,8,128]{3,2,1,0:T(8,128)}), f32[32,10,8,128]{3,2,1,0:T(8,128)S(1)}, u32[]{:S(2)}, u32[]{:S(2)}) async-start(f32[32,10,8,128]{3,2,1,0:T(8,128)} %get-tuple-element.23), calls=%async_computation.1 | async-start | bytes 2621440 | tf_op jit(solution)/shard_map/all_to_all | solution.py:816
  54.1 0.0 copy-done.10
  54.1 13.4 %shard_map.133 = (f32[25,256,128]{2,1,0:T(8,128)S(1)}, f32[1024,128]{1,0:T(8,128)S(1)}, f32[1024,128]{1,0:T(8,128)S(1)}, s32[8,8,128]{2,1,0:T(8,128)S(1)}) custom-call(f32[256,128]{1,0:T(8,128)S(1)} %bitcast.15), custom_call_target="tpu_custom_call" | custom-call | tf_op jit(solution)/shard_map/pallas_call | solution.py:707
  67.5 0.0 copy-start.2
  67.6 1.7 %copy-done.2 = f32[25,256,128]{2,1,0:T(8,128)} copy-done((f32[25,256,128]{2,1,0:T(8,128)}, f32[25,256,128]{2,1,0:T(8,128)S(1)}, u32[]{:S(2)}) %copy-start.2) | copy-done | bytes 3276824
  69.3 0.0 copy-start.6
  69.3 0.8 copy-done.6
  70.1 0.8 copy-done.8
  70.9 3.3 %all-to-all-done.1.late = f32[32,10,8,128]{3,2,1,0:T(8,128)S(1)} async-done(((f32[32,10,8,128]{3,2,1,0:T(8,128)}), f32[32,10,8,128]{3,2,1,0:T(8,128)S(1)}, u32[]{:S(2)}, u32[]{:S(2)}) %all-to-all-start.1) | async-done | bytes 1310752 | tf_op jit(solution)/shard_map/all_to_all | solution.py:816
  74.2 0.0 copy-done.5
  74.2 1.9 %copy-done = f32[25,256,128]{2,1,0:T(8,128)S(1)} copy-done((f32[25,256,128]{2,1,0:T(8,128)S(1)}, f32[25,256,128]{2,1,0:T(8,128)}, u32[]{:S(2)}) %copy-start) | copy-done | bytes 3276824
  76.1 1.9 %copy-done.3 = f32[25,256,128]{2,1,0:T(8,128)S(1)} copy-done((f32[25,256,128]{2,1,0:T(8,128)S(1)}, f32[25,256,128]{2,1,0:T(8,128)}, u32[]{:S(2)}) %copy-start.3) | copy-done | bytes 3276824
  78.0 2.7 %shard_map.134.field = f32[25,256,128]{2,1,0:T(8,128)S(1)} custom-call(s32[8,8,128]{2,1,0:T(8,128)S(1)} %get-tuple-element.20.cells, f32[25,256,128]{2,1,0:T(8,128)S(1)} %copy-done.3, f32[32,10,8,128]{3,2,1,0:T(8,128)S(1)} %all-to-all-done.early, f32[16,5,2,8,128]{4,3,2,1,0:T(8,128)S(1)} %copy-done.5, f32[32,10,8,128]{3,2,1,0:T(8,128)S(1)} %all-to-all-done.1.late, ...), custom_call_target="tpu_custom_call" | custom-call | tf_op jit(solution)/shard_map/pallas_call | solution.py:756
  80.7 0.0 copy-start.1
  80.7 16.3 %shard_map.135 = (f32[3,288,128]{2,1,0:T(8,128)S(1)}, f32[3,288,128]{2,1,0:T(8,128)S(1)}, f32[256,128]{1,0:T(8,128)S(1)}, f32[256,128]{1,0:T(8,128)S(1)}) custom-call(f32[25,256,128]{2,1,0:T(8,128)S(1)} %shard_map.134.field), custom_call_target="tpu_custom_call" | custom-call | tf_op jit(solution)/shard_map/pallas_call | solution.py:176
  97.1 0.0 copy-done.4
  97.1 0.0 copy-done.7
  97.1 0.0 copy-done.9
  97.1 0.0 copy-done.1
  97.1 0.0 copy-start.11
  97.1 50.4 %shard_map.136 = (f32[25,256,128]{2,1,0:T(8,128)}, f32[256,128]{1,0:T(8,128)S(1)}) custom-call(f32[25,256,128]{2,1,0:T(8,128)S(1)} %shard_map.134.field, f32[25,256,128]{2,1,0:T(8,128)S(1)} %copy-done.1, f32[3,288,128]{2,1,0:T(8,128)S(1)} %get-tuple-element.24.west_cols, f32[3,288,128]{2,1,0:T(8,128)S(1)} %get-tuple-element.25.east_cols, ...), custom_call_target="tpu_custom_call" | custom-call | tf_op jit(solution)/shard_map/pallas_call | solution.py:380
  147.5 13.6 %shard_map.137 = f32[8,16,2,128]{3,2,1,0:T(2,128)S(1)} custom-call(f32[8,16,2,128]{3,2,1,0:T(2,128)S(1)} %bitcast.16), custom_call_target="tpu_custom_call" | custom-call | tf_op jit(solution)/shard_map/pallas_call | solution.py:624
  161.2 0.0 copy-done.11
  161.2 2.1 %shard_map.138 = f32[25,512]{1,0:T(8,128)} custom-call(f32[256,128]{1,0:T(8,128)S(1)} %bitcast.14, s32[1,512]{1,0:T(1,128)S(1)} %copy-done.11), custom_call_target="tpu_custom_call" | custom-call | tf_op jit(solution)/shard_map/pallas_call | solution.py:783
  (7 shorter events, 0.0 us)
Async XLA Ops:
  0.6 12.1 %copy-start.16 = (s32[512,1]{0,1:T(1,128)S(1)}, s32[512,1]{0,1:T(1,128)}, u32[]{:S(2)}) copy-start(s32[512,1]{0,1:T(1,128)} %param.13) | copy-start | bytes 6148
  3.1 10.5 %copy-start.17 = (s32[512]{0:T(512)S(1)}, s32[512]{0:T(512)}, u32[]{:S(2)}) copy-start(s32[512]{0:T(512)} %param.15) | copy-start | bytes 6148
  3.1 10.5 %copy-start.18 = (s32[512]{0:T(512)S(1)}, s32[512]{0:T(512)}, u32[]{:S(2)}) copy-start(s32[512]{0:T(512)} %param.14) | copy-start | bytes 6148
  3.1 15.0 %copy-start.12 = (s32[256,128]{1,0:T(8,128)S(1)}, s32[256,128]{1,0:T(8,128)}, u32[]{:S(2)}) copy-start(s32[256,128]{1,0:T(8,128)} %param.22) | copy-start | bytes 393220
  3.1 15.1 %copy-start.13 = (f32[256,128]{1,0:T(8,128)S(1)}, f32[256,128]{1,0:T(8,128)}, u32[]{:S(2)}) copy-start(f32[256,128]{1,0:T(8,128)} %param.21) | copy-start | bytes 393220
  3.1 15.1 %copy-start.14 = (f32[256,128]{1,0:T(8,128)S(1)}, f32[256,128]{1,0:T(8,128)}, u32[]{:S(2)}) copy-start(f32[256,128]{1,0:T(8,128)} %param.20) | copy-start | bytes 393220
  3.1 15.1 %copy-start.15 = (f32[256,128]{1,0:T(8,128)S(1)}, f32[256,128]{1,0:T(8,128)}, u32[]{:S(2)}) copy-start(f32[256,128]{1,0:T(8,128)} %param.19) | copy-start | bytes 393220
  3.1 43.2 %all-to-all-start = ((f32[32,10,8,128]{3,2,1,0:T(8,128)}), f32[32,10,8,128]{3,2,1,0:T(8,128)S(1)}, u32[]{:S(2)}, u32[]{:S(2)}) async-start(f32[32,10,8,128]{3,2,1,0:T(8,128)} %copy_bitcast_fusion), calls=%async_computation | async-start | bytes 2621440 | tf_op jit(solution)/shard_map/all_to_all | solution.py:809
  46.3 7.8 %copy-start.10 = (f32[8,16,2,128]{3,2,1,0:T(2,128)S(1)}, f32[8,16,2,128]{3,2,1,0:T(2,128)}, u32[]{:S(2)}) copy-start(f32[8,16,2,128]{3,2,1,0:T(2,128)} %get-tuple-element.19) | copy-start | bytes 393220
  46.3 27.9 %copy-start.5 = (f32[16,5,2,8,128]{4,3,2,1,0:T(8,128)S(1)}, f32[16,5,2,8,128]{4,3,2,1,0:T(8,128)}, u32[]{:S(2)}) copy-start(f32[16,5,2,8,128]{4,3,2,1,0:T(8,128)} %get-tuple-element.22.middle) | copy-start | bytes 1966084
  46.3 27.8 %all-to-all-start.1 = ((f32[32,10,8,128]{3,2,1,0:T(8,128)}), f32[32,10,8,128]{3,2,1,0:T(8,128)S(1)}, u32[]{:S(2)}, u32[]{:S(2)}) async-start(f32[32,10,8,128]{3,2,1,0:T(8,128)} %get-tuple-element.23), calls=%async_computation.1 | async-start | bytes 2621440 | tf_op jit(solution)/shard_map/all_to_all | solution.py:816
  67.5 1.7 %copy-start.2 = (f32[25,256,128]{2,1,0:T(8,128)}, f32[25,256,128]{2,1,0:T(8,128)S(1)}, u32[]{:S(2)}) copy-start(f32[25,256,128]{2,1,0:T(8,128)S(1)} %get-tuple-element.21.seen) | copy-start | bytes 9830404
  69.3 0.8 copy-start.6
  70.1 0.8 copy-start.8
  74.2 1.9 %copy-start = (f32[25,256,128]{2,1,0:T(8,128)S(1)}, f32[25,256,128]{2,1,0:T(8,128)}, u32[]{:S(2)}) copy-start(f32[25,256,128]{2,1,0:T(8,128)} %norm.3) | copy-start | bytes 9830404
  76.1 1.9 %copy-start.3 = (f32[25,256,128]{2,1,0:T(8,128)S(1)}, f32[25,256,128]{2,1,0:T(8,128)}, u32[]{:S(2)}) copy-start(f32[25,256,128]{2,1,0:T(8,128)} %copy-done.2) | copy-start | bytes 9830404
  78.0 19.0 %copy-start.4 = (f32[2,7,280,128]{3,2,1,0:T(8,128)S(1)}, f32[2,7,280,128]{3,2,1,0:T(8,128)}, u32[]{:S(2)}) copy-start(f32[2,7,280,128]{3,2,1,0:T(8,128)} %get-tuple-element.28.weights) | copy-start | bytes 6021124
  78.0 19.1 %copy-start.7 = (f32[1024,128]{1,0:T(8,128)S(1)}, f32[1024,128]{1,0:T(8,128)}, u32[]{:S(2)}) copy-start(f32[1024,128]{1,0:T(8,128)} %copy-done.6) | copy-start | bytes 1572868
  78.0 19.1 %copy-start.9 = (f32[1024,128]{1,0:T(8,128)S(1)}, f32[1024,128]{1,0:T(8,128)}, u32[]{:S(2)}) copy-start(f32[1024,128]{1,0:T(8,128)} %copy-done.8) | copy-start | bytes 1572868
  80.7 16.4 %copy-start.1 = (f32[25,256,128]{2,1,0:T(8,128)S(1)}, f32[25,256,128]{2,1,0:T(8,128)}, u32[]{:S(2)}) copy-start(f32[25,256,128]{2,1,0:T(8,128)} %norm.3) | copy-start | bytes 9830404
  97.1 64.1 %copy-start.11 = (s32[1,512]{1,0:T(1,128)S(1)}, s32[1,512]{1,0:T(1,128)}, u32[]{:S(2)}) copy-start(s32[1,512]{1,0:T(1,128)} %get-tuple-element.33.slots) | copy-start | bytes 6148

commit v9 on v8

--- a/solution.py
+++ b/solution.py
@@ -29,6 +29,20 @@
     return lax.broadcasted_iota(jnp.int32, shape, len(shape) - 1)
 
 
+SPARE = ((0, 60, 50, 4, 60), (0, 124, 114, 4, 120), (1, 60, 50, 2, 52))
+
+
+def spare_columns(cols, last):
+    values = jnp.zeros(cols.shape[1:], jnp.float32)
+    lane = lane_ids(values.shape)
+    place = COLS - STEPS if last else LANES // 2 - COLS
+    for tile, first_lane, last_lane, width, _ in SPARE:
+        moved = turn(cols[tile], place - (last_lane if last else first_lane))
+        values = jnp.where(within(lane, place, width), moved, values)
+        place += width
+    return values
+
+
 def within(lane, start, width):
     start = start % LANES
     return jnp.logical_and(lane >= start, lane < start + width)
@@ -66,11 +80,13 @@
     own = jnp.where(upper_half, high, low)
     east = jnp.where(
         jnp.logical_and(inside, within(lane, half - COLS, cols)),
-        turn(east, half - COLS - cols * k),
+        east if k is None else turn(east, half - COLS - cols * k),
         0.0,
     )
     west = jnp.where(
-        jnp.logical_and(inside, within(lane, COLS - cols, cols)), turn(west, COLS - cols * k), east
+        jnp.logical_and(inside, within(lane, COLS - cols, cols)),
+        west if k is None else turn(west, COLS - cols * k),
+        east,
     )
     return jnp.where(jnp.logical_and(lane >= COLS, lane < half - COLS), own, west)
 
@@ -142,16 +158,19 @@
         at = pl.ds(STEPS * level, STEPS)
         pack_high[at, :] = field[level, pl.ds(rows - STEPS, STEPS), :]
         pack_low[at, :] = field[level, pl.ds(0, STEPS), :]
-    pl.semaphore_wait(barrier, 8)
-    send(pack_high, south_rows, (up, lon))
-    send(pack_low, north_rows, (down, lon))
+    lane = lane_ids((rows, LANES))
     for tile in range(pack_first.shape[0]):
         low, high = packed_columns(
             lambda plane: field[plane], levels, rows, STEPS, tile * PAIRS, PAIRS
         )
+        for at, first_lane, last_lane, width, shift in SPARE:
+            if at == tile:
+                values = turn(field[levels - 1], shift)
+                low = jnp.where(within(lane, first_lane, width), values, low)
+                high = jnp.where(within(lane, last_lane, width), values, high)
         pack_first[tile] = low
         pack_last[tile] = high
-
+    pl.semaphore_wait(barrier, 8)
     first = pl.ds(0, HALO)
     last = pl.ds(rows - HALO, HALO)
     own = pl.ds(HALO, rows)
@@ -162,13 +181,15 @@
     send(pack_first.at[:, last, :], east_cols.at[:, first, :], (up, left))
     send(pack_last.at[:, first, :], west_cols.at[:, above, :], (down, right))
     send(pack_first.at[:, first, :], east_cols.at[:, above, :], (down, left))
+    send(pack_high, south_rows, (up, lon))
+    send(pack_low, north_rows, (down, lon))
     for copy in copies:
         copy.wait()
 
 
 def exchange(field, n_lat, n_lon):
     levels, rows, lanes = field.shape
-    tiles = -(-((levels + 1) // 2) // PAIRS)
+    tiles = levels // 2 // PAIRS
     edge = -(-levels * STEPS // 8) * 8
     whole = pl.BlockSpec(memory_space=pltpu.VMEM)
     packed = jax.ShapeDtypeStruct((tiles, rows + 2 * HALO, lanes), jnp.float32)
@@ -274,12 +295,13 @@
         grid[level, pl.ds(HALO + rows, STEPS), :] = jnp.where(has_north, north_rows[at, :], 0.0)
     for pair in range(strips):
         tile, k = divmod(pair, PAIRS)
+        alone = 2 * pair + 1 >= levels
         grid[levels + pair] = strip_plane(
             grid[2 * pair],
             grid[min(2 * pair + 1, levels - 1)],
-            east_cols[tile],
-            west_cols[tile],
-            k,
+            spare_columns(east_cols, False) if alone else east_cols[tile],
+            spare_columns(west_cols, True) if alone else west_cols[tile],
+            None if alone else k,
             STEPS,
             inside,
         )

time: 164 us -> 160 us (0.976)
  Pallas kernels: 130 us -> 126 us
    pallas_call x1, Pallas kernels: 16.3 us -> 13 us  [exchange(): pl.pallas_call(functools.partial(exchange_kernel, n_lat, n_lon), out_shap...]
  transfers between devices with their start and end apart: 2 -> 2, of which waited for: 1 -> 1; matrix products, arithmetic and copies ran while one was open for 1% -> 1% of each run, Pallas kernels for 27% -> 28%
where the time goes in v9:
time: 160 us
  Pallas kernels  126 us (79%)
  starting transfers between devices  17.4 us (11%)
  local copies, waits for them, and re-layouts  10.5 us (7%)
  waiting for transfers between devices  3.3 us (2%)
    pallas_call x1, Pallas kernels, diffuse(): pl.pallas_call(functools.partial(diffuse_kernel, n_lat), out_shape=(jax.S...  50.3 us
    pallas_call x2, Pallas kernels, post(): pl.pallas_call(functools.partial(post_kernel, has_coef), out_shape=out_sh...  41 us
    pallas_call x1, Pallas kernels, spread(): pl.pallas_call(functools.partial(spread_kernel, levels), out_shape=(jax.S...  13.4 us
    pallas_call x1, Pallas kernels, exchange(): pl.pallas_call(functools.partial(exchange_kernel, n_lat, n_lon), out_shap...  13 us
    all_to_all x1, starting transfers between devices, on_device(): lax.all_to_all(jnp.transpose(model_tiles[:EARLY], (1, 0, 2, 3)), 'lon', s...  9.6 us
    unnamed x39, local copies, waits for them, and re-layouts  8.07 us
    all_to_all x1, starting transfers between devices, on_device(): late = lax.all_to_all(late, 'lon', split_axis=0, concat_axis=0, tiled=True)  7.78 us
    pallas_call x1, Pallas kernels, route(): pl.pallas_call(route_kernel, out_shape=(jax.ShapeDtypeStruct((devices * C...  3.93 us
  transfers between devices with their start and end apart: 2, of which 1 were waited for; matrix products, arithmetic and copies ran while one was open for 1% of the time, Pallas kernels for 28%

profile of v9, /device:TPU:1, one launch (start us, length us, event | category | flops | bytes accessed | tf_op | source)
XLA Modules:
  0.0 159.9 jit_solution(5867123316671805524)
XLA Ops:
  0.6 0.0 copy-start.16
  0.6 2.5 %copy_bitcast_fusion = f32[32,10,8,128]{3,2,1,0:T(8,128)} fusion(f32[25,32,8,128]{3,2,1,0:T(8,128)} %refs_1_.1), kind=kLoop, calls=%fused_computation | loop fusion | bytes 2621440 | tf_op jit(solution)/shard_map/transpose | solution.py:832
  3.1 0.0 copy-start.17
  3.1 0.0 copy-start.18
  3.1 0.0 copy-start.12
  3.1 0.0 copy-start.13
  3.1 0.0 copy-start.14
  3.1 0.0 copy-start.15
  3.1 9.6 %all-to-all-start = ((f32[32,10,8,128]{3,2,1,0:T(8,128)}), f32[32,10,8,128]{3,2,1,0:T(8,128)S(1)}, u32[]{:S(2)}, u32[]{:S(2)}) async-start(f32[32,10,8,128]{3,2,1,0:T(8,128)} %copy_bitcast_fusion), calls=%async_computation | async-start | bytes 2621440 | tf_op jit(solution)/shard_map/all_to_all | solution.py:831
  12.7 0.0 copy-done.16
  12.8 0.9 copy.14.owner_column
  13.6 0.0 copy-done.17
  13.6 0.0 copy-done.18
  13.6 0.6 pad_add_fusion.place
  14.2 3.9 %shard_map.131 = (f32[256,128]{1,0:T(8,128)}, s32[1,512]{1,0:T(1,128)}) custom-call(f32[25,512]{1,0:T(8,128)} %innovations.1, f32[4,512]{1,0:T(4,128)} %weights.1, s32[2,512]{1,0:T(2,128)} %pad_add_fusion.place, s32[512,1]{1,0:T(8,128)} %copy.14.owner_column, s32[1,512]{1,0:T(1,128)} %bitcast.21, s32[1,32]{1,0:T(1,128)} %ids.1), custom_call_target="tpu_custom_call" | custom-call | tf_op jit(solution)/shard_map/pallas_call | solution.py:472
  18.1 0.0 copy-done.12
  18.2 0.0 copy-done.13
  18.2 0.0 copy-done.14
  18.2 0.0 copy-done.15
  18.2 0.9 pad_maximum_fusion.refs_0_
  19.0 27.2 %shard_map.132 = (f32[8,16,2,128]{3,2,1,0:T(2,128)}, f32[2,7,280,128]{3,2,1,0:T(8,128)}, f32[16,5,2,8,128]{4,3,2,1,0:T(8,128)}, f32[32,10,8,128]{3,2,1,0:T(8,128)}) custom-call(f32[8,16,2,128]{3,2,1,0:T(2,128)} %bitcast.17, f32[4,256,128]{2,1,0:T(8,128)} %pad_maximum_fusion.refs_0_, f32[25,32,8,128]{3,2,1,0:T(8,128)} %refs_1_.1), custom_call_target="tpu_custom_call" | custom-call | tf_op jit(solution)/shard_map/pallas_call | solution.py:646
  46.3 0.0 copy-start.10
  46.3 0.0 copy-start.5
  46.3 0.0 all-to-all-done.early
  46.3 7.8 %all-to-all-start.1 = ((f32[32,10,8,128]{3,2,1,0:T(8,128)}), f32[32,10,8,128]{3,2,1,0:T(8,128)S(1)}, u32[]{:S(2)}, u32[]{:S(2)}) async-start(f32[32,10,8,128]{3,2,1,0:T(8,128)} %get-tuple-element.23), calls=%async_computation.1 | async-start | bytes 2621440 | tf_op jit(solution)/shard_map/all_to_all | solution.py:838
  54.1 0.0 copy-done.10
  54.1 13.4 %shard_map.133 = (f32[25,256,128]{2,1,0:T(8,128)S(1)}, f32[1024,128]{1,0:T(8,128)S(1)}, f32[1024,128]{1,0:T(8,128)S(1)}, s32[8,8,128]{2,1,0:T(8,128)S(1)}) custom-call(f32[256,128]{1,0:T(8,128)S(1)} %bitcast.15), custom_call_target="tpu_custom_call" | custom-call | tf_op jit(solution)/shard_map/pallas_call | solution.py:729
  67.5 0.0 copy-start.2
  67.6 1.7 %copy-done.2 = f32[25,256,128]{2,1,0:T(8,128)} copy-done((f32[25,256,128]{2,1,0:T(8,128)}, f32[25,256,128]{2,1,0:T(8,128)S(1)}, u32[]{:S(2)}) %copy-start.2) | copy-done | bytes 3276824
  69.3 0.0 copy-start.6
  69.3 0.8 copy-done.6
  70.1 0.8 copy-done.8
  70.9 3.3 %all-to-all-done.1.late = f32[32,10,8,128]{3,2,1,0:T(8,128)S(1)} async-done(((f32[32,10,8,128]{3,2,1,0:T(8,128)}), f32[32,10,8,128]{3,2,1,0:T(8,128)S(1)}, u32[]{:S(2)}, u32[]{:S(2)}) %all-to-all-start.1) | async-done | bytes 1310752 | tf_op jit(solution)/shard_map/all_to_all | solution.py:838
  74.2 0.0 copy-done.5
  74.2 1.9 %copy-done = f32[25,256,128]{2,1,0:T(8,128)S(1)} copy-done((f32[25,256,128]{2,1,0:T(8,128)S(1)}, f32[25,256,128]{2,1,0:T(8,128)}, u32[]{:S(2)}) %copy-start) | copy-done | bytes 3276824
  76.1 1.9 %copy-done.3 = f32[25,256,128]{2,1,0:T(8,128)S(1)} copy-done((f32[25,256,128]{2,1,0:T(8,128)S(1)}, f32[25,256,128]{2,1,0:T(8,128)}, u32[]{:S(2)}) %copy-start.3) | copy-done | bytes 3276824
  78.0 2.7 %shard_map.134.field = f32[25,256,128]{2,1,0:T(8,128)S(1)} custom-call(s32[8,8,128]{2,1,0:T(8,128)S(1)} %get-tuple-element.20.cells, f32[25,256,128]{2,1,0:T(8,128)S(1)} %copy-done.3, f32[32,10,8,128]{3,2,1,0:T(8,128)S(1)} %all-to-all-done.early, f32[16,5,2,8,128]{4,3,2,1,0:T(8,128)S(1)} %copy-done.5, f32[32,10,8,128]{3,2,1,0:T(8,128)S(1)} %all-to-all-done.1.late, ...), custom_call_target="tpu_custom_call" | custom-call | tf_op jit(solution)/shard_map/pallas_call | solution.py:778
  80.7 0.0 copy-start.1
  80.7 13.0 %shard_map.135 = (f32[2,288,128]{2,1,0:T(8,128)S(1)}, f32[2,288,128]{2,1,0:T(8,128)S(1)}, f32[256,128]{1,0:T(8,128)S(1)}, f32[256,128]{1,0:T(8,128)S(1)}) custom-call(f32[25,256,128]{2,1,0:T(8,128)S(1)} %shard_map.134.field), custom_call_target="tpu_custom_call" | custom-call | tf_op jit(solution)/shard_map/pallas_call | solution.py:197
  93.7 0.0 copy-done.4
  93.7 0.0 copy-done.7
  93.7 0.0 copy-done.9
  93.8 0.0 copy-done.1
  93.8 0.0 copy-start.11
  93.8 50.3 %shard_map.136 = (f32[25,256,128]{2,1,0:T(8,128)}, f32[256,128]{1,0:T(8,128)S(1)}) custom-call(f32[25,256,128]{2,1,0:T(8,128)S(1)} %shard_map.134.field, f32[25,256,128]{2,1,0:T(8,128)S(1)} %copy-done.1, f32[2,288,128]{2,1,0:T(8,128)S(1)} %get-tuple-element.24.west_cols, f32[2,288,128]{2,1,0:T(8,128)S(1)} %get-tuple-element.25.east_cols, ...), custom_call_target="tpu_custom_call" | custom-call | tf_op jit(solution)/shard_map/pallas_call | solution.py:402
  144.1 13.7 %shard_map.137 = f32[8,16,2,128]{3,2,1,0:T(2,128)S(1)} custom-call(f32[8,16,2,128]{3,2,1,0:T(2,128)S(1)} %bitcast.16), custom_call_target="tpu_custom_call" | custom-call | tf_op jit(solution)/shard_map/pallas_call | solution.py:646
  157.8 0.0 copy-done.11
  157.8 2.1 %shard_map.138 = f32[25,512]{1,0:T(8,128)} custom-call(f32[256,128]{1,0:T(8,128)S(1)} %bitcast.14, s32[1,512]{1,0:T(1,128)S(1)} %copy-done.11), custom_call_target="tpu_custom_call" | custom-call | tf_op jit(solution)/shard_map/pallas_call | solution.py:805
  (7 shorter events, 0.0 us)
Async XLA Ops:
  0.6 12.1 %copy-start.16 = (s32[512,1]{0,1:T(1,128)S(1)}, s32[512,1]{0,1:T(1,128)}, u32[]{:S(2)}) copy-start(s32[512,1]{0,1:T(1,128)} %param.13) | copy-start | bytes 6148
  3.1 10.5 %copy-start.17 = (s32[512]{0:T(512)S(1)}, s32[512]{0:T(512)}, u32[]{:S(2)}) copy-start(s32[512]{0:T(512)} %param.15) | copy-start | bytes 6148
  3.1 10.5 %copy-start.18 = (s32[512]{0:T(512)S(1)}, s32[512]{0:T(512)}, u32[]{:S(2)}) copy-start(s32[512]{0:T(512)} %param.14) | copy-start | bytes 6148
  3.1 15.0 %copy-start.12 = (s32[256,128]{1,0:T(8,128)S(1)}, s32[256,128]{1,0:T(8,128)}, u32[]{:S(2)}) copy-start(s32[256,128]{1,0:T(8,128)} %param.22) | copy-start | bytes 393220
  3.1 15.1 %copy-start.13 = (f32[256,128]{1,0:T(8,128)S(1)}, f32[256,128]{1,0:T(8,128)}, u32[]{:S(2)}) copy-start(f32[256,128]{1,0:T(8,128)} %param.21) | copy-start | bytes 393220
  3.1 15.1 %copy-start.14 = (f32[256,128]{1,0:T(8,128)S(1)}, f32[256,128]{1,0:T(8,128)}, u32[]{:S(2)}) copy-start(f32[256,128]{1,0:T(8,128)} %param.20) | copy-start | bytes 393220
  3.1 15.1 %copy-start.15 = (f32[256,128]{1,0:T(8,128)S(1)}, f32[256,128]{1,0:T(8,128)}, u32[]{:S(2)}) copy-start(f32[256,128]{1,0:T(8,128)} %param.19) | copy-start | bytes 393220
  3.1 43.2 %all-to-all-start = ((f32[32,10,8,128]{3,2,1,0:T(8,128)}), f32[32,10,8,128]{3,2,1,0:T(8,128)S(1)}, u32[]{:S(2)}, u32[]{:S(2)}) async-start(f32[32,10,8,128]{3,2,1,0:T(8,128)} %copy_bitcast_fusion), calls=%async_computation | async-start | bytes 2621440 | tf_op jit(solution)/shard_map/all_to_all | solution.py:831
  46.3 7.8 %copy-start.10 = (f32[8,16,2,128]{3,2,1,0:T(2,128)S(1)}, f32[8,16,2,128]{3,2,1,0:T(2,128)}, u32[]{:S(2)}) copy-start(f32[8,16,2,128]{3,2,1,0:T(2,128)} %get-tuple-element.19) | copy-start | bytes 393220
  46.3 27.9 %copy-start.5 = (f32[16,5,2,8,128]{4,3,2,1,0:T(8,128)S(1)}, f32[16,5,2,8,128]{4,3,2,1,0:T(8,128)}, u32[]{:S(2)}) copy-start(f32[16,5,2,8,128]{4,3,2,1,0:T(8,128)} %get-tuple-element.22.middle) | copy-start | bytes 1966084
  46.3 27.8 %all-to-all-start.1 = ((f32[32,10,8,128]{3,2,1,0:T(8,128)}), f32[32,10,8,128]{3,2,1,0:T(8,128)S(1)}, u32[]{:S(2)}, u32[]{:S(2)}) async-start(f32[32,10,8,128]{3,2,1,0:T(8,128)} %get-tuple-element.23), calls=%async_computation.1 | async-start | bytes 2621440 | tf_op jit(solution)/shard_map/all_to_all | solution.py:838
  67.5 1.7 %copy-start.2 = (f32[25,256,128]{2,1,0:T(8,128)}, f32[25,256,128]{2,1,0:T(8,128)S(1)}, u32[]{:S(2)}) copy-start(f32[25,256,128]{2,1,0:T(8,128)S(1)} %get-tuple-element.21.seen) | copy-start | bytes 9830404
  69.3 0.8 copy-start.6
  70.1 0.8 copy-start.8
  74.2 1.9 %copy-start = (f32[25,256,128]{2,1,0:T(8,128)S(1)}, f32[25,256,128]{2,1,0:T(8,128)}, u32[]{:S(2)}) copy-start(f32[25,256,128]{2,1,0:T(8,128)} %norm.3) | copy-start | bytes 9830404
  76.1 1.9 %copy-start.3 = (f32[25,256,128]{2,1,0:T(8,128)S(1)}, f32[25,256,128]{2,1,0:T(8,128)}, u32[]{:S(2)}) copy-start(f32[25,256,128]{2,1,0:T(8,128)} %copy-done.2) | copy-start | bytes 9830404
  78.0 15.7 %copy-start.4 = (f32[2,7,280,128]{3,2,1,0:T(8,128)S(1)}, f32[2,7,280,128]{3,2,1,0:T(8,128)}, u32[]{:S(2)}) copy-start(f32[2,7,280,128]{3,2,1,0:T(8,128)} %get-tuple-element.28.weights) | copy-start | bytes 6021124
  78.0 15.7 %copy-start.7 = (f32[1024,128]{1,0:T(8,128)S(1)}, f32[1024,128]{1,0:T(8,128)}, u32[]{:S(2)}) copy-start(f32[1024,128]{1,0:T(8,128)} %copy-done.6) | copy-start | bytes 1572868
  78.0 15.7 %copy-start.9 = (f32[1024,128]{1,0:T(8,128)S(1)}, f32[1024,128]{1,0:T(8,128)}, u32[]{:S(2)}) copy-start(f32[1024,128]{1,0:T(8,128)} %copy-done.8) | copy-start | bytes 1572868
  80.7 13.0 %copy-start.1 = (f32[25,256,128]{2,1,0:T(8,128)S(1)}, f32[25,256,128]{2,1,0:T(8,128)}, u32[]{:S(2)}) copy-start(f32[25,256,128]{2,1,0:T(8,128)} %norm.3) | copy-start | bytes 9830404
  93.8 64.0 %copy-start.11 = (s32[1,512]{1,0:T(1,128)S(1)}, s32[1,512]{1,0:T(1,128)}, u32[]{:S(2)}) copy-start(s32[1,512]{1,0:T(1,128)} %get-tuple-element.33.slots) | copy-start | bytes 6148

commit v10 on v9

--- a/solution.py
+++ b/solution.py
@@ -11,7 +11,7 @@
 CAPACITY = 8
 PAD = 32
 DEEP = 40
-UNROLL = 32
+UNROLL = 128
 BIG = 62 << 20
 HALO = 16
 LANES = 128

time: 160 us -> 159 us (level)
  Pallas kernels: 126 us -> 121 us
  waiting for transfers between devices: 3.3 us -> 7.29 us
    pallas_call x1, Pallas kernels: 13.4 us -> 9.44 us  [spread(): pl.pallas_call(functools.partial(spread_kernel, levels), out_shape=(jax.S...]
    all_to_all x1, waiting for transfers between devices: 3.3 us -> 7.29 us  [on_device(): late = lax.all_to_all(late, 'lon', split_axis=0, concat_axis=0, tiled=True)]
    pallas_call x1, Pallas kernels: 50.3 us -> 48.7 us  [diffuse(): pl.pallas_call(functools.partial(diffuse_kernel, n_lat), out_shape=(jax.S...]
  transfers between devices with their start and end apart: 2 -> 2, of which waited for: 1 -> 1; matrix products, arithmetic and copies ran while one was open for 1% -> 1% of each run, Pallas kernels for 28% -> 26%
where the time goes in v10:
time: 159 us; the launch traced here: 158 us
  Pallas kernels  121 us (76%)
  starting transfers between devices  17.4 us (11%)
  local copies, waits for them, and re-layouts  10.5 us (7%)
  waiting for transfers between devices  7.29 us (5%)
    pallas_call x1, Pallas kernels, diffuse(): pl.pallas_call(functools.partial(diffuse_kernel, n_lat), out_shape=(jax.S...  48.7 us
    pallas_call x2, Pallas kernels, post(): pl.pallas_call(functools.partial(post_kernel, has_coef), out_shape=out_sh...  41 us
    pallas_call x1, Pallas kernels, exchange(): pl.pallas_call(functools.partial(exchange_kernel, n_lat, n_lon), out_shap...  13 us
    all_to_all x1, starting transfers between devices, on_device(): lax.all_to_all(jnp.transpose(model_tiles[:EARLY], (1, 0, 2, 3)), 'lon', s...  9.6 us
    pallas_call x1, Pallas kernels, spread(): pl.pallas_call(functools.partial(spread_kernel, levels), out_shape=(jax.S...  9.44 us
    unnamed x39, local copies, waits for them, and re-layouts  8.07 us
    all_to_all x1, starting transfers between devices, on_device(): late = lax.all_to_all(late, 'lon', split_axis=0, concat_axis=0, tiled=True)  7.78 us
    all_to_all x1, waiting for transfers between devices, on_device(): late = lax.all_to_all(late, 'lon', split_axis=0, concat_axis=0, tiled=True)  7.29 us
  transfers between devices with their start and end apart: 2, of which 1 were waited for; matrix products, arithmetic and copies ran while one was open for 1% of the time, Pallas kernels for 26%

profile of v10, /device:TPU:1, one launch (start us, length us, event | category | flops | bytes accessed | tf_op | source)
XLA Modules:
  0.0 158.3 jit_solution(2217653239545979613)
XLA Ops:
  0.6 0.0 copy-start.16
  0.6 2.5 %copy_bitcast_fusion = f32[32,10,8,128]{3,2,1,0:T(8,128)} fusion(f32[25,32,8,128]{3,2,1,0:T(8,128)} %refs_1_.1), kind=kLoop, calls=%fused_computation | loop fusion | bytes 2621440 | tf_op jit(solution)/shard_map/transpose | solution.py:832
  3.1 0.0 copy-start.17
  3.1 0.0 copy-start.12
  3.1 0.0 copy-start.13
  3.1 0.0 copy-start.14
  3.1 0.0 copy-start.15
  3.1 9.6 %all-to-all-start = ((f32[32,10,8,128]{3,2,1,0:T(8,128)}), f32[32,10,8,128]{3,2,1,0:T(8,128)S(1)}, u32[]{:S(2)}, u32[]{:S(2)}) async-start(f32[32,10,8,128]{3,2,1,0:T(8,128)} %copy_bitcast_fusion), calls=%async_computation | async-start | bytes 2621440 | tf_op jit(solution)/shard_map/all_to_all | solution.py:831
  12.7 0.0 copy-done.16
  12.8 0.9 copy.14.owner_column
  13.6 0.0 copy-done.17
  13.6 0.0 copy-done.18
  13.6 0.6 pad_add_fusion.place
  14.2 3.9 %shard_map.131 = (f32[256,128]{1,0:T(8,128)}, s32[1,512]{1,0:T(1,128)}) custom-call(f32[25,512]{1,0:T(8,128)} %innovations.1, f32[4,512]{1,0:T(4,128)} %weights.1, s32[2,512]{1,0:T(2,128)} %pad_add_fusion.place, s32[512,1]{1,0:T(8,128)} %copy.14.owner_column, s32[1,512]{1,0:T(1,128)} %bitcast.21, s32[1,32]{1,0:T(1,128)} %ids.1), custom_call_target="tpu_custom_call" | custom-call | tf_op jit(solution)/shard_map/pallas_call | solution.py:472
  18.1 0.0 copy-done.12
  18.2 0.0 copy-done.13
  18.2 0.0 copy-done.14
  18.2 0.0 copy-done.15
  18.2 0.9 pad_maximum_fusion.refs_0_
  19.0 27.2 %shard_map.132 = (f32[8,16,2,128]{3,2,1,0:T(2,128)}, f32[2,7,280,128]{3,2,1,0:T(8,128)}, f32[16,5,2,8,128]{4,3,2,1,0:T(8,128)}, f32[32,10,8,128]{3,2,1,0:T(8,128)}) custom-call(f32[8,16,2,128]{3,2,1,0:T(2,128)} %bitcast.17, f32[4,256,128]{2,1,0:T(8,128)} %pad_maximum_fusion.refs_0_, f32[25,32,8,128]{3,2,1,0:T(8,128)} %refs_1_.1), custom_call_target="tpu_custom_call" | custom-call | tf_op jit(solution)/shard_map/pallas_call | solution.py:646
  46.3 0.0 copy-start.10
  46.3 0.0 copy-start.5
  46.3 0.0 all-to-all-done.early
  46.3 7.8 %all-to-all-start.1 = ((f32[32,10,8,128]{3,2,1,0:T(8,128)}), f32[32,10,8,128]{3,2,1,0:T(8,128)S(1)}, u32[]{:S(2)}, u32[]{:S(2)}) async-start(f32[32,10,8,128]{3,2,1,0:T(8,128)} %get-tuple-element.23), calls=%async_computation.1 | async-start | bytes 2621440 | tf_op jit(solution)/shard_map/all_to_all | solution.py:838
  54.1 0.0 copy-done.10
  54.1 9.4 %shard_map.133 = (f32[25,256,128]{2,1,0:T(8,128)S(1)}, f32[1024,128]{1,0:T(8,128)S(1)}, f32[1024,128]{1,0:T(8,128)S(1)}, s32[8,8,128]{2,1,0:T(8,128)S(1)}) custom-call(f32[256,128]{1,0:T(8,128)S(1)} %bitcast.15), custom_call_target="tpu_custom_call" | custom-call | tf_op jit(solution)/shard_map/pallas_call | solution.py:729
  63.6 0.0 copy-start.2
  63.6 1.7 %copy-done.2 = f32[25,256,128]{2,1,0:T(8,128)} copy-done((f32[25,256,128]{2,1,0:T(8,128)}, f32[25,256,128]{2,1,0:T(8,128)S(1)}, u32[]{:S(2)}) %copy-start.2) | copy-done | bytes 3276824
  65.3 0.0 copy-start.6
  65.3 0.8 copy-done.6
  66.1 0.0 copy-start.8
  66.1 0.8 copy-done.8
  66.9 7.3 %all-to-all-done.1.late = f32[32,10,8,128]{3,2,1,0:T(8,128)S(1)} async-done(((f32[32,10,8,128]{3,2,1,0:T(8,128)}), f32[32,10,8,128]{3,2,1,0:T(8,128)S(1)}, u32[]{:S(2)}, u32[]{:S(2)}) %all-to-all-start.1) | async-done | bytes 1310752 | tf_op jit(solution)/shard_map/all_to_all | solution.py:838
  74.2 0.0 copy-done.5
  74.2 1.9 %copy-done = f32[25,256,128]{2,1,0:T(8,128)S(1)} copy-done((f32[25,256,128]{2,1,0:T(8,128)S(1)}, f32[25,256,128]{2,1,0:T(8,128)}, u32[]{:S(2)}) %copy-start) | copy-done | bytes 3276824
  76.1 1.9 %copy-done.3 = f32[25,256,128]{2,1,0:T(8,128)S(1)} copy-done((f32[25,256,128]{2,1,0:T(8,128)S(1)}, f32[25,256,128]{2,1,0:T(8,128)}, u32[]{:S(2)}) %copy-start.3) | copy-done | bytes 3276824
  78.0 2.7 %shard_map.134.field = f32[25,256,128]{2,1,0:T(8,128)S(1)} custom-call(s32[8,8,128]{2,1,0:T(8,128)S(1)} %get-tuple-element.20.cells, f32[25,256,128]{2,1,0:T(8,128)S(1)} %copy-done.3, f32[32,10,8,128]{3,2,1,0:T(8,128)S(1)} %all-to-all-done.early, f32[16,5,2,8,128]{4,3,2,1,0:T(8,128)S(1)} %copy-done.5, f32[32,10,8,128]{3,2,1,0:T(8,128)S(1)} %all-to-all-done.1.late, ...), custom_call_target="tpu_custom_call" | custom-call | tf_op jit(solution)/shard_map/pallas_call | solution.py:778
  80.7 0.0 copy-start.1
  80.7 13.0 %shard_map.135 = (f32[2,288,128]{2,1,0:T(8,128)S(1)}, f32[2,288,128]{2,1,0:T(8,128)S(1)}, f32[256,128]{1,0:T(8,128)S(1)}, f32[256,128]{1,0:T(8,128)S(1)}) custom-call(f32[25,256,128]{2,1,0:T(8,128)S(1)} %shard_map.134.field), custom_call_target="tpu_custom_call" | custom-call | tf_op jit(solution)/shard_map/pallas_call | solution.py:197
  93.7 0.0 copy-done.4
  93.7 0.0 copy-done.7
  93.7 0.0 copy-done.9
  93.8 0.0 copy-done.1
  93.8 0.0 copy-start.11
  93.8 48.7 %shard_map.136 = (f32[25,256,128]{2,1,0:T(8,128)}, f32[256,128]{1,0:T(8,128)S(1)}) custom-call(f32[25,256,128]{2,1,0:T(8,128)S(1)} %shard_map.134.field, f32[25,256,128]{2,1,0:T(8,128)S(1)} %copy-done.1, f32[2,288,128]{2,1,0:T(8,128)S(1)} %get-tuple-element.24.west_cols, f32[2,288,128]{2,1,0:T(8,128)S(1)} %get-tuple-element.25.east_cols, ...), custom_call_target="tpu_custom_call" | custom-call | tf_op jit(solution)/shard_map/pallas_call | solution.py:402
  142.4 13.7 %shard_map.137 = f32[8,16,2,128]{3,2,1,0:T(2,128)S(1)} custom-call(f32[8,16,2,128]{3,2,1,0:T(2,128)S(1)} %bitcast.16), custom_call_target="tpu_custom_call" | custom-call | tf_op jit(solution)/shard_map/pallas_call | solution.py:646
  156.2 0.0 copy-done.11
  156.2 2.1 %shard_map.138 = f32[25,512]{1,0:T(8,128)} custom-call(f32[256,128]{1,0:T(8,128)S(1)} %bitcast.14, s32[1,512]{1,0:T(1,128)S(1)} %copy-done.11), custom_call_target="tpu_custom_call" | custom-call | tf_op jit(solution)/shard_map/pallas_call | solution.py:805
  (7 shorter events, 0.0 us)
Async XLA Ops:
  0.6 12.1 %copy-start.16 = (s32[512,1]{0,1:T(1,128)S(1)}, s32[512,1]{0,1:T(1,128)}, u32[]{:S(2)}) copy-start(s32[512,1]{0,1:T(1,128)} %param.13) | copy-start | bytes 6148
  3.1 10.5 %copy-start.17 = (s32[512]{0:T(512)S(1)}, s32[512]{0:T(512)}, u32[]{:S(2)}) copy-start(s32[512]{0:T(512)} %param.15) | copy-start | bytes 6148
  3.1 10.5 %copy-start.18 = (s32[512]{0:T(512)S(1)}, s32[512]{0:T(512)}, u32[]{:S(2)}) copy-start(s32[512]{0:T(512)} %param.14) | copy-start | bytes 6148
  3.1 15.0 %copy-start.12 = (s32[256,128]{1,0:T(8,128)S(1)}, s32[256,128]{1,0:T(8,128)}, u32[]{:S(2)}) copy-start(s32[256,128]{1,0:T(8,128)} %param.22) | copy-start | bytes 393220
  3.1 15.1 %copy-start.13 = (f32[256,128]{1,0:T(8,128)S(1)}, f32[256,128]{1,0:T(8,128)}, u32[]{:S(2)}) copy-start(f32[256,128]{1,0:T(8,128)} %param.21) | copy-start | bytes 393220
  3.1 15.1 %copy-start.14 = (f32[256,128]{1,0:T(8,128)S(1)}, f32[256,128]{1,0:T(8,128)}, u32[]{:S(2)}) copy-start(f32[256,128]{1,0:T(8,128)} %param.20) | copy-start | bytes 393220
  3.1 15.1 %copy-start.15 = (f32[256,128]{1,0:T(8,128)S(1)}, f32[256,128]{1,0:T(8,128)}, u32[]{:S(2)}) copy-start(f32[256,128]{1,0:T(8,128)} %param.19) | copy-start | bytes 393220
  3.1 43.2 %all-to-all-start = ((f32[32,10,8,128]{3,2,1,0:T(8,128)}), f32[32,10,8,128]{3,2,1,0:T(8,128)S(1)}, u32[]{:S(2)}, u32[]{:S(2)}) async-start(f32[32,10,8,128]{3,2,1,0:T(8,128)} %copy_bitcast_fusion), calls=%async_computation | async-start | bytes 2621440 | tf_op jit(solution)/shard_map/all_to_all | solution.py:831
  46.3 7.8 %copy-start.10 = (f32[8,16,2,128]{3,2,1,0:T(2,128)S(1)}, f32[8,16,2,128]{3,2,1,0:T(2,128)}, u32[]{:S(2)}) copy-start(f32[8,16,2,128]{3,2,1,0:T(2,128)} %get-tuple-element.19) | copy-start | bytes 393220
  46.3 27.9 %copy-start.5 = (f32[16,5,2,8,128]{4,3,2,1,0:T(8,128)S(1)}, f32[16,5,2,8,128]{4,3,2,1,0:T(8,128)}, u32[]{:S(2)}) copy-start(f32[16,5,2,8,128]{4,3,2,1,0:T(8,128)} %get-tuple-element.22.middle) | copy-start | bytes 1966084
  46.3 27.8 %all-to-all-start.1 = ((f32[32,10,8,128]{3,2,1,0:T(8,128)}), f32[32,10,8,128]{3,2,1,0:T(8,128)S(1)}, u32[]{:S(2)}, u32[]{:S(2)}) async-start(f32[32,10,8,128]{3,2,1,0:T(8,128)} %get-tuple-element.23), calls=%async_computation.1 | async-start | bytes 2621440 | tf_op jit(solution)/shard_map/all_to_all | solution.py:838
  63.6 1.7 %copy-start.2 = (f32[25,256,128]{2,1,0:T(8,128)}, f32[25,256,128]{2,1,0:T(8,128)S(1)}, u32[]{:S(2)}) copy-start(f32[25,256,128]{2,1,0:T(8,128)S(1)} %get-tuple-element.21.seen) | copy-start | bytes 9830404
  65.3 0.8 copy-start.6
  66.1 0.8 copy-start.8
  74.2 1.9 %copy-start = (f32[25,256,128]{2,1,0:T(8,128)S(1)}, f32[25,256,128]{2,1,0:T(8,128)}, u32[]{:S(2)}) copy-start(f32[25,256,128]{2,1,0:T(8,128)} %norm.3) | copy-start | bytes 9830404
  76.1 1.9 %copy-start.3 = (f32[25,256,128]{2,1,0:T(8,128)S(1)}, f32[25,256,128]{2,1,0:T(8,128)}, u32[]{:S(2)}) copy-start(f32[25,256,128]{2,1,0:T(8,128)} %copy-done.2) | copy-start | bytes 9830404
  78.0 15.7 %copy-start.4 = (f32[2,7,280,128]{3,2,1,0:T(8,128)S(1)}, f32[2,7,280,128]{3,2,1,0:T(8,128)}, u32[]{:S(2)}) copy-start(f32[2,7,280,128]{3,2,1,0:T(8,128)} %get-tuple-element.28.weights) | copy-start | bytes 6021124
  78.0 15.7 %copy-start.7 = (f32[1024,128]{1,0:T(8,128)S(1)}, f32[1024,128]{1,0:T(8,128)}, u32[]{:S(2)}) copy-start(f32[1024,128]{1,0:T(8,128)} %copy-done.6) | copy-start | bytes 1572868
  78.0 15.7 %copy-start.9 = (f32[1024,128]{1,0:T(8,128)S(1)}, f32[1024,128]{1,0:T(8,128)}, u32[]{:S(2)}) copy-start(f32[1024,128]{1,0:T(8,128)} %copy-done.8) | copy-start | bytes 1572868
  80.7 13.0 %copy-start.1 = (f32[25,256,128]{2,1,0:T(8,128)S(1)}, f32[25,256,128]{2,1,0:T(8,128)}, u32[]{:S(2)}) copy-start(f32[25,256,128]{2,1,0:T(8,128)} %norm.3) | copy-start | bytes 9830404
  93.8 62.4 %copy-start.11 = (s32[1,512]{1,0:T(1,128)S(1)}, s32[1,512]{1,0:T(1,128)}, u32[]{:S(2)}) copy-start(s32[1,512]{1,0:T(1,128)} %get-tuple-element.33.slots) | copy-start | bytes 6148
